TPU v7x, 256 devices: a whole 4x4x8 slice. The times are simulated.
256 devices in a mesh: tm: 8 (over x_lo, y), space: 32 (over x_hi, z, core).
Axes of the slice: x: 4 (x_hi: 2, x_lo: 2; x = x_hi * 2 + x_lo), y: 4, z: 8, core: 2. Of those that a mesh axis runs over, the one named last changes fastest.
Arguments:
- source: float32 [32, 128, 96, 128], P('tm', 'space'), may hold values from -6 to 6
- initial: float32 [128, 96, 128], P('space'), may hold values from -6 to 6
- mobility: float32 [128, 96, 128], P('space'), may hold values from 0.5 to 2
- labels: int32 [128, 96, 128], P('space'), may hold values from 0 to 3
- electrode: int32 [128, 96, 128], P('space'), may hold values 0 or 1
- rates: float32 [4], replicated, may hold values from 0.2 to 1
Outputs:
- density: float32 [32, 128, 96, 128], P('tm', 'space')
All inputs are finite; a program needn't handle non-finite values. No bound on the sum of `electrode` on one device may be relied on, other than what follows from the above.
Results may differ from a plain program's by a relative error of at most 0.00002.
Values sent between devices are 32-bit elements; how exact they have to be, the bound alone decides.
No kernel may reach another device: no remote copies, remote signals or barrier semaphores. Data moves between devices by JAX's collectives and lax.ppermute only.
A program may use at most 64 MiB of HBM per device.

v0:
```python
import jax
import jax.numpy as jnp
from jax import lax
from jax.sharding import PartitionSpec as P

PASSES = 4


source_coef = 0.5
drift_coef = 0.5
react_coef = 0.5
damping = 0.8
coarse_lateral = 0.06
coarse_axial = 0.12


def with_halo(cells, sides, width):
    for axis, dim in sides:
        count = lax.axis_size(axis)
        ends = count - 1
        head = lax.slice_in_dim(cells, 0, width, axis=dim)
        tail = lax.slice_in_dim(cells, cells.shape[dim] - width, cells.shape[dim], axis=dim)
        cells = jnp.concatenate(
            [
                lax.ppermute(tail, axis, [(i, (i + 1) % count) for i in range(ends)]),
                cells,
                lax.ppermute(head, axis, [((i + 1) % count, i) for i in range(ends)]),
            ],
            axis=dim,
        )
    return cells


def passed_along(value, axis, steps):
    count = lax.axis_size(axis)
    first, last = (max(0, -steps), min(count, count - steps))
    return lax.ppermute(value, axis, [(source, source + steps) for source in range(first, last)])


def laid_out(pieces, dim):
    shape = list(pieces.shape[1:])
    shape[dim] *= pieces.shape[0]
    return jnp.moveaxis(pieces, 0, dim).reshape(shape)


def sent_to_all(value, axis):
    size = lax.axis_size(axis)
    return lax.all_to_all(
        jnp.broadcast_to(value[None], (size, *value.shape)), axis, 0, 0, tiled=True
    )


def gathered_copies(value, axis, dim):
    return laid_out(sent_to_all(value, axis), dim)


def pad_across(values):
    return jnp.pad(values, ((0, 0), (0, 0), (1, 1), (1, 1)))


def balance(window, mobile, rate_field, forcing):
    current = window[1:, 1:-1]
    former = window[:-1, 1:-1]
    middle = mobile[:, 1:-1]
    spread = pad_across(middle)
    below_x = 0.5 * (middle + mobile[:, :-2])
    above_x = 0.5 * (middle + mobile[:, 2:])
    below_y = 0.5 * (middle + spread[:, :, :-2, 1:-1])
    above_y = 0.5 * (middle + spread[:, :, 2:, 1:-1])
    below_z = 0.5 * (middle + spread[:, :, 1:-1, :-2])
    above_z = 0.5 * (middle + spread[:, :, 1:-1, 2:])
    beside_all = pad_across(current)
    lower_z = beside_all[:, :, 1:-1, :-2]
    summed = below_x + above_x + below_y + above_y + below_z + above_z
    inflow = (
        below_x * window[1:, :-2]
        + above_x * window[1:, 2:]
        + below_y * beside_all[:, :, :-2, 1:-1]
        + above_y * beside_all[:, :, 2:, 1:-1]
        + below_z * lower_z
        + above_z * beside_all[:, :, 1:-1, 2:]
        - summed * current
    )
    carried = below_z * lower_z - above_z * current
    magnitude = jnp.abs(current)
    excess = (
        current
        - former
        - inflow
        - drift_coef * carried
        + react_coef * rate_field * current * magnitude
    )
    residue = forcing - excess
    diagonal = 1.0 + summed + drift_coef * above_z + rate_field * magnitude
    return (residue, diagonal, current)


def relax(window, mobile, rate_field, freedom, forcing):
    residue, diagonal, current = balance(window, mobile, rate_field, forcing)
    updated = current + damping * freedom * residue / diagonal
    return jnp.concatenate([window[:1, 1:-1], updated], axis=0)


def coarse_change(extended, mobility_ext):
    centre = extended[1:-1, 1:-1]
    centre_mob = mobility_ext[1:-1, 1:-1]
    padded_value = jnp.pad(centre, ((0, 0), (0, 0), (1, 1)))
    padded_mob = jnp.pad(centre_mob, ((0, 0), (0, 0), (1, 1)))

    def couple(value_near, mobile_near):
        return 0.5 * (centre_mob + mobile_near) * (value_near - centre)

    lateral = (
        couple(extended[:-2, 1:-1], mobility_ext[:-2, 1:-1])
        + couple(extended[2:, 1:-1], mobility_ext[2:, 1:-1])
        + couple(extended[1:-1, :-2], mobility_ext[1:-1, :-2])
        + couple(extended[1:-1, 2:], mobility_ext[1:-1, 2:])
    )
    along_z = couple(padded_value[:, :, :-2], padded_mob[:, :, :-2]) + couple(
        padded_value[:, :, 2:], padded_mob[:, :, 2:]
    )
    return centre + coarse_lateral * lateral + coarse_axial * along_z


def region_rates(labels, rates):
    matches = labels[None] == jnp.arange(rates.shape[0], dtype=jnp.int32)[:, None, None, None]
    return jnp.sum(jnp.where(matches, rates[:, None, None, None], 0.0), axis=0)


def restrict(residue):
    step_count, planes, across, depth_z = residue.shape
    grouped = residue.reshape(step_count // 4, 4, planes // 2, 2, across // 2, 2, depth_z)
    return 0.25 * jnp.sum(grouped, axis=(1, 3, 5))


def coarse_mobility(mobility):
    planes, across, depth_z = mobility.shape
    return 0.25 * jnp.sum(mobility.reshape(planes // 2, 2, across // 2, 2, depth_z), axis=(1, 3))


def prolong(correction):
    return jnp.repeat(jnp.repeat(jnp.repeat(correction, 4, axis=0), 2, axis=1), 2, axis=2)


def on_device(source, initial, mobility, labels, electrode, rates):
    rate_field = region_rates(labels, rates)[None]
    freedom = (1.0 - electrode.astype(jnp.float32))[None]
    forcing = source_coef * source
    leading = lax.axis_index("tm") == 0
    near_mob = with_halo(mobility[None], (("space", 1),), 1)

    def with_previous(iterate):
        arrived = passed_along(iterate[-1], "tm", 1)
        opening = jnp.where(leading, initial, arrived)
        return jnp.concatenate([opening[None], iterate], axis=0)

    def sweep(iterate):
        window = with_previous(iterate)
        for number in range(PASSES):
            extended = with_halo(window, (("space", 1),), 1)
            window = relax(extended, near_mob, rate_field, freedom, forcing)
        return window[1:]

    iterate = jnp.broadcast_to(initial, source.shape)
    iterate = sweep(iterate)
    extended = with_halo(with_previous(iterate), (("space", 1),), 1)
    residue = balance(extended, near_mob, rate_field, forcing)[0]
    coarse_rhs = restrict(residue)
    coarse_mob = with_halo(coarse_mobility(mobility), (("space", 0),), 1)
    quarter = coarse_rhs.shape[0]
    gathered = gathered_copies(coarse_rhs, "tm", 0)
    mob_ext = jnp.pad(coarse_mob, ((0, 0), (1, 1), (0, 0)))

    def advance(carry_state, forcing_row):
        bordered = with_halo(carry_state, (("space", 0),), 1)
        bordered = jnp.pad(bordered, ((0, 0), (1, 1), (0, 0)))
        advanced = coarse_change(bordered, mob_ext) + forcing_row
        return (advanced, advanced)

    final_state, history = lax.scan(advance, jnp.zeros(gathered.shape[1:], jnp.float32), gathered)
    returned = lax.dynamic_slice_in_dim(history, lax.axis_index("tm") * quarter, quarter, 0)
    iterate = iterate + freedom * prolong(returned)
    iterate = sweep(iterate)
    return iterate


def solution(mesh):
    return jax.shard_map(
        on_device,
        mesh=mesh,
        in_specs=(
            P("tm", "space", None, None),
            P("space", None, None),
            P("space", None, None),
            P("space", None, None),
            P("space", None, None),
            P(),
        ),
        out_specs=P("tm", "space", None, None),
        check_vma=False,
    )
```

profile of v0, /device:TPU:6, one launch (start us, length us, event | category | flops | bytes accessed | tf_op | source)
XLA Modules:
  0.0 295.7 jit_solution(17498469333336894550)
XLA Ops:
  2.8 8.0 %collective-permute-start.5 = (f32[1,1,96,128]{3,2,1,0:T(8,128)S(1)}, f32[1,1,96,128]{3,2,1,0:T(8,128)S(1)}, u32[]{:S(2)}, u32[]{:S(2)}) collective-permute-start(f32[1,1,96,128]{3,2,1,0:T(8,128)S(1)} %get-tuple-element.179), channel_id=1, source_target_pairs={{1,0},{2,1},{3,2},{4,3},{5,4},{6,5},{7,6},{8,7},{9,8},{10,9},{11,1... | collective-permute-start | bytes 147464 | tf_op jit(solution)/shard_map/ppermute | solution.py:27
  23.1 7.3 %collective-permute-start.6 = (f32[5,1,96,128]{3,2,1,0:T(8,128)S(1)}, f32[5,1,96,128]{3,2,1,0:T(8,128)S(1)}, u32[]{:S(2)}, u32[]{:S(2)}) collective-permute-start(f32[5,1,96,128]{3,2,1,0:T(8,128)S(1)} %get-tuple-element.167), channel_id=1, source_target_pairs={{1,0},{2,1},{3,2},{4,3},{5,4},{6,5},{7,6},{8,7},{9,8},{10,9},{11,1... | collective-permute-start | bytes 737288 | tf_op jit(solution)/shard_map/ppermute | solution.py:27
  36.9 7.4 %collective-permute-start.8 = (f32[5,1,96,128]{3,2,1,0:T(8,128)S(1)}, f32[5,1,96,128]{3,2,1,0:T(8,128)S(1)}, u32[]{:S(2)}, u32[]{:S(2)}) collective-permute-start(f32[5,1,96,128]{3,2,1,0:T(8,128)S(1)} %get-tuple-element.165), channel_id=1, source_target_pairs={{1,0},{2,1},{3,2},{4,3},{5,4},{6,5},{7,6},{8,7},{9,8},{10,9},{11,1... | collective-permute-start | bytes 737288 | tf_op jit(solution)/shard_map/ppermute | solution.py:27
  49.1 7.4 %collective-permute-start.10 = (f32[5,1,96,128]{3,2,1,0:T(8,128)S(1)}, f32[5,1,96,128]{3,2,1,0:T(8,128)S(1)}, u32[]{:S(2)}, u32[]{:S(2)}) collective-permute-start(f32[5,1,96,128]{3,2,1,0:T(8,128)S(1)} %get-tuple-element.163), channel_id=1, source_target_pairs={{1,0},{2,1},{3,2},{4,3},{5,4},{6,5},{7,6},{8,7},{9,8},{10,9},{11,1... | collective-permute-start | bytes 737288 | tf_op jit(solution)/shard_map/ppermute | solution.py:27
  60.3 7.4 %collective-permute-done.9 = f32[5,1,96,128]{3,2,1,0:T(8,128)S(1)} collective-permute-done((f32[5,1,96,128]{3,2,1,0:T(8,128)S(1)}, f32[5,1,96,128]{3,2,1,0:T(8,128)S(1)}, u32[]{:S(2)}, u32[]{:S(2)}) %collective-permute-start.9) | collective-permute-done | bytes 245792 | tf_op jit(solution)/shard_map/ppermute | solution.py:25
  70.7 7.3 %collective-permute-start.12 = (f32[5,1,96,128]{3,2,1,0:T(8,128)S(1)}, f32[5,1,96,128]{3,2,1,0:T(8,128)S(1)}, u32[]{:S(2)}, u32[]{:S(2)}) collective-permute-start(f32[5,1,96,128]{3,2,1,0:T(8,128)S(1)} %get-tuple-element.161), channel_id=1, source_target_pairs={{1,0},{2,1},{3,2},{4,3},{5,4},{6,5},{7,6},{8,7},{9,8},{10,9},{11,1... | collective-permute-start | bytes 737288 | tf_op jit(solution)/shard_map/ppermute | solution.py:27
  87.0 6.4 %collective-permute-done.15 = f32[4,96,128]{2,1,0:T(8,128)} collective-permute-done((f32[4,96,128]{2,1,0:T(8,128)}, f32[4,96,128]{2,1,0:T(8,128)}, u32[]{:S(2)}, u32[]{:S(2)}) %collective-permute-start.15) | collective-permute-done | bytes 196640 | tf_op jit(solution)/shard_map/ppermute | solution.py:37
  97.2 7.3 %collective-permute-start.17 = (f32[5,1,96,128]{3,2,1,0:T(8,128)}, f32[5,1,96,128]{3,2,1,0:T(8,128)}, u32[]{:S(2)}, u32[]{:S(2)}) collective-permute-start(f32[5,1,96,128]{3,2,1,0:T(8,128)} %get-tuple-element.159), channel_id=1, source_target_pairs={{1,0},{2,1},{3,2},{4,3},{5,4},{6,5},{7,6},{8,7},{9,8},{10,9},{11,1... | collective-permute-start | bytes 737288 | tf_op jit(solution)/shard_map/ppermute | solution.py:27
  107.0 7.3 %collective-permute-start.14 = (f32[1,48,128]{2,1,0:T(8,128)}, f32[1,48,128]{2,1,0:T(8,128)}, u32[]{:S(2)}, u32[]{:S(2)}) collective-permute-start(f32[1,48,128]{2,1,0:T(8,128)} %get-tuple-element.184), channel_id=1, source_target_pairs={{1,0},{2,1},{3,2},{4,3},{5,4},{6,5},{7,6},{8,7},{9,8},{10,9},{11,1... | collective-permute-start | bytes 73736 | tf_op jit(solution)/shard_map/ppermute | solution.py:27
  124.7 4.3 %all-to-all-done = f32[8,1,2,48,128]{4,3,2,1,0:T(8,128)} async-done(((f32[8,1,2,48,128]{4,3,2,1,0:T(8,128)}), f32[8,1,2,48,128]{4,3,2,1,0:T(8,128)}, u32[]{:S(2)}, u32[]{:S(2)}) %all-to-all-start) | async-done | bytes 393248 | tf_op jit(solution)/shard_map/all_to_all | solution.py:48
  129.0 98.3 %while.15 = (s32[]{:T(128)}, f32[2,48,128]{2,1,0:T(8,128)S(1)}, f32[8,2,48,128]{3,2,1,0:T(8,128)}, f32[2,48,128]{2,1,0:T(8,128)S(1)}, f32[2,48,128]{2,1,0:T(8,12...) while((s32[]{:T(128)}, f32[2,48,128]{2,1,0:T(8,128)S(1)}, ...), condition=%wide.region_5.6_spmd.clone, body=%wide.region_4.5_spmd.clone.sunk | while | flops 598019 | bytes 1282259 | solution.py:180
  133.5 6.3 %collective-permute-done.1 = f32[1,48,128]{2,1,0:T(8,128)S(1)} collective-permute-done((f32[1,48,128]{2,1,0:T(8,128)S(1)}, f32[1,48,128]{2,1,0:T(8,128)S(1)}, u32[]{:S(2)}, u32[]{:S(2)}) %collective-permute-start.1) | collective-permute-done | bytes 24608 | tf_op jit(solution)/shard_map/while/body/eval_jaxpr/ppermute | solution.py:25
  145.8 6.3 %collective-permute-done.1 = f32[1,48,128]{2,1,0:T(8,128)S(1)} collective-permute-done((f32[1,48,128]{2,1,0:T(8,128)S(1)}, f32[1,48,128]{2,1,0:T(8,128)S(1)}, u32[]{:S(2)}, u32[]{:S(2)}) %collective-permute-start.1) | collective-permute-done | bytes 24608 | tf_op jit(solution)/shard_map/while/body/eval_jaxpr/ppermute | solution.py:25
  158.1 6.3 %collective-permute-done.1 = f32[1,48,128]{2,1,0:T(8,128)S(1)} collective-permute-done((f32[1,48,128]{2,1,0:T(8,128)S(1)}, f32[1,48,128]{2,1,0:T(8,128)S(1)}, u32[]{:S(2)}, u32[]{:S(2)}) %collective-permute-start.1) | collective-permute-done | bytes 24608 | tf_op jit(solution)/shard_map/while/body/eval_jaxpr/ppermute | solution.py:25
  170.4 6.3 %collective-permute-done.1 = f32[1,48,128]{2,1,0:T(8,128)S(1)} collective-permute-done((f32[1,48,128]{2,1,0:T(8,128)S(1)}, f32[1,48,128]{2,1,0:T(8,128)S(1)}, u32[]{:S(2)}, u32[]{:S(2)}) %collective-permute-start.1) | collective-permute-done | bytes 24608 | tf_op jit(solution)/shard_map/while/body/eval_jaxpr/ppermute | solution.py:25
  182.6 6.3 %collective-permute-done.1 = f32[1,48,128]{2,1,0:T(8,128)S(1)} collective-permute-done((f32[1,48,128]{2,1,0:T(8,128)S(1)}, f32[1,48,128]{2,1,0:T(8,128)S(1)}, u32[]{:S(2)}, u32[]{:S(2)}) %collective-permute-start.1) | collective-permute-done | bytes 24608 | tf_op jit(solution)/shard_map/while/body/eval_jaxpr/ppermute | solution.py:25
  194.9 6.3 %collective-permute-done.1 = f32[1,48,128]{2,1,0:T(8,128)S(1)} collective-permute-done((f32[1,48,128]{2,1,0:T(8,128)S(1)}, f32[1,48,128]{2,1,0:T(8,128)S(1)}, u32[]{:S(2)}, u32[]{:S(2)}) %collective-permute-start.1) | collective-permute-done | bytes 24608 | tf_op jit(solution)/shard_map/while/body/eval_jaxpr/ppermute | solution.py:25
  207.2 6.3 %collective-permute-done.1 = f32[1,48,128]{2,1,0:T(8,128)S(1)} collective-permute-done((f32[1,48,128]{2,1,0:T(8,128)S(1)}, f32[1,48,128]{2,1,0:T(8,128)S(1)}, u32[]{:S(2)}, u32[]{:S(2)}) %collective-permute-start.1) | collective-permute-done | bytes 24608 | tf_op jit(solution)/shard_map/while/body/eval_jaxpr/ppermute | solution.py:25
  219.4 6.3 %collective-permute-done.1 = f32[1,48,128]{2,1,0:T(8,128)S(1)} collective-permute-done((f32[1,48,128]{2,1,0:T(8,128)S(1)}, f32[1,48,128]{2,1,0:T(8,128)S(1)}, u32[]{:S(2)}, u32[]{:S(2)}) %collective-permute-start.1) | collective-permute-done | bytes 24608 | tf_op jit(solution)/shard_map/while/body/eval_jaxpr/ppermute | solution.py:25
  231.4 6.9 %collective-permute-done.18 = f32[4,96,128]{2,1,0:T(8,128)S(1)} collective-permute-done((f32[4,96,128]{2,1,0:T(8,128)S(1)}, f32[4,96,128]{2,1,0:T(8,128)S(1)}, u32[]{:S(2)}, u32[]{:S(2)}) %collective-permute-start.18) | collective-permute-done | bytes 196640 | tf_op jit(solution)/shard_map/ppermute | solution.py:37
  240.4 7.3 %collective-permute-start.20 = (f32[5,1,96,128]{3,2,1,0:T(8,128)S(1)}, f32[5,1,96,128]{3,2,1,0:T(8,128)S(1)}, u32[]{:S(2)}, u32[]{:S(2)}) collective-permute-start(f32[5,1,96,128]{3,2,1,0:T(8,128)S(1)} %get-tuple-element.157), channel_id=1, source_target_pairs={{1,0},{2,1},{3,2},{4,3},{5,4},{6,5},{7,6},{8,7},{9,8},{10,9},{11,1... | collective-permute-start | bytes 737288 | tf_op jit(solution)/shard_map/ppermute | solution.py:27
  254.4 7.4 %collective-permute-start.22 = (f32[5,1,96,128]{3,2,1,0:T(8,128)S(1)}, f32[5,1,96,128]{3,2,1,0:T(8,128)S(1)}, u32[]{:S(2)}, u32[]{:S(2)}) collective-permute-start(f32[5,1,96,128]{3,2,1,0:T(8,128)S(1)} %get-tuple-element.155), channel_id=1, source_target_pairs={{1,0},{2,1},{3,2},{4,3},{5,4},{6,5},{7,6},{8,7},{9,8},{10,9},{11,1... | collective-permute-start | bytes 737288 | tf_op jit(solution)/shard_map/ppermute | solution.py:27
  268.5 7.4 %collective-permute-start.24 = (f32[5,1,96,128]{3,2,1,0:T(8,128)S(1)}, f32[5,1,96,128]{3,2,1,0:T(8,128)S(1)}, u32[]{:S(2)}, u32[]{:S(2)}) collective-permute-start(f32[5,1,96,128]{3,2,1,0:T(8,128)S(1)} %get-tuple-element.153), channel_id=1, source_target_pairs={{1,0},{2,1},{3,2},{4,3},{5,4},{6,5},{7,6},{8,7},{9,8},{10,9},{11,1... | collective-permute-start | bytes 737288 | tf_op jit(solution)/shard_map/ppermute | solution.py:27
  282.6 7.4 %collective-permute-start.26 = (f32[5,1,96,128]{3,2,1,0:T(8,128)S(1)}, f32[5,1,96,128]{3,2,1,0:T(8,128)S(1)}, u32[]{:S(2)}, u32[]{:S(2)}) collective-permute-start(f32[5,1,96,128]{3,2,1,0:T(8,128)S(1)} %get-tuple-element.151), channel_id=1, source_target_pairs={{1,0},{2,1},{3,2},{4,3},{5,4},{6,5},{7,6},{8,7},{9,8},{10,9},{11,1... | collective-permute-start | bytes 737288 | tf_op jit(solution)/shard_map/ppermute | solution.py:27
  (175 shorter events, 137.7 us)
Async XLA Ops:
  0.9 15.6 %collective-permute-start.3 = (f32[1,1,96,128]{3,2,1,0:T(8,128)S(1)}, f32[1,1,96,128]{3,2,1,0:T(8,128)S(1)}, u32[]{:S(2)}, u32[]{:S(2)}) collective-permute-start(f32[1,1,96,128]{3,2,1,0:T(8,128)S(1)} %get-tuple-element.178), channel_id=1, source_target_pairs={{0,1},{1,2},{2,3},{3,4},{4,5},{5,6},{6,7},{7,8},{8,9},{9,10},{10,1... | collective-permute-start | bytes 147464 | tf_op jit(solution)/shard_map/ppermute | solution.py:25
  2.8 13.6 %collective-permute-start.5 = (f32[1,1,96,128]{3,2,1,0:T(8,128)S(1)}, f32[1,1,96,128]{3,2,1,0:T(8,128)S(1)}, u32[]{:S(2)}, u32[]{:S(2)}) collective-permute-start(f32[1,1,96,128]{3,2,1,0:T(8,128)S(1)} %get-tuple-element.179), channel_id=1, source_target_pairs={{1,0},{2,1},{3,2},{4,3},{5,4},{6,5},{7,6},{8,7},{9,8},{10,9},{11,1... | collective-permute-start | bytes 147464 | tf_op jit(solution)/shard_map/ppermute | solution.py:27
  21.1 11.3 %collective-permute-start.4 = (f32[5,1,96,128]{3,2,1,0:T(8,128)S(1)}, f32[5,1,96,128]{3,2,1,0:T(8,128)S(1)}, u32[]{:S(2)}, u32[]{:S(2)}) collective-permute-start(f32[5,1,96,128]{3,2,1,0:T(8,128)S(1)} %get-tuple-element.166), channel_id=1, source_target_pairs={{0,1},{1,2},{2,3},{3,4},{4,5},{5,6},{6,7},{7,8},{8,9},{9,10},{10,1... | collective-permute-start | bytes 737288 | tf_op jit(solution)/shard_map/ppermute | solution.py:25
  23.1 11.0 %collective-permute-start.6 = (f32[5,1,96,128]{3,2,1,0:T(8,128)S(1)}, f32[5,1,96,128]{3,2,1,0:T(8,128)S(1)}, u32[]{:S(2)}, u32[]{:S(2)}) collective-permute-start(f32[5,1,96,128]{3,2,1,0:T(8,128)S(1)} %get-tuple-element.167), channel_id=1, source_target_pairs={{1,0},{2,1},{3,2},{4,3},{5,4},{6,5},{7,6},{8,7},{9,8},{10,9},{11,1... | collective-permute-start | bytes 737288 | tf_op jit(solution)/shard_map/ppermute | solution.py:27
  35.0 11.3 %collective-permute-start.7 = (f32[5,1,96,128]{3,2,1,0:T(8,128)S(1)}, f32[5,1,96,128]{3,2,1,0:T(8,128)S(1)}, u32[]{:S(2)}, u32[]{:S(2)}) collective-permute-start(f32[5,1,96,128]{3,2,1,0:T(8,128)S(1)} %get-tuple-element.164), channel_id=1, source_target_pairs={{0,1},{1,2},{2,3},{3,4},{4,5},{5,6},{6,7},{7,8},{8,9},{9,10},{10,1... | collective-permute-start | bytes 737288 | tf_op jit(solution)/shard_map/ppermute | solution.py:25
  36.9 11.1 %collective-permute-start.8 = (f32[5,1,96,128]{3,2,1,0:T(8,128)S(1)}, f32[5,1,96,128]{3,2,1,0:T(8,128)S(1)}, u32[]{:S(2)}, u32[]{:S(2)}) collective-permute-start(f32[5,1,96,128]{3,2,1,0:T(8,128)S(1)} %get-tuple-element.165), channel_id=1, source_target_pairs={{1,0},{2,1},{3,2},{4,3},{5,4},{6,5},{7,6},{8,7},{9,8},{10,9},{11,1... | collective-permute-start | bytes 737288 | tf_op jit(solution)/shard_map/ppermute | solution.py:27
  49.1 11.1 %collective-permute-start.10 = (f32[5,1,96,128]{3,2,1,0:T(8,128)S(1)}, f32[5,1,96,128]{3,2,1,0:T(8,128)S(1)}, u32[]{:S(2)}, u32[]{:S(2)}) collective-permute-start(f32[5,1,96,128]{3,2,1,0:T(8,128)S(1)} %get-tuple-element.163), channel_id=1, source_target_pairs={{1,0},{2,1},{3,2},{4,3},{5,4},{6,5},{7,6},{8,7},{9,8},{10,9},{11,1... | collective-permute-start | bytes 737288 | tf_op jit(solution)/shard_map/ppermute | solution.py:27
  56.6 11.1 %collective-permute-start.9 = (f32[5,1,96,128]{3,2,1,0:T(8,128)S(1)}, f32[5,1,96,128]{3,2,1,0:T(8,128)S(1)}, u32[]{:S(2)}, u32[]{:S(2)}) collective-permute-start(f32[5,1,96,128]{3,2,1,0:T(8,128)S(1)} %get-tuple-element.162), channel_id=1, source_target_pairs={{0,1},{1,2},{2,3},{3,4},{4,5},{5,6},{6,7},{7,8},{8,9},{9,10},{10,1... | collective-permute-start | bytes 737288 | tf_op jit(solution)/shard_map/ppermute | solution.py:25
  68.8 11.1 %collective-permute-start.11 = (f32[5,1,96,128]{3,2,1,0:T(8,128)S(1)}, f32[5,1,96,128]{3,2,1,0:T(8,128)S(1)}, u32[]{:S(2)}, u32[]{:S(2)}) collective-permute-start(f32[5,1,96,128]{3,2,1,0:T(8,128)S(1)} %get-tuple-element.160), channel_id=1, source_target_pairs={{0,1},{1,2},{2,3},{3,4},{4,5},{5,6},{6,7},{7,8},{8,9},{9,10},{10,1... | collective-permute-start | bytes 737288 | tf_op jit(solution)/shard_map/ppermute | solution.py:25
  70.7 11.0 %collective-permute-start.12 = (f32[5,1,96,128]{3,2,1,0:T(8,128)S(1)}, f32[5,1,96,128]{3,2,1,0:T(8,128)S(1)}, u32[]{:S(2)}, u32[]{:S(2)}) collective-permute-start(f32[5,1,96,128]{3,2,1,0:T(8,128)S(1)} %get-tuple-element.161), channel_id=1, source_target_pairs={{1,0},{2,1},{3,2},{4,3},{5,4},{6,5},{7,6},{8,7},{9,8},{10,9},{11,1... | collective-permute-start | bytes 737288 | tf_op jit(solution)/shard_map/ppermute | solution.py:27
  83.4 10.0 %collective-permute-start.15 = (f32[4,96,128]{2,1,0:T(8,128)}, f32[4,96,128]{2,1,0:T(8,128)}, u32[]{:S(2)}, u32[]{:S(2)}) collective-permute-start(f32[4,96,128]{2,1,0:T(8,128)} %slice_bitcast_fusion.1), channel_id=1, source_target_pairs={{0,32},{32,64},{64,96},{96,128},{128,160},{160,192},{192,224},{1,3... | collective-permute-start | bytes 589832 | tf_op jit(solution)/shard_map/ppermute | solution.py:37
  95.2 19.1 %collective-permute-start.16 = (f32[5,1,96,128]{3,2,1,0:T(8,128)}, f32[5,1,96,128]{3,2,1,0:T(8,128)}, u32[]{:S(2)}, u32[]{:S(2)}) collective-permute-start(f32[5,1,96,128]{3,2,1,0:T(8,128)} %get-tuple-element.158), channel_id=1, source_target_pairs={{0,1},{1,2},{2,3},{3,4},{4,5},{5,6},{6,7},{7,8},{8,9},{9,10},{10,1... | collective-permute-start | bytes 737288 | tf_op jit(solution)/shard_map/ppermute | solution.py:25
  97.2 17.2 %collective-permute-start.17 = (f32[5,1,96,128]{3,2,1,0:T(8,128)}, f32[5,1,96,128]{3,2,1,0:T(8,128)}, u32[]{:S(2)}, u32[]{:S(2)}) collective-permute-start(f32[5,1,96,128]{3,2,1,0:T(8,128)} %get-tuple-element.159), channel_id=1, source_target_pairs={{1,0},{2,1},{3,2},{4,3},{5,4},{6,5},{7,6},{8,7},{9,8},{10,9},{11,1... | collective-permute-start | bytes 737288 | tf_op jit(solution)/shard_map/ppermute | solution.py:27
  105.1 18.0 %collective-permute-start.13 = (f32[1,48,128]{2,1,0:T(8,128)}, f32[1,48,128]{2,1,0:T(8,128)}, u32[]{:S(2)}, u32[]{:S(2)}) collective-permute-start(f32[1,48,128]{2,1,0:T(8,128)} %get-tuple-element.185), channel_id=1, source_target_pairs={{0,1},{1,2},{2,3},{3,4},{4,5},{5,6},{6,7},{7,8},{8,9},{9,10},{10,1... | collective-permute-start | bytes 73736 | tf_op jit(solution)/shard_map/ppermute | solution.py:25
  107.0 16.1 %collective-permute-start.14 = (f32[1,48,128]{2,1,0:T(8,128)}, f32[1,48,128]{2,1,0:T(8,128)}, u32[]{:S(2)}, u32[]{:S(2)}) collective-permute-start(f32[1,48,128]{2,1,0:T(8,128)} %get-tuple-element.184), channel_id=1, source_target_pairs={{1,0},{2,1},{3,2},{4,3},{5,4},{6,5},{7,6},{8,7},{9,8},{10,9},{11,1... | collective-permute-start | bytes 73736 | tf_op jit(solution)/shard_map/ppermute | solution.py:27
  118.9 10.1 %all-to-all-start = ((f32[8,1,2,48,128]{4,3,2,1,0:T(8,128)}), f32[8,1,2,48,128]{4,3,2,1,0:T(8,128)}, u32[]{:S(2)}, u32[]{:S(2)}) async-start(f32[8,1,2,48,128]{4,3,2,1,0:T(8,128)} %broadcast_in_dim.79), calls=%async_computation | async-start | bytes 786432 | tf_op jit(solution)/shard_map/all_to_all | solution.py:48
  238.3 11.3 %collective-permute-start.19 = (f32[5,1,96,128]{3,2,1,0:T(8,128)S(1)}, f32[5,1,96,128]{3,2,1,0:T(8,128)S(1)}, u32[]{:S(2)}, u32[]{:S(2)}) collective-permute-start(f32[5,1,96,128]{3,2,1,0:T(8,128)S(1)} %get-tuple-element.156), channel_id=1, source_target_pairs={{0,1},{1,2},{2,3},{3,4},{4,5},{5,6},{6,7},{7,8},{8,9},{9,10},{10,1... | collective-permute-start | bytes 737288 | tf_op jit(solution)/shard_map/ppermute | solution.py:25
  240.4 11.0 %collective-permute-start.20 = (f32[5,1,96,128]{3,2,1,0:T(8,128)S(1)}, f32[5,1,96,128]{3,2,1,0:T(8,128)S(1)}, u32[]{:S(2)}, u32[]{:S(2)}) collective-permute-start(f32[5,1,96,128]{3,2,1,0:T(8,128)S(1)} %get-tuple-element.157), channel_id=1, source_target_pairs={{1,0},{2,1},{3,2},{4,3},{5,4},{6,5},{7,6},{8,7},{9,8},{10,9},{11,1... | collective-permute-start | bytes 737288 | tf_op jit(solution)/shard_map/ppermute | solution.py:27
  252.4 11.3 %collective-permute-start.21 = (f32[5,1,96,128]{3,2,1,0:T(8,128)S(1)}, f32[5,1,96,128]{3,2,1,0:T(8,128)S(1)}, u32[]{:S(2)}, u32[]{:S(2)}) collective-permute-start(f32[5,1,96,128]{3,2,1,0:T(8,128)S(1)} %get-tuple-element.154), channel_id=1, source_target_pairs={{0,1},{1,2},{2,3},{3,4},{4,5},{5,6},{6,7},{7,8},{8,9},{9,10},{10,1... | collective-permute-start | bytes 737288 | tf_op jit(solution)/shard_map/ppermute | solution.py:25
  254.4 11.1 %collective-permute-start.22 = (f32[5,1,96,128]{3,2,1,0:T(8,128)S(1)}, f32[5,1,96,128]{3,2,1,0:T(8,128)S(1)}, u32[]{:S(2)}, u32[]{:S(2)}) collective-permute-start(f32[5,1,96,128]{3,2,1,0:T(8,128)S(1)} %get-tuple-element.155), channel_id=1, source_target_pairs={{1,0},{2,1},{3,2},{4,3},{5,4},{6,5},{7,6},{8,7},{9,8},{10,9},{11,1... | collective-permute-start | bytes 737288 | tf_op jit(solution)/shard_map/ppermute | solution.py:27
  266.6 11.3 %collective-permute-start.23 = (f32[5,1,96,128]{3,2,1,0:T(8,128)S(1)}, f32[5,1,96,128]{3,2,1,0:T(8,128)S(1)}, u32[]{:S(2)}, u32[]{:S(2)}) collective-permute-start(f32[5,1,96,128]{3,2,1,0:T(8,128)S(1)} %get-tuple-element.152), channel_id=1, source_target_pairs={{0,1},{1,2},{2,3},{3,4},{4,5},{5,6},{6,7},{7,8},{8,9},{9,10},{10,1... | collective-permute-start | bytes 737288 | tf_op jit(solution)/shard_map/ppermute | solution.py:25
  268.5 11.1 %collective-permute-start.24 = (f32[5,1,96,128]{3,2,1,0:T(8,128)S(1)}, f32[5,1,96,128]{3,2,1,0:T(8,128)S(1)}, u32[]{:S(2)}, u32[]{:S(2)}) collective-permute-start(f32[5,1,96,128]{3,2,1,0:T(8,128)S(1)} %get-tuple-element.153), channel_id=1, source_target_pairs={{1,0},{2,1},{3,2},{4,3},{5,4},{6,5},{7,6},{8,7},{9,8},{10,9},{11,1... | collective-permute-start | bytes 737288 | tf_op jit(solution)/shard_map/ppermute | solution.py:27
  280.7 11.3 %collective-permute-start.25 = (f32[5,1,96,128]{3,2,1,0:T(8,128)S(1)}, f32[5,1,96,128]{3,2,1,0:T(8,128)S(1)}, u32[]{:S(2)}, u32[]{:S(2)}) collective-permute-start(f32[5,1,96,128]{3,2,1,0:T(8,128)S(1)} %get-tuple-element.150), channel_id=1, source_target_pairs={{0,1},{1,2},{2,3},{3,4},{4,5},{5,6},{6,7},{7,8},{8,9},{9,10},{10,1... | collective-permute-start | bytes 737288 | tf_op jit(solution)/shard_map/ppermute | solution.py:25
  282.6 11.1 %collective-permute-start.26 = (f32[5,1,96,128]{3,2,1,0:T(8,128)S(1)}, f32[5,1,96,128]{3,2,1,0:T(8,128)S(1)}, u32[]{:S(2)}, u32[]{:S(2)}) collective-permute-start(f32[5,1,96,128]{3,2,1,0:T(8,128)S(1)} %get-tuple-element.151), channel_id=1, source_target_pairs={{1,0},{2,1},{3,2},{4,3},{5,4},{6,5},{7,6},{8,7},{9,8},{10,9},{11,1... | collective-permute-start | bytes 737288 | tf_op jit(solution)/shard_map/ppermute | solution.py:27
  (33 other events, 431.7 us)
where the time goes:
time: 298 us; the launch traced here: 296 us
  starting transfers between devices  150 us (50%)
  waiting for transfers between devices  107 us (36%)
  other arithmetic  33.3 us (11%)
  local copies, waits for them, and re-layouts  4.41 us (1%)
    ppermute x19, starting transfers between devices, with_halo(): lax.ppermute(head, axis, [((i + 1) % count, i) for i in range(ends)])  97 us
    ppermute x19, waiting for transfers between devices, with_halo(): lax.ppermute(tail, axis, [(i, (i + 1) % count) for i in range(ends)])  71.4 us
    ppermute x19, starting transfers between devices, with_halo(): lax.ppermute(tail, axis, [(i, (i + 1) % count) for i in range(ends)])  40.6 us
    ppermute x3, waiting for transfers between devices, passed_along(): lax.ppermute(value, axis, [(source, source + steps) for source in range(f...  17.4 us
    ppermute x19, waiting for transfers between devices, with_halo(): lax.ppermute(head, axis, [((i + 1) % count, i) for i in range(ends)])  14.1 us
    dynamic_update_slice x8, other arithmetic, on_device(): lax.scan(advance, jnp.zeros(gathered.shape[1:], jnp.float32), gathered)  12.4 us
    add x8, other arithmetic, relax(): updated = current + damping * freedom * residue / diagonal  8.93 us
    ppermute x3, starting transfers between devices, passed_along(): lax.ppermute(value, axis, [(source, source + steps) for source in range(f...  8.16 us
  transfers between devices with their start and end apart: 42, of which 28 were waited for; matrix products, arithmetic and copies ran while one was open for 4% of the time, Pallas kernels for 0%

commit v1 on v0

v1 whole, which is shorter than its diff:
```python
import jax
import jax.numpy as jnp
from jax import lax
from jax.sharding import PartitionSpec as P

PASSES = 4
DAMPING = 0.8
LATERAL = 0.06
AXIAL = 0.12


def pad_across(values):
    return jnp.pad(values, ((0, 0), (0, 0), (1, 1), (1, 1)))


def balance(cells, former, mobile, rate_field, forcing):
    current = cells[:, 1:-1]
    middle = mobile[:, 1:-1]
    spread = pad_across(middle)
    below_x = 0.5 * (middle + mobile[:, :-2])
    above_x = 0.5 * (middle + mobile[:, 2:])
    below_y = 0.5 * (middle + spread[:, :, :-2, 1:-1])
    above_y = 0.5 * (middle + spread[:, :, 2:, 1:-1])
    below_z = 0.5 * (middle + spread[:, :, 1:-1, :-2])
    above_z = 0.5 * (middle + spread[:, :, 1:-1, 2:])
    beside_all = pad_across(current)
    lower_z = beside_all[:, :, 1:-1, :-2]
    summed = below_x + above_x + below_y + above_y + below_z + above_z
    inflow = (
        below_x * cells[:, :-2]
        + above_x * cells[:, 2:]
        + below_y * beside_all[:, :, :-2, 1:-1]
        + above_y * beside_all[:, :, 2:, 1:-1]
        + below_z * lower_z
        + above_z * beside_all[:, :, 1:-1, 2:]
        - summed * current
    )
    carried = below_z * lower_z - above_z * current
    magnitude = jnp.abs(current)
    excess = current - former - inflow - 0.5 * carried + 0.5 * rate_field * current * magnitude
    residue = forcing - excess
    diagonal = 1.0 + summed + 0.5 * above_z + rate_field * magnitude
    return (residue, diagonal, current)


def inner(values, dim, cut):
    return lax.slice_in_dim(values, cut, values.shape[dim] - cut, axis=dim)


def sweep(cells, opening, mobile, rate_field, freedom, forcing):
    for number in range(PASSES):
        first = inner(opening, 0, number)[None]
        former = jnp.concatenate([first, cells[:-1, 1:-1]], axis=0)
        residue, diagonal, current = balance(
            cells,
            former,
            inner(mobile, 0, number)[None],
            inner(rate_field, 0, number)[None],
            inner(forcing, 1, number),
        )
        cells = current + DAMPING * inner(freedom, 0, number)[None] * residue / diagonal
    return cells


def region_rates(labels, rates):
    matches = labels[None] == jnp.arange(rates.shape[0], dtype=jnp.int32)[:, None, None, None]
    return jnp.sum(jnp.where(matches, rates[:, None, None, None], 0.0), axis=0)


def coarsen(values):
    lead = values.shape[:-3]
    planes, across, depth_z = values.shape[-3:]
    grouped = values.reshape(lead + (planes // 2, 2, across // 2, 2, depth_z))
    return 0.25 * jnp.sum(grouped, axis=(-4, -2))


def prolong(correction):
    return jnp.repeat(jnp.repeat(correction, 2, axis=-3), 2, axis=-2)


class Coupling:
    def __init__(self, mob, inside):
        centre = mob[1:-1]
        padded = jnp.pad(centre, ((0, 0), (1, 1), (1, 1)))
        keep = inside[1:-1, None, None]
        half = 0.5 * LATERAL * keep
        axial = 0.5 * AXIAL * keep
        self.xl = half * (centre + mob[:-2])
        self.xh = half * (centre + mob[2:])
        self.yl = half * (centre + padded[:, :-2, 1:-1])
        self.yh = half * (centre + padded[:, 2:, 1:-1])
        self.zl = axial * (centre + padded[:, 1:-1, :-2])
        self.zh = axial * (centre + padded[:, 1:-1, 2:])
        self.own = keep - (self.xl + self.xh + self.yl + self.yh + self.zl + self.zh)

    def step(self, values):
        planes = values.shape[-3] - 2
        cut = (self.own.shape[0] - planes) // 2
        take = lambda w: inner(w, 0, cut)
        centre = values[..., 1:-1, :, :]
        pads = [(0, 0)] * (values.ndim - 2) + [(1, 1), (1, 1)]
        padded = jnp.pad(centre, pads)
        return (
            take(self.own) * centre
            + take(self.xl) * values[..., :-2, :, :]
            + take(self.xh) * values[..., 2:, :, :]
            + take(self.yl) * padded[..., :-2, 1:-1]
            + take(self.yh) * padded[..., 2:, 1:-1]
            + take(self.zl) * padded[..., 1:-1, :-2]
            + take(self.zh) * padded[..., 1:-1, 2:]
        )

    def steps(self, values, count):
        for number in range(count):
            values = self.step(values)
        return values


def swap(low, high):
    count = lax.axis_size("space")
    odd = lax.axis_index("space") % 2 == 1
    far_pairs = [(i, i + 1 if i % 2 else i - 1) for i in range(1, count - 1)]
    near_pairs = [(i, i ^ 1) for i in range(count)]
    far = lax.ppermute(jnp.where(odd, high, low), "space", far_pairs)
    near = lax.ppermute(jnp.where(odd, low, high), "space", near_pairs)
    return jnp.where(odd, near, far), jnp.where(odd, far, near)


def arrived(value, steps, shift=0):
    times = lax.axis_size("tm")
    count = lax.axis_size("space")
    if shift == 0:
        return lax.ppermute(value, "tm", [(k, k + steps) for k in range(times - steps)])
    pairs = [
        (k * count + s + shift, (k + steps) * count + s)
        for k in range(times - steps)
        for s in range(count)
        if 0 <= s + shift < count
    ]
    return lax.ppermute(value, ("tm", "space"), pairs)


def on_device(source, initial, mobility, labels, electrode, rates):
    slab = initial.shape[0]
    place = lax.axis_index("space")
    leading = lax.axis_index("tm") == 0
    rate_field = region_rates(labels, rates)
    freedom = 1.0 - electrode.astype(jnp.float32)
    forcing = 0.5 * source
    inside = lambda reach: (
        (2 * place + jnp.arange(-reach, 2 + reach) >= 0)
        & (2 * place + jnp.arange(-reach, 2 + reach) < 2 * lax.axis_size("space"))
    ).astype(jnp.float32)
    flat = lambda v: v.reshape((-1,) + v.shape[-2:])

    def parcel(begin):
        part = slice(begin, begin + slab - 1)
        return jnp.concatenate(
            [flat(forcing[:, part]), initial, mobility, freedom, rate_field[part]], axis=0
        )

    def unpack(block):
        count = slab - 1
        sizes = [4 * count, slab, slab, slab, count]
        out = []
        at = 0
        for size in sizes:
            out.append(block[at : at + size])
            at += size
        out[0] = out[0].reshape((4, count) + block.shape[-2:])
        return out

    below, above = swap(parcel(0), parcel(1))
    below, above = unpack(below), unpack(above)
    wide = lambda i, own, dim=0: jnp.concatenate([below[i], own, above[i]], axis=dim)
    forcing_w = wide(0, forcing, 1)
    initial_w = wide(1, initial)
    mobility_w = wide(2, mobility)
    freedom_w = wide(3, freedom)
    rate_w = wide(4, rate_field)

    start = jnp.broadcast_to(initial_w, (4,) + initial_w.shape)
    first = sweep(start, inner(initial_w, 0, 1), mobility_w, rate_w, inner(freedom_w, 0, 1), forcing_w)

    rough = coarsen(mobility_w)
    block = flat(first)
    pack = lambda c: c.reshape((-1,) + block.shape[-2:])
    low, high = swap(
        jnp.concatenate([block, pack(rough[4:6])], axis=0),
        jnp.concatenate([block, pack(rough[0:2])], axis=0),
    )
    side = lambda b: b[: 4 * slab].reshape((4, slab) + b.shape[-2:])
    coarse_shape = rough.shape[1:]
    rough_of = lambda b: b[4 * slab :].reshape((2,) + coarse_shape)
    states = jnp.concatenate([side(low), first, side(high)], axis=1)
    rough_w = jnp.concatenate([rough_of(low), rough, rough_of(high)], axis=0)

    near = inner(states, 1, 1)
    opening0 = jnp.where(leading, inner(initial_w, 0, 2), 0.0)
    former = jnp.concatenate([opening0[None], inner(states, 1, 2)[:-1]], axis=0)
    residue = balance(
        near,
        former,
        inner(mobility_w, 0, 1)[None],
        inner(rate_w, 0, 1)[None],
        inner(forcing_w, 1, 1),
    )[0]
    base = coarsen(jnp.sum(residue, axis=0)) * inside(1)[:, None, None]
    closing = coarsen(inner(states[3], 0, 2))

    both = jnp.stack([base, closing])
    one = arrived(both, 1)
    two = arrived(both, 2)
    three = arrived(closing, 3)
    opening = arrived(inner(states[3], 0, 1), 1)

    coupling1 = Coupling(inner(rough_w, 0, 2), inside(2))
    rhs = base + one[1]
    rhs1 = one[0] + two[1]
    rhs2 = two[0] + three
    pair = jnp.stack([inner(rhs, 0, 1), inner(rhs1, 0, 1)])
    pair = pair + Coupling(inner(rough_w, 0, 3), inside(1)).step(jnp.stack([rhs1, rhs2]))

    older = [arrived(pair, 2, d) for d in (-1, 0, 1)]
    older = jnp.concatenate(older, axis=1)
    pair = pair + coupling1.steps(older, 2)

    cargo = lambda c: jnp.concatenate([pair.reshape((4,) + coarse_shape), c], axis=0)
    low, high = swap(cargo(rough_w[8:10]), cargo(rough_w[0:2]))
    older = [arrived(pair, 4, d) for d in (-3, -2, -1, 0, 1, 2, 3)]
    older = jnp.concatenate(older, axis=1)
    pair_of = lambda b: b[:4].reshape(pair.shape)
    rough_far = jnp.concatenate([low[4:], rough_w, high[4:]], axis=0)
    pair_w = jnp.concatenate([pair_of(low), pair, pair_of(high)], axis=1)
    correction = pair_w + Coupling(rough_far, inside(6)).steps(older, 4)

    fine = prolong(correction)
    cells = states + freedom_w[None] * fine[0][None]
    near_free = inner(freedom_w, 0, 1)
    opening = jnp.where(leading, inner(initial_w, 0, 1), opening)
    opening = opening + near_free * inner(fine[1], 0, 1)
    return sweep(cells, opening, mobility_w, rate_w, near_free, forcing_w)


def solution(mesh):
    cells = P("space", None, None)
    times = P("tm", "space", None, None)
    return jax.shard_map(
        on_device,
        mesh=mesh,
        in_specs=(times, cells, cells, cells, cells, P()),
        out_specs=times,
        check_vma=False,
    )
```

time: 298 us -> 194 us (0.65)
  starting transfers between devices: 150 us -> 52.3 us
  waiting for transfers between devices: 107 us -> 44.2 us
  local copies, waits for them, and re-layouts: 4.41 us -> 34 us
  other arithmetic: 33.3 us -> 59 us
    ppermute x41 -> x20, starting transfers between devices: 146 us -> 52.3 us  [the longest x3 20.2 us: swap(): far = lax.ppermute(jnp.where(odd, high, low), 'space', far_pairs)]
    ppermute x41 -> x20, waiting for transfers between devices: 103 us -> 44.2 us  [the longest x3 25.7 us: swap(): far = lax.ppermute(jnp.where(odd, high, low), 'space', far_pairs)]
    unnamed x30 -> x281, local copies, waits for them, and re-layouts: 0.21 us -> 18.6 us
    add x10 -> x22, other arithmetic: 9.77 us -> 27.8 us  [the longest x8 19.7 us: sweep(): current + DAMPING * inner(freedom, 0, number)[None] * residue / diagonal]
    dynamic_update_slice x8 -> x0, other arithmetic: 12.4 us -> none  [on_device(): lax.scan(advance, jnp.zeros(gathered.shape[1:], jnp.float32), gathered)]
    slice x18 -> x80, local copies, waits for them, and re-layouts: 1.62 us -> 13.5 us  [the longest x12 4.23 us: balance(): current = cells[:, 1:-1]]
    reduce_sum x3 -> x4, other arithmetic: 5.45 us -> 14.1 us  [the longest x1 8.13 us: on_device(): base = coarsen(jnp.sum(residue, axis=0)) * inside(1)[:, None, None]]
    mul x7 -> x17, other arithmetic: 1.5 us -> 7.48 us  [the longest x2 2.57 us: coarsen(): return 0.25 * jnp.sum(grouped, axis=(-4, -2))]
  transfers between devices with their start and end apart: 42 -> 20, of which waited for: 28 -> 11; matrix products, arithmetic and copies ran while one was open for 4% -> 6% of each run, Pallas kernels for 0% -> 0%
where the time goes in v1:
time: 194 us; the launch traced here: 192 us
  other arithmetic  59 us (30%)
  starting transfers between devices  52.3 us (27%)
  waiting for transfers between devices  44.2 us (23%)
  local copies, waits for them, and re-layouts  34 us (18%)
  between operations  2.75 us (1%)
    ppermute x3, waiting for transfers between devices, swap(): far = lax.ppermute(jnp.where(odd, high, low), 'space', far_pairs)  25.7 us
    ppermute x3, starting transfers between devices, swap(): far = lax.ppermute(jnp.where(odd, high, low), 'space', far_pairs)  20.2 us
    add x8, other arithmetic, sweep(): current + DAMPING * inner(freedom, 0, number)[None] * residue / diagonal  19.7 us
    unnamed x281, local copies, waits for them, and re-layouts  18.6 us
    ppermute x6, starting transfers between devices, arrived(): lax.ppermute(value, 'tm', [(k, k + steps) for k in range(times - steps)])  15.8 us
    ppermute x8, starting transfers between devices, arrived(): return lax.ppermute(value, ('tm', 'space'), pairs)  15.7 us
    ppermute x8, waiting for transfers between devices, arrived(): return lax.ppermute(value, ('tm', 'space'), pairs)  12.9 us
    reduce_sum x1, other arithmetic, on_device(): base = coarsen(jnp.sum(residue, axis=0)) * inside(1)[:, None, None]  8.13 us
  transfers between devices with their start and end apart: 20, of which 11 were waited for; matrix products, arithmetic and copies ran while one was open for 6% of the time, Pallas kernels for 0%

profile of v1, /device:TPU:6, one launch (start us, length us, event | category | flops | bytes accessed | tf_op | source)
XLA Modules:
  0.0 192.3 jit_solution(2541889340774460389)
XLA Ops:
  5.1 8.7 %collective-permute-start.1 = (f32[27,96,128]{2,1,0:T(8,128)}, f32[27,96,128]{2,1,0:T(8,128)}, u32[]{:S(2)}, u32[]{:S(2)}) collective-permute-start(f32[27,96,128]{2,1,0:T(8,128)} %get-tuple-element.44), channel_id=1, source_target_pairs={{1,2},{2,1},{3,4},{4,3},{5,6},{6,5},{7,8},{8,7},{9,10},{10,9},{11,... | collective-permute-start | bytes 3981320 | tf_op jit(solution)/shard_map/ppermute | solution.py:124
  15.2 14.4 %collective-permute-done.1 = f32[27,96,128]{2,1,0:T(8,128)} collective-permute-done((f32[27,96,128]{2,1,0:T(8,128)}, f32[27,96,128]{2,1,0:T(8,128)}, u32[]{:S(2)}, u32[]{:S(2)}) %collective-permute-start.1) | collective-permute-done | bytes 1327136 | tf_op jit(solution)/shard_map/ppermute | solution.py:124
  35.9 2.7 %fusion.34 = f32[4,10,96,128]{3,2,1,0:T(8,128)S(1)} fusion(f32[4,10,96,128]{3,2,1,0:T(8,128)S(1)} %broadcast_in_dim.70, f32[3,10,96,128]{3,2,1,0:T(8,128)S(1)} %broadcast_in_dim.72, f32[1,10,96,128]{3,2,1,0:T(8,128)S(1)} %get-tuple-element.64, f32[10,96,128]{2,1,0:T(8,128)S(1)} %get-tuple-element.39, f32[10,96,128]{2,1,0:T(8,128)S(1)} %get-tuple-element.57, ...), kind=kLoop, calls=%fused_computation.80 | loop fusion | flops 10813440 | bytes 12779520 | tf_op jit(solution)/shard_map/add | solution.py:61
  44.6 2.3 %fusion.47 = f32[4,8,96,128]{3,2,1,0:T(8,128)S(1)} fusion(f32[4,8,96,128]{3,2,1,0:T(8,128)S(1)} %slice-done.1, f32[4,10,96,128]{3,2,1,0:T(8,128)S(1)} %copy-done.3, f32[3,8,96,128]{3,2,1,0:T(8,128)S(1)} %slice.1129, f32[1,8,96,128]{3,2,1,0:T(8,128)S(1)} %get-tuple-element.63, f32[4,10,96,128]{3,2,1,0:T(8,128)S(1)} %pad_maximum_fusion.1, ...), kind=kLoop, calls=%fused_computation.101 | loop fusion | flops 11796480 | bytes 13762560 | tf_op jit(solution)/shard_map/add | solution.py:61
  54.7 2.1 %reduce_sum.48 = f32[6,48,128]{2,1,0:T(8,128)} reduce(f32[6,2,48,2,128]{4,3,2,1,0:T(2,128)} %bitcast.141, f32[]{:T(128)} %constant.32.clone.1), dimensions={1,3}, to_apply=%region_1.2 | reduce | flops 110592 | bytes 737284 | tf_op jit(solution)/shard_map/reduce_sum | solution.py:74
  61.7 2.0 %fusion.130 = f32[4,4,96,128]{3,2,1,0:T(8,128)S(1)} fusion(f32[4,4,96,128]{3,2,1,0:T(8,128)S(1)} %slice-done.3, f32[4,6,96,128]{3,2,1,0:T(8,128)S(1)} %copy-done.7, f32[3,4,96,128]{3,2,1,0:T(8,128)S(1)} %copy-done.85, f32[1,4,96,128]{3,2,1,0:T(8,128)S(1)} %bitcast.157, f32[4,96,128]{2,1,0:T(8,128)S(1)} %select_reduce_fusion, ...), kind=kLoop, calls=%fused_computation.222 | loop fusion | flops 6094848 | bytes 6881280 | tf_op jit(solution)/shard_map/add | solution.py:61
  64.3 7.3 %collective-permute-start.3 = (f32[17,96,128]{2,1,0:T(8,128)S(1)}, f32[17,96,128]{2,1,0:T(8,128)S(1)}, u32[]{:S(2)}, u32[]{:S(2)}) collective-permute-start(f32[17,96,128]{2,1,0:T(8,128)S(1)} %get-tuple-element.59), channel_id=1, source_target_pairs={{1,2},{2,1},{3,4},{4,3},{5,6},{6,5},{7,8},{8,7},{9,10},{10,9},{11,... | collective-permute-start | bytes 2506760 | tf_op jit(solution)/shard_map/ppermute | solution.py:124
  73.6 8.1 %collective-permute-done.3 = f32[17,96,128]{2,1,0:T(8,128)S(1)} collective-permute-done((f32[17,96,128]{2,1,0:T(8,128)S(1)}, f32[17,96,128]{2,1,0:T(8,128)S(1)}, u32[]{:S(2)}, u32[]{:S(2)}) %collective-permute-start.3) | collective-permute-done | bytes 835616 | tf_op jit(solution)/shard_map/ppermute | solution.py:124
  90.8 8.1 %fusion.83 = f32[8,96,128]{2,1,0:T(8,128)} fusion(f32[4,8,96,128]{3,2,1,0:T(8,128)} %slice.1161, f32[4,12,96,128]{3,2,1,0:T(8,128)} %copy-done.1, f32[3,8,96,128]{3,2,1,0:T(8,128)} %slice.1162, f32[1,8,96,128]{3,2,1,0:T(8,128)} %get-tuple-element.62, f32[4,10,96,128]{3,2,1,0:T(8,128)S(1)} %pad_maximum_fusion.1, f32[8,96,128]{2,1,0:T(8,128)} %copy-done.39, ...), kind=kLoop, calls=%fused_computation.146 | loop fusion | flops 10125312 | bytes 11403264 | tf_op jit(solution)/shard_map/reduce_sum | solution.py:208
  102.8 3.6 %collective-permute-start.4 = (f32[2,4,48,128]{3,2,1,0:T(8,128)S(1)}, f32[2,4,48,128]{3,2,1,0:T(8,128)S(1)}, u32[]{:S(2)}, u32[]{:S(2)}) collective-permute-start(f32[2,4,48,128]{3,2,1,0:T(8,128)S(1)} %pad_maximum_fusion.10), channel_id=1, source_target_pairs={{0,32},{32,64},{64,96},{96,128},{128,160},{160,192},{192,224},{1,3... | collective-permute-start | bytes 589832 | tf_op jit(solution)/shard_map/ppermute | solution.py:133
  106.5 4.8 %collective-permute-start.5 = (f32[2,4,48,128]{3,2,1,0:T(8,128)S(1)}, f32[2,4,48,128]{3,2,1,0:T(8,128)S(1)}, u32[]{:S(2)}, u32[]{:S(2)}) collective-permute-start(f32[2,4,48,128]{3,2,1,0:T(8,128)S(1)} %pad_maximum_fusion.10), channel_id=1, source_target_pairs={{0,64},{32,96},{64,128},{96,160},{128,192},{160,224},{1,65},{33,97... | collective-permute-start | bytes 589832 | tf_op jit(solution)/shard_map/ppermute | solution.py:133
  112.8 1.9 collective-permute-start.6
  114.7 2.3 %collective-permute-done.5 = f32[2,4,48,128]{3,2,1,0:T(8,128)S(1)} collective-permute-done((f32[2,4,48,128]{3,2,1,0:T(8,128)S(1)}, f32[2,4,48,128]{3,2,1,0:T(8,128)S(1)}, u32[]{:S(2)}, u32[]{:S(2)}) %collective-permute-start.5) | collective-permute-done | bytes 196640 | tf_op jit(solution)/shard_map/ppermute | solution.py:133
  117.1 3.1 %collective-permute-done.6 = f32[4,48,128]{2,1,0:T(8,128)S(1)} collective-permute-done((f32[4,48,128]{2,1,0:T(8,128)S(1)}, f32[4,48,128]{2,1,0:T(8,128)S(1)}, u32[]{:S(2)}, u32[]{:S(2)}) %collective-permute-start.6) | collective-permute-done | bytes 98336 | tf_op jit(solution)/shard_map/ppermute | solution.py:133
  120.5 6.1 %collective-permute-start.9 = (f32[2,2,48,128]{3,2,1,0:T(8,128)S(1)}, f32[2,2,48,128]{3,2,1,0:T(8,128)S(1)}, u32[]{:S(2)}, u32[]{:S(2)}) collective-permute-start(f32[2,2,48,128]{3,2,1,0:T(8,128)S(1)} %fusion.264), channel_id=1, source_target_pairs={{1,64},{2,65},{3,66},{4,67},{5,68},{6,69},{7,70},{8,71},{9,72},{10... | collective-permute-start | bytes 294920 | tf_op jit(solution)/shard_map/ppermute | solution.py:140
  128.5 1.9 collective-permute-start.7
  133.1 2.3 %collective-permute-start.19 = (f32[10,96,128]{2,1,0:T(8,128)S(1)}, f32[10,96,128]{2,1,0:T(8,128)S(1)}, u32[]{:S(2)}, u32[]{:S(2)}) collective-permute-start(f32[10,96,128]{2,1,0:T(8,128)S(1)} %slice_bitcast_fusion), channel_id=1, source_target_pairs={{0,32},{32,64},{64,96},{96,128},{128,160},{160,192},{192,224},{1,3... | collective-permute-start | bytes 1474568 | tf_op jit(solution)/shard_map/ppermute | solution.py:133
  135.6 5.7 %collective-permute-done.7 = f32[2,2,48,128]{3,2,1,0:T(8,128)S(1)} collective-permute-done((f32[2,2,48,128]{3,2,1,0:T(8,128)S(1)}, f32[2,2,48,128]{3,2,1,0:T(8,128)S(1)}, u32[]{:S(2)}, u32[]{:S(2)}) %collective-permute-start.7) | collective-permute-done | bytes 98336 | tf_op jit(solution)/shard_map/ppermute | solution.py:140
  146.9 4.9 %collective-permute-done.12 = f32[2,2,48,128]{3,2,1,0:T(8,128)S(1)} collective-permute-done((f32[2,2,48,128]{3,2,1,0:T(8,128)S(1)}, f32[2,2,48,128]{3,2,1,0:T(8,128)S(1)}, u32[]{:S(2)}, u32[]{:S(2)}) %collective-permute-start.12) | collective-permute-done | bytes 98336 | tf_op jit(solution)/shard_map/ppermute | solution.py:140
  156.0 4.2 %collective-permute-start.11 = (f32[6,48,128]{2,1,0:T(8,128)S(1)}, f32[6,48,128]{2,1,0:T(8,128)S(1)}, u32[]{:S(2)}, u32[]{:S(2)}) collective-permute-start(f32[6,48,128]{2,1,0:T(8,128)S(1)} %get-tuple-element.99), channel_id=1, source_target_pairs={{1,2},{2,1},{3,4},{4,3},{5,6},{6,5},{7,8},{8,7},{9,10},{10,9},{11,... | collective-permute-start | bytes 442376 | tf_op jit(solution)/shard_map/ppermute | solution.py:124
  162.8 3.3 %collective-permute-done.11 = f32[6,48,128]{2,1,0:T(8,128)S(1)} collective-permute-done((f32[6,48,128]{2,1,0:T(8,128)S(1)}, f32[6,48,128]{2,1,0:T(8,128)S(1)}, u32[]{:S(2)}, u32[]{:S(2)}) %collective-permute-start.11) | collective-permute-done | bytes 147488 | tf_op jit(solution)/shard_map/ppermute | solution.py:124
  175.5 4.9 %fusion.12 = f32[4,10,96,128]{3,2,1,0:T(8,128)S(1)} fusion(f32[4,10,96,128]{3,2,1,0:T(8,128)S(1)} %slice-done, f32[4,12,96,128]{3,2,1,0:T(8,128)} %copy-done, f32[3,10,96,128]{3,2,1,0:T(8,128)S(1)} %slice.1237, f32[1,10,96,128]{3,2,1,0:T(8,128)S(1)} %bitcast.142, f32[10,96,128]{2,1,0:T(8,128)S(1)} %copy-done.42, f32[10,96,128]{2,1,0:T(8,128)S(1)} %copy-done.86, ...), kind=kLoop, calls=%fused_computation.53 | loop fusion | flops 15728640 | bytes 17203200 | tf_op jit(solution)/shard_map/add | solution.py:61
  182.6 2.4 %fusion.76 = f32[4,8,96,128]{3,2,1,0:T(8,128)S(1)} fusion(f32[4,8,96,128]{3,2,1,0:T(8,128)S(1)} %slice.1240, f32[4,10,96,128]{3,2,1,0:T(8,128)S(1)} %fusion.12, f32[3,8,96,128]{3,2,1,0:T(8,128)S(1)} %slice.1242, f32[1,8,96,128]{3,2,1,0:T(8,128)S(1)} %slice_bitcast_fusion.2, f32[4,10,96,128]{3,2,1,0:T(8,128)S(1)} %pad_maximum_fusion.1, ...), kind=kLoop, calls=%fused_computation.130 | loop fusion | flops 11796480 | bytes 13762560 | tf_op jit(solution)/shard_map/add | solution.py:61
  190.3 2.0 %fusion.146 = f32[4,4,96,128]{3,2,1,0:T(8,128)} fusion(f32[4,4,96,128]{3,2,1,0:T(8,128)S(1)} %slice.1250, f32[4,6,96,128]{3,2,1,0:T(8,128)S(1)} %fusion.112, f32[3,4,96,128]{3,2,1,0:T(8,128)S(1)} %slice.1252, f32[1,4,96,128]{3,2,1,0:T(8,128)S(1)} %slice_bitcast_fusion.9, f32[4,96,128]{2,1,0:T(8,128)S(1)} %select_reduce_fusion, ...), kind=kLoop, calls=%fused_computation.238 | loop fusion | flops 6094848 | bytes 6881280 | tf_op jit(solution)/shard_map/add | solution.py:61
  (465 shorter events, 80.5 us)
Async XLA Ops:
  3.3 30.5 %copy-start.94 = (f32[4,96,128]{2,1,0:T(8,128)}, f32[4,96,128]{2,1,0:T(8,128)S(1)}, u32[]{:S(2)}) copy-start(f32[4,96,128]{2,1,0:T(8,128)S(1)} %get-tuple-element.106) | copy-start | bytes 589828
  5.1 10.1 %collective-permute-start = (f32[27,96,128]{2,1,0:T(8,128)}, f32[27,96,128]{2,1,0:T(8,128)}, u32[]{:S(2)}, u32[]{:S(2)}) collective-permute-start(f32[27,96,128]{2,1,0:T(8,128)} %get-tuple-element.43), channel_id=1, source_target_pairs={{0,1},{1,0},{2,3},{3,2},{4,5},{5,4},{6,7},{7,6},{8,9},{9,8},{10,11... | collective-permute-start | bytes 3981320 | tf_op jit(solution)/shard_map/ppermute | solution.py:125
  5.1 24.5 %collective-permute-start.1 = (f32[27,96,128]{2,1,0:T(8,128)}, f32[27,96,128]{2,1,0:T(8,128)}, u32[]{:S(2)}, u32[]{:S(2)}) collective-permute-start(f32[27,96,128]{2,1,0:T(8,128)} %get-tuple-element.44), channel_id=1, source_target_pairs={{1,2},{2,1},{3,4},{4,3},{5,6},{6,5},{7,8},{8,7},{9,10},{10,9},{11,... | collective-permute-start | bytes 3981320 | tf_op jit(solution)/shard_map/ppermute | solution.py:124
  31.9 22.1 %copy-start.14 = (f32[12,96,128]{2,1,0:T(8,128)}, f32[12,96,128]{2,1,0:T(8,128)S(1)}, u32[]{:S(2)}) copy-start(f32[12,96,128]{2,1,0:T(8,128)S(1)} %get-tuple-element.67) | copy-start | bytes 1769476
  63.8 19.4 %copy-start.8 = (f32[4,4,96,128]{3,2,1,0:T(8,128)}, f32[4,4,96,128]{3,2,1,0:T(8,128)S(1)}, u32[]{:S(2)}) copy-start(f32[4,4,96,128]{3,2,1,0:T(8,128)S(1)} %fusion.130) | copy-start | bytes 2359300
  64.0 9.6 %collective-permute-start.2 = (f32[17,96,128]{2,1,0:T(8,128)S(1)}, f32[17,96,128]{2,1,0:T(8,128)S(1)}, u32[]{:S(2)}, u32[]{:S(2)}) collective-permute-start(f32[17,96,128]{2,1,0:T(8,128)S(1)} %get-tuple-element.58), channel_id=1, source_target_pairs={{0,1},{1,0},{2,3},{3,2},{4,5},{5,4},{6,7},{7,6},{8,9},{9,8},{10,11... | collective-permute-start | bytes 2506760 | tf_op jit(solution)/shard_map/ppermute | solution.py:125
  64.3 17.4 %collective-permute-start.3 = (f32[17,96,128]{2,1,0:T(8,128)S(1)}, f32[17,96,128]{2,1,0:T(8,128)S(1)}, u32[]{:S(2)}, u32[]{:S(2)}) collective-permute-start(f32[17,96,128]{2,1,0:T(8,128)S(1)} %get-tuple-element.59), channel_id=1, source_target_pairs={{1,2},{2,1},{3,4},{4,3},{5,6},{6,5},{7,8},{8,7},{9,10},{10,9},{11,... | collective-permute-start | bytes 2506760 | tf_op jit(solution)/shard_map/ppermute | solution.py:124
  102.8 17.5 %copy-start.120 = (f32[2,48,128]{2,1,0:T(8,128)S(1)}, f32[2,48,128]{2,1,0:T(8,128)}, u32[]{:S(2)}) copy-start(f32[2,48,128]{2,1,0:T(8,128)} %get-tuple-element.19) | copy-start | bytes 147460
  102.8 11.9 %collective-permute-start.4 = (f32[2,4,48,128]{3,2,1,0:T(8,128)S(1)}, f32[2,4,48,128]{3,2,1,0:T(8,128)S(1)}, u32[]{:S(2)}, u32[]{:S(2)}) collective-permute-start(f32[2,4,48,128]{3,2,1,0:T(8,128)S(1)} %pad_maximum_fusion.10), channel_id=1, source_target_pairs={{0,32},{32,64},{64,96},{96,128},{128,160},{160,192},{192,224},{1,3... | collective-permute-start | bytes 589832 | tf_op jit(solution)/shard_map/ppermute | solution.py:133
  106.5 10.5 %collective-permute-start.5 = (f32[2,4,48,128]{3,2,1,0:T(8,128)S(1)}, f32[2,4,48,128]{3,2,1,0:T(8,128)S(1)}, u32[]{:S(2)}, u32[]{:S(2)}) collective-permute-start(f32[2,4,48,128]{3,2,1,0:T(8,128)S(1)} %pad_maximum_fusion.10), channel_id=1, source_target_pairs={{0,64},{32,96},{64,128},{96,160},{128,192},{160,224},{1,65},{33,97... | collective-permute-start | bytes 589832 | tf_op jit(solution)/shard_map/ppermute | solution.py:133
  112.8 7.4 %collective-permute-start.6 = (f32[4,48,128]{2,1,0:T(8,128)S(1)}, f32[4,48,128]{2,1,0:T(8,128)S(1)}, u32[]{:S(2)}, u32[]{:S(2)}) collective-permute-start(f32[4,48,128]{2,1,0:T(8,128)S(1)} %copy-done.129), channel_id=1, source_target_pairs={{0,96},{32,128},{64,160},{96,192},{128,224},{1,97},{33,129},{65,16... | collective-permute-start | bytes 294920 | tf_op jit(solution)/shard_map/ppermute | solution.py:133
  120.5 14.9 %collective-permute-start.9 = (f32[2,2,48,128]{3,2,1,0:T(8,128)S(1)}, f32[2,2,48,128]{3,2,1,0:T(8,128)S(1)}, u32[]{:S(2)}, u32[]{:S(2)}) collective-permute-start(f32[2,2,48,128]{3,2,1,0:T(8,128)S(1)} %fusion.264), channel_id=1, source_target_pairs={{1,64},{2,65},{3,66},{4,67},{5,68},{6,69},{7,70},{8,71},{9,72},{10... | collective-permute-start | bytes 294920 | tf_op jit(solution)/shard_map/ppermute | solution.py:140
  126.6 9.0 %collective-permute-start.8 = (f32[2,2,48,128]{3,2,1,0:T(8,128)S(1)}, f32[2,2,48,128]{3,2,1,0:T(8,128)S(1)}, u32[]{:S(2)}, u32[]{:S(2)}) collective-permute-start(f32[2,2,48,128]{3,2,1,0:T(8,128)S(1)} %fusion.264), channel_id=1, source_target_pairs={{0,64},{32,96},{64,128},{96,160},{128,192},{160,224},{1,65},{33,97... | collective-permute-start | bytes 294920 | tf_op jit(solution)/shard_map/ppermute | solution.py:133
  128.5 12.8 %collective-permute-start.7 = (f32[2,2,48,128]{3,2,1,0:T(8,128)S(1)}, f32[2,2,48,128]{3,2,1,0:T(8,128)S(1)}, u32[]{:S(2)}, u32[]{:S(2)}) collective-permute-start(f32[2,2,48,128]{3,2,1,0:T(8,128)S(1)} %fusion.264), channel_id=1, source_target_pairs={{0,65},{1,66},{2,67},{3,68},{4,69},{5,70},{6,71},{7,72},{8,73},{9,... | collective-permute-start | bytes 294920 | tf_op jit(solution)/shard_map/ppermute | solution.py:140
  133.1 39.5 %collective-permute-start.19 = (f32[10,96,128]{2,1,0:T(8,128)S(1)}, f32[10,96,128]{2,1,0:T(8,128)S(1)}, u32[]{:S(2)}, u32[]{:S(2)}) collective-permute-start(f32[10,96,128]{2,1,0:T(8,128)S(1)} %slice_bitcast_fusion), channel_id=1, source_target_pairs={{0,32},{32,64},{64,96},{96,128},{128,160},{160,192},{192,224},{1,3... | collective-permute-start | bytes 1474568 | tf_op jit(solution)/shard_map/ppermute | solution.py:133
  141.7 10.2 %collective-permute-start.12 = (f32[2,2,48,128]{3,2,1,0:T(8,128)S(1)}, f32[2,2,48,128]{3,2,1,0:T(8,128)S(1)}, u32[]{:S(2)}, u32[]{:S(2)}) collective-permute-start(f32[2,2,48,128]{3,2,1,0:T(8,128)S(1)} %fusion.283), channel_id=1, source_target_pairs={{0,131},{1,132},{2,133},{3,134},{4,135},{5,136},{6,137},{7,138},{8... | collective-permute-start | bytes 294920 | tf_op jit(solution)/shard_map/ppermute | solution.py:140
  143.0 10.3 %collective-permute-start.13 = (f32[2,2,48,128]{3,2,1,0:T(8,128)S(1)}, f32[2,2,48,128]{3,2,1,0:T(8,128)S(1)}, u32[]{:S(2)}, u32[]{:S(2)}) collective-permute-start(f32[2,2,48,128]{3,2,1,0:T(8,128)S(1)} %fusion.283), channel_id=1, source_target_pairs={{0,130},{1,131},{2,132},{3,133},{4,134},{5,135},{6,136},{7,137},{8... | collective-permute-start | bytes 294920 | tf_op jit(solution)/shard_map/ppermute | solution.py:140
  144.3 10.3 %collective-permute-start.14 = (f32[2,2,48,128]{3,2,1,0:T(8,128)S(1)}, f32[2,2,48,128]{3,2,1,0:T(8,128)S(1)}, u32[]{:S(2)}, u32[]{:S(2)}) collective-permute-start(f32[2,2,48,128]{3,2,1,0:T(8,128)S(1)} %fusion.283), channel_id=1, source_target_pairs={{0,129},{1,130},{2,131},{3,132},{4,133},{5,134},{6,135},{7,136},{8... | collective-permute-start | bytes 294920 | tf_op jit(solution)/shard_map/ppermute | solution.py:140
  145.6 10.4 %collective-permute-start.15 = (f32[2,2,48,128]{3,2,1,0:T(8,128)S(1)}, f32[2,2,48,128]{3,2,1,0:T(8,128)S(1)}, u32[]{:S(2)}, u32[]{:S(2)}) collective-permute-start(f32[2,2,48,128]{3,2,1,0:T(8,128)S(1)} %fusion.283), channel_id=1, source_target_pairs={{0,128},{32,160},{64,192},{96,224},{1,129},{33,161},{65,193},{97,2... | collective-permute-start | bytes 294920 | tf_op jit(solution)/shard_map/ppermute | solution.py:133
  151.9 8.4 %collective-permute-start.16 = (f32[2,2,48,128]{3,2,1,0:T(8,128)S(1)}, f32[2,2,48,128]{3,2,1,0:T(8,128)S(1)}, u32[]{:S(2)}, u32[]{:S(2)}) collective-permute-start(f32[2,2,48,128]{3,2,1,0:T(8,128)S(1)} %fusion.283), channel_id=1, source_target_pairs={{1,128},{2,129},{3,130},{4,131},{5,132},{6,133},{7,134},{8,135},{9... | collective-permute-start | bytes 294920 | tf_op jit(solution)/shard_map/ppermute | solution.py:140
  153.3 8.6 %collective-permute-start.17 = (f32[2,2,48,128]{3,2,1,0:T(8,128)S(1)}, f32[2,2,48,128]{3,2,1,0:T(8,128)S(1)}, u32[]{:S(2)}, u32[]{:S(2)}) collective-permute-start(f32[2,2,48,128]{3,2,1,0:T(8,128)S(1)} %fusion.283), channel_id=1, source_target_pairs={{2,128},{3,129},{4,130},{5,131},{6,132},{7,133},{8,134},{9,135},{1... | collective-permute-start | bytes 294920 | tf_op jit(solution)/shard_map/ppermute | solution.py:140
  154.6 8.1 %collective-permute-start.18 = (f32[2,2,48,128]{3,2,1,0:T(8,128)S(1)}, f32[2,2,48,128]{3,2,1,0:T(8,128)S(1)}, u32[]{:S(2)}, u32[]{:S(2)}) collective-permute-start(f32[2,2,48,128]{3,2,1,0:T(8,128)S(1)} %fusion.283), channel_id=1, source_target_pairs={{3,128},{4,129},{5,130},{6,131},{7,132},{8,133},{9,134},{10,135},{... | collective-permute-start | bytes 294920 | tf_op jit(solution)/shard_map/ppermute | solution.py:140
  156.0 10.1 %collective-permute-start.11 = (f32[6,48,128]{2,1,0:T(8,128)S(1)}, f32[6,48,128]{2,1,0:T(8,128)S(1)}, u32[]{:S(2)}, u32[]{:S(2)}) collective-permute-start(f32[6,48,128]{2,1,0:T(8,128)S(1)} %get-tuple-element.99), channel_id=1, source_target_pairs={{1,2},{2,1},{3,4},{4,3},{5,6},{6,5},{7,8},{8,7},{9,10},{10,9},{11,... | collective-permute-start | bytes 442376 | tf_op jit(solution)/shard_map/ppermute | solution.py:124
  160.2 5.8 %collective-permute-start.10 = (f32[6,48,128]{2,1,0:T(8,128)S(1)}, f32[6,48,128]{2,1,0:T(8,128)S(1)}, u32[]{:S(2)}, u32[]{:S(2)}) collective-permute-start(f32[6,48,128]{2,1,0:T(8,128)S(1)} %get-tuple-element.100), channel_id=1, source_target_pairs={{0,1},{1,0},{2,3},{3,2},{4,5},{5,4},{6,7},{7,6},{8,9},{9,8},{10,11... | collective-permute-start | bytes 442376 | tf_op jit(solution)/shard_map/ppermute | solution.py:125
  (135 other events, 492.6 us)

commit v2 on v1

v2 whole, which is shorter than its diff:
```python
import functools

import jax
import jax.numpy as jnp
from jax import lax
from jax.experimental import pallas as pl
from jax.experimental.pallas import tpu as pltpu
from jax.sharding import PartitionSpec as P

PASSES = 4
DAMPING = 0.8
LATERAL = 0.06
AXIAL = 0.12
STEPS = 4
SLAB = 4
EDGE = 8

VMEM = pl.BlockSpec(memory_space=pltpu.VMEM)
SMEM = pl.BlockSpec(memory_space=pltpu.SMEM)

P_INIT, P_MOB, P_FREE, P_KAP, PARCEL = 12, 16, 20, 24, 27


def shifted(values, by, axis):
    size = values.shape[axis]
    return pltpu.roll(values, by % size, axis)


def parcel_kernel(who, rates, source, initial, mobility, labels, electrode, far, near, kappa, free):
    odd = who[0]

    @pl.loop(0, SLAB)
    def _(p):
        kind = labels[p]
        value = jnp.zeros(kind.shape, jnp.float32)
        for n in range(rates.shape[0]):
            value = jnp.where(kind == n, rates[n], value)
        kappa[p] = value
        open_cell = 1.0 - electrode[p].astype(jnp.float32)
        free[p] = open_cell
        for out in (far, near):
            out[P_INIT + p] = initial[p]
            out[P_MOB + p] = mobility[p]
            out[P_FREE + p] = open_cell

    for out, begin in ((far, odd), (near, 1 - odd)):

        @pl.loop(0, SLAB - 1)
        def _(j):
            out[P_KAP + j] = kappa[begin + j]
            for t in range(STEPS):
                out[3 * t + j] = 0.5 * source[t, begin + j]


def load_static(odd, source, initial, mobility, kappa, free, far, near, force, begin, mob, kap, open_cell):
    rows = pl.ds(EDGE, mobility.shape[1])

    @pl.loop(0, SLAB)
    def _(p):
        begin[4 + p] = initial[p]
        mob[4 + p, rows] = mobility[p]
        open_cell[4 + p] = free[p]
        kap[3 + p] = kappa[p]
        for t in range(STEPS):
            force[t, 3 + p] = 0.5 * source[t, p]
        for block, wide in ((far, 8 * odd), (near, 8 - 8 * odd)):
            begin[wide + p] = block[P_INIT + p]
            mob[wide + p, rows] = block[P_MOB + p]
            open_cell[wide + p] = block[P_FREE + p]

    @pl.loop(0, SLAB - 1)
    def _(p):
        for block, wide in ((far, 7 * odd), (near, 7 - 7 * odd)):
            kap[wide + p] = block[P_KAP + p]
            for t in range(STEPS):
                force[t, wide + p] = block[3 * t + p]

    zero = jnp.zeros((EDGE, mob.shape[2]), jnp.float32)

    @pl.loop(0, mob.shape[0])
    def _(p):
        mob[p, pl.ds(0, EDGE)] = zero
        mob[p, pl.ds(mob.shape[1] - EDGE, EDGE)] = zero


def make_weights(mob, weights, first, last):
    height = mob.shape[1] - 2 * EDGE

    @pl.loop(first, last)
    def _(j):
        for r in range(0, height, 8):
            at = lambda p, d: mob[p, pl.ds(EDGE + r + d, 8)]
            here = at(j + 1, 0)
            lane = lax.broadcasted_iota(jnp.int32, here.shape, 1)
            lowest, highest = lane == 0, lane == here.shape[1] - 1
            xl = 0.5 * (here + at(j, 0))
            xh = 0.5 * (here + at(j + 2, 0))
            yl = 0.5 * (here + at(j + 1, -1))
            yh = 0.5 * (here + at(j + 1, 1))
            zl = 0.5 * (here + jnp.where(lowest, 0.0, shifted(here, 1, 1)))
            zh = 0.5 * (here + jnp.where(highest, 0.0, shifted(here, -1, 1)))
            rows = pl.ds(r, 8)
            weights[j, 0, rows] = xl
            weights[j, 1, rows] = xh
            weights[j, 2, rows] = yl
            weights[j, 3, rows] = yh
            weights[j, 4, rows] = jnp.where(lowest, 0.0, 1.5 * zl)
            weights[j, 5, rows] = jnp.where(highest, 0.0, zh)
            weights[j, 6, rows] = 1.0 + (xl + xh + yl + yh + zl + zh) + 0.5 * zh


def clear_edges(cells):
    zero = jnp.zeros((EDGE, cells.shape[-1]), jnp.float32)
    for b in range(cells.shape[0]):
        for t in range(STEPS):

            @pl.loop(0, cells.shape[2])
            def _(p):
                cells[b, t, p, pl.ds(0, EDGE)] = zero
                cells[b, t, p, pl.ds(cells.shape[3] - EDGE, EDGE)] = zero


def gathered(w, cells, b, t, p, r):
    here = cells[b, t, p, pl.ds(EDGE + r, 8)]
    total = w[0] * cells[b, t, p - 1, pl.ds(EDGE + r, 8)]
    total += w[1] * cells[b, t, p + 1, pl.ds(EDGE + r, 8)]
    total += w[2] * cells[b, t, p, pl.ds(EDGE + r - 1, 8)]
    total += w[3] * cells[b, t, p, pl.ds(EDGE + r + 1, 8)]
    total += w[4] * shifted(here, 1, 1)
    total += w[5] * shifted(here, -1, 1)
    return here, total


def run_sweep(cells, weights, kap, open_cell, force, opening):
    height = cells.shape[3] - 2 * EDGE

    @pl.loop(0, PASSES)
    def _(number):
        b = number % 2

        @pl.loop(number, 10 - number)
        def _(j):
            for r in range(0, height, 8):
                rows = pl.ds(r, 8)
                w = [weights[j, n, rows] for n in range(7)]
                rate = kap[j, rows]
                gain = DAMPING * open_cell[j + 1, rows]
                former = opening[j, rows]
                for t in range(STEPS):
                    here, total = gathered(w, cells, b, t, j + 1, r)
                    pull = rate * jnp.abs(here)
                    residue = force[t, j, rows] + former + total - here * (w[6] + 0.5 * pull)
                    cells[1 - b, t, j + 1, pl.ds(EDGE + r, 8)] = here + gain * residue / (w[6] + pull)
                    former = here


def halved(read):
    return 0.25 * ((read(0, 0) + read(0, 1)) + (read(1, 0) + read(1, 1)))


def first_kernel(who, source, initial, mobility, kappa, free, far, near, to_far, to_near, rough_out,
                 force, begin, mob, kap, open_cell, weights, cells):
    odd = who[0]
    height = mobility.shape[1]
    load_static(odd, source, initial, mobility, kappa, free, far, near, force, begin, mob, kap, open_cell)
    make_weights(mob, weights, 0, 10)
    clear_edges(cells)

    @pl.loop(0, 12)
    def _(p):
        value = begin[p]
        for t in range(STEPS):
            cells[0, t, p, pl.ds(EDGE, height)] = value

    run_sweep(cells, weights, kap, open_cell, force, begin.at[pl.ds(1, 10)])
    half = height // 2
    for a in range(6):
        rough_out[a] = halved(lambda x, y: mob[2 * a + x, pl.ds(EDGE + y, half, stride=2)])
    for out, base in ((to_far, 4 - 4 * odd), (to_near, 4 * odd)):
        for t in range(STEPS):
            for p in range(SLAB):
                out[4 * t + p] = cells[0, t, 4 + p, pl.ds(EDGE, height)]
        out[16, pl.ds(0, half)] = rough_out[base]
        out[16, pl.ds(half, half)] = rough_out[base + 1]


def residual_kernel(who, source, initial, mobility, kappa, free, far, near, own, low_far, low_near,
                    both, closing, force, begin, mob, kap, open_cell, weights, cells, residues):
    odd, leading, place, count = who[0], who[1], who[2], who[3]
    height = mobility.shape[1]
    half = height // 2
    load_static(odd, source, initial, mobility, kappa, free, far, near, force, begin, mob, kap, open_cell)
    make_weights(mob, weights, 1, 9)
    clear_edges(cells)
    rows = pl.ds(EDGE, height)
    for t in range(STEPS):

        @pl.loop(0, SLAB)
        def _(p):
            cells[0, t, 4 + p, rows] = own[4 * t + p]
            cells[0, t, 8 * odd + p, rows] = low_far[4 * t + p]
            cells[0, t, 8 - 8 * odd + p, rows] = low_near[4 * t + p]

    @pl.loop(1, 9)
    def _(j):
        for r in range(0, height, 8):
            rows = pl.ds(r, 8)
            w = [weights[j, n, rows] for n in range(7)]
            rate = kap[j, rows]
            former = jnp.where(leading == 1, begin[j + 1, rows], 0.0)
            acc = jnp.zeros_like(former)
            for t in range(STEPS):
                here, total = gathered(w, cells, 0, t, j + 1, r)
                pull = rate * jnp.abs(here)
                acc += force[t, j, rows] + former + total - here * (w[6] + 0.5 * pull)
                former = here
            residues[j - 1, rows] = acc

    for a in range(4):
        coarse = 2 * place - 1 + a
        inside = jnp.logical_and(coarse >= 0, coarse < 2 * count)
        value = halved(lambda x, y: residues[2 * a + x, pl.ds(y, half, stride=2)])
        both[0, a] = jnp.where(inside, value, 0.0)
        both[1, a] = halved(lambda x, y: cells[0, STEPS - 1, 2 + 2 * a + x, pl.ds(EDGE + y, half, stride=2)])

    @pl.loop(0, 10)
    def _(j):
        closing[j] = cells[0, STEPS - 1, j + 1, pl.ds(EDGE, height)]


def last_kernel(who, source, initial, mobility, kappa, free, far, near, own, low_far, low_near, arriving, correction,
                out, force, begin, mob, kap, open_cell, weights, cells, opening):
    odd, leading = who[0], who[1]
    height = mobility.shape[1]
    half = height // 2
    load_static(odd, source, initial, mobility, kappa, free, far, near, force, begin, mob, kap, open_cell)
    make_weights(mob, weights, 0, 10)
    clear_edges(cells)
    for y in range(2):
        rows = pl.ds(y, half, stride=2)
        into = pl.ds(EDGE + y, half, stride=2)

        @pl.loop(0, SLAB)
        def _(p):
            for block, at in ((own, 4), (low_far, 8 * odd), (low_near, 8 - 8 * odd)):
                plane = at + p
                change = open_cell[plane, rows] * correction[0, plane // 2]
                for t in range(STEPS):
                    cells[0, t, plane, into] = block[4 * t + p, rows] + change

        @pl.loop(0, 10)
        def _(j):
            base = jnp.where(leading == 1, begin[j + 1, rows], arriving[j, rows])
            opening[j, rows] = base + open_cell[j + 1, rows] * correction[1, (j + 1) // 2]

    run_sweep(cells, weights, kap, open_cell, force, opening)
    for t in range(STEPS):
        for p in range(SLAB):
            out[t, p] = cells[0, t, 4 + p, pl.ds(EDGE, height)]


def windows(height, depth):
    plane = (height, depth)
    tall = (height + 2 * EDGE, depth)
    f32 = jnp.float32
    return [
        pltpu.VMEM((STEPS, 10) + plane, f32),
        pltpu.VMEM((12,) + plane, f32),
        pltpu.VMEM((12,) + tall, f32),
        pltpu.VMEM((10,) + plane, f32),
        pltpu.VMEM((12,) + plane, f32),
        pltpu.VMEM((10, 7) + plane, f32),
    ]


def call(kernel, name, inputs, outputs, scratch, scalars=1):
    return pl.pallas_call(
        kernel,
        out_shape=[jax.ShapeDtypeStruct(o, jnp.float32) for o in outputs],
        in_specs=[SMEM] * scalars + [VMEM] * (len(inputs) - scalars),
        out_specs=[VMEM] * len(outputs),
        scratch_shapes=scratch,
        name=name,
        compiler_params=pltpu.CompilerParams(vmem_limit_bytes=28 << 20),
    )(*inputs)


def inner(values, dim, cut):
    return lax.slice_in_dim(values, cut, values.shape[dim] - cut, axis=dim)


class Coupling:
    def __init__(self, mob, inside):
        centre = mob[1:-1]
        padded = jnp.pad(centre, ((0, 0), (1, 1), (1, 1)))
        keep = inside[1:-1, None, None]
        half = 0.5 * LATERAL * keep
        axial = 0.5 * AXIAL * keep
        self.xl = half * (centre + mob[:-2])
        self.xh = half * (centre + mob[2:])
        self.yl = half * (centre + padded[:, :-2, 1:-1])
        self.yh = half * (centre + padded[:, 2:, 1:-1])
        self.zl = axial * (centre + padded[:, 1:-1, :-2])
        self.zh = axial * (centre + padded[:, 1:-1, 2:])
        self.own = keep - (self.xl + self.xh + self.yl + self.yh + self.zl + self.zh)

    def step(self, values):
        planes = values.shape[-3] - 2
        cut = (self.own.shape[0] - planes) // 2
        take = lambda w: inner(w, 0, cut)
        centre = values[..., 1:-1, :, :]
        pads = [(0, 0)] * (values.ndim - 2) + [(1, 1), (1, 1)]
        padded = jnp.pad(centre, pads)
        return (
            take(self.own) * centre
            + take(self.xl) * values[..., :-2, :, :]
            + take(self.xh) * values[..., 2:, :, :]
            + take(self.yl) * padded[..., :-2, 1:-1]
            + take(self.yh) * padded[..., 2:, 1:-1]
            + take(self.zl) * padded[..., 1:-1, :-2]
            + take(self.zh) * padded[..., 1:-1, 2:]
        )

    def steps(self, values, count):
        for number in range(count):
            values = self.step(values)
        return values


def traded(far, near):
    count = lax.axis_size("space")
    far_pairs = [(i, i + 1 if i % 2 else i - 1) for i in range(1, count - 1)]
    near_pairs = [(i, i ^ 1) for i in range(count)]
    return lax.ppermute(far, "space", far_pairs), lax.ppermute(near, "space", near_pairs)


def by_side(odd, far, near):
    return jnp.where(odd, near, far), jnp.where(odd, far, near)


def arrived(value, steps, shift=0):
    times = lax.axis_size("tm")
    count = lax.axis_size("space")
    if shift == 0:
        return lax.ppermute(value, "tm", [(k, k + steps) for k in range(times - steps)])
    pairs = [
        (k * count + s + shift, (k + steps) * count + s)
        for k in range(times - steps)
        for s in range(count)
        if 0 <= s + shift < count
    ]
    return lax.ppermute(value, ("tm", "space"), pairs)


def on_device(source, initial, mobility, labels, electrode, rates):
    _, height, depth = initial.shape
    plane = (height, depth)
    place = lax.axis_index("space")
    odd = place % 2
    leading = lax.axis_index("tm") == 0
    who = jnp.stack([odd, leading.astype(jnp.int32), place, jnp.int32(lax.axis_size("space"))]).astype(jnp.int32)
    inside = lambda reach: (
        (2 * place + jnp.arange(-reach, 2 + reach) >= 0)
        & (2 * place + jnp.arange(-reach, 2 + reach) < 2 * lax.axis_size("space"))
    ).astype(jnp.float32)

    far, near, kappa, free = call(
        parcel_kernel,
        "parcel",
        (who, rates, source, initial, mobility, labels, electrode),
        [(PARCEL,) + plane] * 2 + [initial.shape] * 2,
        [],
        2,
    )
    far, near = traded(far, near)
    static = (who, source, initial, mobility, kappa, free, far, near)
    tall = (height + 2 * EDGE, depth)

    coarse = (height // 2, depth)
    to_far, to_near, rough = call(
        first_kernel,
        "first",
        static,
        [(17,) + plane] * 2 + [(6,) + coarse],
        windows(height, depth) + [pltpu.VMEM((2, STEPS, 12) + tall, jnp.float32)],
    )
    got_far, got_near = traded(to_far, to_near)
    states = (to_far, got_far, got_near)

    both, closing = call(
        residual_kernel,
        "residual",
        static + states,
        [(2, 4) + coarse, (10,) + plane],
        windows(height, depth)
        + [pltpu.VMEM((1, STEPS, 12) + tall, jnp.float32), pltpu.VMEM((8,) + plane, jnp.float32)],
    )
    rough_of = lambda b: b[16].reshape((2,) + coarse)
    low, high = by_side(odd == 1, rough_of(got_far), rough_of(got_near))
    rough_w = jnp.concatenate([low, rough, high], axis=0)

    one = arrived(both, 1)
    two = arrived(both, 2)
    three = arrived(both[1], 3)
    rhs = both[0] + one[1]
    rhs1 = one[0] + two[1]
    rhs2 = two[0] + three
    pair = jnp.stack([inner(rhs, 0, 1), inner(rhs1, 0, 1)])
    pair = pair + Coupling(inner(rough_w, 0, 3), inside(1)).step(jnp.stack([rhs1, rhs2]))

    cargo = lambda c: jnp.concatenate([pair.reshape((4,) + coarse), c], axis=0)
    to_low, to_high = cargo(rough_w[8:10]), cargo(rough_w[0:2])
    low, high = by_side(odd == 1, *traded(*by_side(odd == 1, to_low, to_high)))
    opening = arrived(closing, 1)
    pair_of = lambda b: b[:4].reshape(pair.shape)
    rough_far = jnp.concatenate([low[4:], rough_w, high[4:]], axis=0)
    pair = jnp.concatenate([pair_of(low), pair, pair_of(high)], axis=1)
    low, high = arrived(pair, 2, -1), arrived(pair, 2, 1)
    middle = jnp.where(place == 0, high[:, :2], low[:, 4:])
    older = jnp.concatenate([low[:, :4], middle, high[:, 2:]], axis=1)
    coupling = Coupling(rough_far, inside(6))
    pair = pair + coupling.steps(older, 2)
    older = jnp.concatenate([arrived(pair[:, :4], 4, -2), arrived(pair, 4), arrived(pair[:, 2:], 4, 2)], axis=1)
    correction = pair + coupling.steps(older, 4)

    (density,) = call(
        last_kernel,
        "last",
        static + states + (opening, correction),
        [source.shape],
        windows(height, depth)
        + [pltpu.VMEM((2, STEPS, 12) + tall, jnp.float32), pltpu.VMEM((10,) + plane, jnp.float32)],
    )
    return density


def solution(mesh):
    cells = P("space", None, None)
    times = P("tm", "space", None, None)
    return jax.shard_map(
        on_device,
        mesh=mesh,
        in_specs=(times, cells, cells, cells, cells, P()),
        out_specs=times,
        check_vma=False,
    )
```

time: 194 us -> 352 us (1.81)
  Pallas kernels: 0 us -> 223 us
  other arithmetic: 59 us -> 4.91 us
  local copies, waits for them, and re-layouts: 34 us -> 16.4 us
  waiting for transfers between devices: 44.2 us -> 60.8 us
  starting transfers between devices: 52.3 us -> 45.8 us
    pallas_call x0 -> x4, Pallas kernels: none -> 223 us  [call(): pl.pallas_call(kernel, out_shape=[jax.ShapeDtypeStruct(o, jnp.float32) fo...]
    add x17 -> x3, other arithmetic: 26.2 us -> 0.57 us  [the longest x1 0.28 us: on_device(): correction = pair + coupling.steps(older, 4)]
    reduce_sum x5 -> x0, other arithmetic: 14.2 us -> none  [the longest x1 8.13 us: on_device(): base = coarsen(jnp.sum(residue, axis=0)) * inside(1)[:, None, None]]
    slice x36 -> x4, local copies, waits for them, and re-layouts: 9.84 us -> 0.07 us  [the longest x1 0.03 us: on_device(): pair[:, 2:]]
    ppermute x6 -> x5, waiting for transfers between devices: 5.62 us -> 14.2 us  [arrived(): lax.ppermute(value, 'tm', [(k, k + steps) for k in range(times - steps)])]
    mul x14 -> x0, other arithmetic: 6.72 us -> none  [the longest x2 2.57 us: coarsen(): return 0.25 * jnp.sum(grouped, axis=(-4, -2))]
    ppermute x8 -> x4, waiting for transfers between devices: 12.9 us -> 18.2 us  [arrived(): return lax.ppermute(value, ('tm', 'space'), pairs)]
    ppermute x8 -> x4, starting transfers between devices: 15.7 us -> 11.3 us  [arrived(): return lax.ppermute(value, ('tm', 'space'), pairs)]
  transfers between devices with their start and end apart: 20 -> 15, of which waited for: 11 -> 10; matrix products, arithmetic and copies ran while one was open for 6% -> 2% of each run, Pallas kernels for 0% -> 0%
where the time goes in v2:
time: 352 us; the launch traced here: 351 us
  Pallas kernels  223 us (63%)
  waiting for transfers between devices  60.8 us (17%)
  starting transfers between devices  45.8 us (13%)
  local copies, waits for them, and re-layouts  16.4 us (5%)
  other arithmetic  4.91 us (1%)
    pallas_call x4, Pallas kernels, call(): pl.pallas_call(kernel, out_shape=[jax.ShapeDtypeStruct(o, jnp.float32) fo...  223 us
    ppermute x3, waiting for transfers between devices, traded(): lax.ppermute(far, 'space', far_pairs)  28.4 us
    ppermute x3, starting transfers between devices, traded(): lax.ppermute(far, 'space', far_pairs)  20.8 us
    ppermute x4, waiting for transfers between devices, arrived(): return lax.ppermute(value, ('tm', 'space'), pairs)  18.2 us
    unnamed x44, local copies, waits for them, and re-layouts  15 us
    ppermute x5, waiting for transfers between devices, arrived(): lax.ppermute(value, 'tm', [(k, k + steps) for k in range(times - steps)])  14.2 us
    ppermute x5, starting transfers between devices, arrived(): lax.ppermute(value, 'tm', [(k, k + steps) for k in range(times - steps)])  13.4 us
    ppermute x4, starting transfers between devices, arrived(): return lax.ppermute(value, ('tm', 'space'), pairs)  11.3 us
  transfers between devices with their start and end apart: 15, of which 10 were waited for; matrix products, arithmetic and copies ran while one was open for 2% of the time, Pallas kernels for 0%

profile of v2, /device:TPU:6, one launch (start us, length us, event | category | flops | bytes accessed | tf_op | source)
XLA Modules:
  0.0 351.4 jit_solution(3785211865806207042)
XLA Ops:
  5.6 2.3 parcel.1
  9.2 8.0 %collective-permute-start = (f32[27,96,128]{2,1,0:T(8,128)}, f32[27,96,128]{2,1,0:T(8,128)S(1)}, u32[]{:S(2)}, u32[]{:S(2)}) collective-permute-start(f32[27,96,128]{2,1,0:T(8,128)} %get-tuple-element.16), channel_id=1, source_target_pairs={{1,2},{2,1},{3,4},{4,3},{5,6},{6,5},{7,8},{8,7},{9,10},{10,9},{11,... | collective-permute-start | bytes 3981320 | tf_op jit(solution)/shard_map/ppermute | solution.py:334
  17.4 15.5 %collective-permute-done.far = f32[27,96,128]{2,1,0:T(8,128)S(1)} collective-permute-done((f32[27,96,128]{2,1,0:T(8,128)}, f32[27,96,128]{2,1,0:T(8,128)S(1)}, u32[]{:S(2)}, u32[]{:S(2)}) %collective-permute-start) | collective-permute-done | bytes 1327136 | tf_op jit(solution)/shard_map/ppermute | solution.py:334
  36.6 107.3 %first.1 = (f32[17,96,128]{2,1,0:T(8,128)}, f32[17,96,128]{2,1,0:T(8,128)}, f32[6,48,128]{2,1,0:T(8,128)S(1)}) custom-call(s32[4]{0:T(128)S(1)} %pad_add_fusion.who, f32[4,4,96,128]{3,2,1,0:T(8,128)S(1)} %copy-done.1, f32[4,96,128]{2,1,0:T(8,128)S(1)} %copy-done.3, f32[4,96,128]{2,1,0:T(8,128)S(1)} %copy-done.6, f32[4,96,128]{2,1,0:T(8,128)S(1)} %copy-done.9, ...), custom_call_target="tpu_custom_call" | custom-call | tf_op jit(solution)/shard_map/first/pallas_call | solution.py:277
  144.6 7.2 %collective-permute-start.2 = (f32[17,96,128]{2,1,0:T(8,128)}, f32[17,96,128]{2,1,0:T(8,128)}, u32[]{:S(2)}, u32[]{:S(2)}) collective-permute-start(f32[17,96,128]{2,1,0:T(8,128)} %get-tuple-element.18.own), channel_id=1, source_target_pairs={{1,2},{2,1},{3,4},{4,3},{5,6},{6,5},{7,8},{8,7},{9,10},{10,9},{11,... | collective-permute-start | bytes 2506760 | tf_op jit(solution)/shard_map/ppermute | solution.py:334
  153.9 8.4 %collective-permute-done.2.low_far = f32[17,96,128]{2,1,0:T(8,128)} collective-permute-done((f32[17,96,128]{2,1,0:T(8,128)}, f32[17,96,128]{2,1,0:T(8,128)}, u32[]{:S(2)}, u32[]{:S(2)}) %collective-permute-start.2) | collective-permute-done | bytes 835616 | tf_op jit(solution)/shard_map/ppermute | solution.py:334
  166.0 4.9 %residual.1 = (f32[2,4,48,128]{3,2,1,0:T(8,128)S(1)}, f32[10,96,128]{2,1,0:T(8,128)S(1)}) custom-call(s32[4]{0:T(128)S(1)} %pad_add_fusion.who, f32[4,4,96,128]{3,2,1,0:T(8,128)S(1)} %copy-done.1, f32[4,96,128]{2,1,0:T(8,128)S(1)} %copy-done.4, f32[4,96,128]{2,1,0:T(8,128)S(1)} %copy-done.7, f32[4,96,128]{2,1,0:T(8,128)S(1)} %copy-done.10, ...), custom_call_target="tpu_custom_call" | custom-call | tf_op jit(solution)/shard_map/residual/pallas_call | solution.py:277
  171.0 3.5 collective-permute-start.5
  174.5 4.8 %collective-permute-start.6 = (f32[2,4,48,128]{3,2,1,0:T(8,128)S(1)}, f32[2,4,48,128]{3,2,1,0:T(8,128)S(1)}, u32[]{:S(2)}, u32[]{:S(2)}) collective-permute-start(f32[2,4,48,128]{3,2,1,0:T(8,128)S(1)} %get-tuple-element.21), channel_id=1, source_target_pairs={{0,64},{32,96},{64,128},{96,160},{128,192},{160,224},{1,65},{33,97... | collective-permute-start | bytes 589832 | tf_op jit(solution)/shard_map/ppermute | solution.py:345
  179.3 1.9 collective-permute-start.7
  182.1 2.4 collective-permute-done.6
  184.5 2.2 collective-permute-done.7
  187.0 5.5 %collective-permute-start.9 = (f32[6,48,128]{2,1,0:T(8,128)S(1)}, f32[6,48,128]{2,1,0:T(8,128)S(1)}, u32[]{:S(2)}, u32[]{:S(2)}) collective-permute-start(f32[6,48,128]{2,1,0:T(8,128)S(1)} %get-tuple-element.44), channel_id=1, source_target_pairs={{1,2},{2,1},{3,4},{4,3},{5,6},{6,5},{7,8},{8,7},{9,10},{10,9},{11,... | collective-permute-start | bytes 442376 | tf_op jit(solution)/shard_map/ppermute | solution.py:334
  192.7 4.4 %collective-permute-done.9 = f32[6,48,128]{2,1,0:T(8,128)S(1)} collective-permute-done((f32[6,48,128]{2,1,0:T(8,128)S(1)}, f32[6,48,128]{2,1,0:T(8,128)S(1)}, u32[]{:S(2)}, u32[]{:S(2)}) %collective-permute-start.9) | collective-permute-done | bytes 147488 | tf_op jit(solution)/shard_map/ppermute | solution.py:334
  197.2 6.8 %collective-permute-start.11 = (f32[2,6,48,128]{3,2,1,0:T(8,128)S(1)}, f32[2,6,48,128]{3,2,1,0:T(8,128)S(1)}, u32[]{:S(2)}, u32[]{:S(2)}) collective-permute-start(f32[2,6,48,128]{3,2,1,0:T(8,128)S(1)} %pad_maximum_fusion.1), channel_id=1, source_target_pairs={{1,64},{2,65},{3,66},{4,67},{5,68},{6,69},{7,70},{8,71},{9,72},{10... | collective-permute-start | bytes 884744 | tf_op jit(solution)/shard_map/ppermute | solution.py:352
  204.0 1.9 collective-permute-start.10
  206.6 2.3 collective-permute-done.11
  209.0 8.8 %collective-permute-done.10 = f32[2,6,48,128]{3,2,1,0:T(8,128)S(1)} collective-permute-done((f32[2,6,48,128]{3,2,1,0:T(8,128)S(1)}, f32[2,6,48,128]{3,2,1,0:T(8,128)S(1)}, u32[]{:S(2)}, u32[]{:S(2)}) %collective-permute-start.10) | collective-permute-done | bytes 294944 | tf_op jit(solution)/shard_map/ppermute | solution.py:352
  221.1 1.9 collective-permute-start.4
  223.3 1.3 collective-permute-start.14
  224.6 4.9 %collective-permute-done.12 = f32[2,4,48,128]{3,2,1,0:T(8,128)S(1)} collective-permute-done((f32[2,4,48,128]{3,2,1,0:T(8,128)S(1)}, f32[2,4,48,128]{3,2,1,0:T(8,128)S(1)}, u32[]{:S(2)}, u32[]{:S(2)}) %collective-permute-start.12) | collective-permute-done | bytes 196640 | tf_op jit(solution)/shard_map/ppermute | solution.py:352
  229.5 2.2 collective-permute-done.14
  233.4 9.6 %collective-permute-done.4.arriving = f32[10,96,128]{2,1,0:T(8,128)S(1)} collective-permute-done((f32[10,96,128]{2,1,0:T(8,128)S(1)}, f32[10,96,128]{2,1,0:T(8,128)S(1)}, u32[]{:S(2)}, u32[]{:S(2)}) %collective-permute-start.4) | collective-permute-done | bytes 491552 | tf_op jit(solution)/shard_map/ppermute | solution.py:345
  243.0 108.4 %last.1 = f32[4,4,96,128]{3,2,1,0:T(8,128)} custom-call(s32[4]{0:T(128)S(1)} %pad_add_fusion.who, f32[4,4,96,128]{3,2,1,0:T(8,128)S(1)} %copy-done.1, f32[4,96,128]{2,1,0:T(8,128)S(1)} %copy-done.4, f32[4,96,128]{2,1,0:T(8,128)S(1)} %copy-done.7, f32[4,96,128]{2,1,0:T(8,128)S(1)} %copy-done.10, f32[4,96,128]{2,1,0:T(8,128)S(1)} %copy-done.13, ...), custom_call_target="tpu_custom_call" | custom-call | tf_op jit(solution)/shard_map/last/pallas_call | solution.py:277
  (118 shorter events, 24.2 us)
Async XLA Ops:
  0.1 1.1 copy-start
  1.2 0.9 copy-start.2
  2.1 0.9 copy-start.5
  3.1 0.9 copy-start.16
  5.6 27.3 %copy-start.1 = (f32[4,4,96,128]{3,2,1,0:T(8,128)S(1)}, f32[4,4,96,128]{3,2,1,0:T(8,128)}, u32[]{:S(2)}) copy-start(f32[4,4,96,128]{3,2,1,0:T(8,128)} %source.7) | copy-start | bytes 2359300
  9.2 23.7 %collective-permute-start = (f32[27,96,128]{2,1,0:T(8,128)}, f32[27,96,128]{2,1,0:T(8,128)S(1)}, u32[]{:S(2)}, u32[]{:S(2)}) collective-permute-start(f32[27,96,128]{2,1,0:T(8,128)} %get-tuple-element.16), channel_id=1, source_target_pairs={{1,2},{2,1},{3,4},{4,3},{5,6},{6,5},{7,8},{8,7},{9,10},{10,9},{11,... | collective-permute-start | bytes 3981320 | tf_op jit(solution)/shard_map/ppermute | solution.py:334
  17.3 15.7 %collective-permute-start.1 = (f32[27,96,128]{2,1,0:T(8,128)}, f32[27,96,128]{2,1,0:T(8,128)S(1)}, u32[]{:S(2)}, u32[]{:S(2)}) collective-permute-start(f32[27,96,128]{2,1,0:T(8,128)} %get-tuple-element.17), channel_id=1, source_target_pairs={{0,1},{1,0},{2,3},{3,2},{4,5},{5,4},{6,7},{7,6},{8,9},{9,8},{10,11... | collective-permute-start | bytes 3981320 | tf_op jit(solution)/shard_map/ppermute | solution.py:334
  32.9 0.9 copy-start.3
  144.6 17.8 %collective-permute-start.2 = (f32[17,96,128]{2,1,0:T(8,128)}, f32[17,96,128]{2,1,0:T(8,128)}, u32[]{:S(2)}, u32[]{:S(2)}) collective-permute-start(f32[17,96,128]{2,1,0:T(8,128)} %get-tuple-element.18.own), channel_id=1, source_target_pairs={{1,2},{2,1},{3,4},{4,3},{5,6},{6,5},{7,8},{8,7},{9,10},{10,9},{11,... | collective-permute-start | bytes 2506760 | tf_op jit(solution)/shard_map/ppermute | solution.py:334
  151.8 10.5 %collective-permute-start.3 = (f32[17,96,128]{2,1,0:T(8,128)}, f32[17,96,128]{2,1,0:T(8,128)}, u32[]{:S(2)}, u32[]{:S(2)}) collective-permute-start(f32[17,96,128]{2,1,0:T(8,128)} %get-tuple-element.19), channel_id=1, source_target_pairs={{0,1},{1,0},{2,3},{3,2},{4,5},{5,4},{6,7},{7,6},{8,9},{9,8},{10,11... | collective-permute-start | bytes 2506760 | tf_op jit(solution)/shard_map/ppermute | solution.py:334
  162.3 0.9 copy-start.4
  163.2 0.9 copy-start.7
  171.0 11.1 %collective-permute-start.5 = (f32[2,4,48,128]{3,2,1,0:T(8,128)S(1)}, f32[2,4,48,128]{3,2,1,0:T(8,128)S(1)}, u32[]{:S(2)}, u32[]{:S(2)}) collective-permute-start(f32[2,4,48,128]{3,2,1,0:T(8,128)S(1)} %get-tuple-element.21), channel_id=1, source_target_pairs={{0,32},{32,64},{64,96},{96,128},{128,160},{160,192},{192,224},{1,3... | collective-permute-start | bytes 589832 | tf_op jit(solution)/shard_map/ppermute | solution.py:345
  174.5 10.0 %collective-permute-start.6 = (f32[2,4,48,128]{3,2,1,0:T(8,128)S(1)}, f32[2,4,48,128]{3,2,1,0:T(8,128)S(1)}, u32[]{:S(2)}, u32[]{:S(2)}) collective-permute-start(f32[2,4,48,128]{3,2,1,0:T(8,128)S(1)} %get-tuple-element.21), channel_id=1, source_target_pairs={{0,64},{32,96},{64,128},{96,160},{128,192},{160,224},{1,65},{33,97... | collective-permute-start | bytes 589832 | tf_op jit(solution)/shard_map/ppermute | solution.py:345
  179.3 7.4 %collective-permute-start.7 = (f32[4,48,128]{2,1,0:T(8,128)S(1)}, f32[4,48,128]{2,1,0:T(8,128)S(1)}, u32[]{:S(2)}, u32[]{:S(2)}) collective-permute-start(f32[4,48,128]{2,1,0:T(8,128)S(1)} %get-tuple-element.46), channel_id=1, source_target_pairs={{0,96},{32,128},{64,160},{96,192},{128,224},{1,97},{33,129},{65,16... | collective-permute-start | bytes 294920 | tf_op jit(solution)/shard_map/ppermute | solution.py:345
  186.9 19.0 %copy-start.15 = (f32[6,48,128]{2,1,0:T(8,128)S(1)}, f32[6,48,128]{2,1,0:T(8,128)}, u32[]{:S(2)}) copy-start(f32[6,48,128]{2,1,0:T(8,128)} %copy-done.14) | copy-start | bytes 442372
  186.9 5.7 %collective-permute-start.8 = (f32[6,48,128]{2,1,0:T(8,128)S(1)}, f32[6,48,128]{2,1,0:T(8,128)S(1)}, u32[]{:S(2)}, u32[]{:S(2)}) collective-permute-start(f32[6,48,128]{2,1,0:T(8,128)S(1)} %get-tuple-element.43), channel_id=1, source_target_pairs={{0,1},{1,0},{2,3},{3,2},{4,5},{5,4},{6,7},{7,6},{8,9},{9,8},{10,11... | collective-permute-start | bytes 442376 | tf_op jit(solution)/shard_map/ppermute | solution.py:334
  187.0 10.1 %collective-permute-start.9 = (f32[6,48,128]{2,1,0:T(8,128)S(1)}, f32[6,48,128]{2,1,0:T(8,128)S(1)}, u32[]{:S(2)}, u32[]{:S(2)}) collective-permute-start(f32[6,48,128]{2,1,0:T(8,128)S(1)} %get-tuple-element.44), channel_id=1, source_target_pairs={{1,2},{2,1},{3,4},{4,3},{5,6},{6,5},{7,8},{8,7},{9,10},{10,9},{11,... | collective-permute-start | bytes 442376 | tf_op jit(solution)/shard_map/ppermute | solution.py:334
  197.2 11.7 %collective-permute-start.11 = (f32[2,6,48,128]{3,2,1,0:T(8,128)S(1)}, f32[2,6,48,128]{3,2,1,0:T(8,128)S(1)}, u32[]{:S(2)}, u32[]{:S(2)}) collective-permute-start(f32[2,6,48,128]{3,2,1,0:T(8,128)S(1)} %pad_maximum_fusion.1), channel_id=1, source_target_pairs={{1,64},{2,65},{3,66},{4,67},{5,68},{6,69},{7,70},{8,71},{9,72},{10... | collective-permute-start | bytes 884744 | tf_op jit(solution)/shard_map/ppermute | solution.py:352
  204.0 13.8 %collective-permute-start.10 = (f32[2,6,48,128]{3,2,1,0:T(8,128)S(1)}, f32[2,6,48,128]{3,2,1,0:T(8,128)S(1)}, u32[]{:S(2)}, u32[]{:S(2)}) collective-permute-start(f32[2,6,48,128]{3,2,1,0:T(8,128)S(1)} %pad_maximum_fusion.1), channel_id=1, source_target_pairs={{0,65},{1,66},{2,67},{3,68},{4,69},{5,70},{6,71},{7,72},{8,73},{9,... | collective-permute-start | bytes 884744 | tf_op jit(solution)/shard_map/ppermute | solution.py:352
  218.5 10.9 %collective-permute-start.12 = (f32[2,4,48,128]{3,2,1,0:T(8,128)S(1)}, f32[2,4,48,128]{3,2,1,0:T(8,128)S(1)}, u32[]{:S(2)}, u32[]{:S(2)}) collective-permute-start(f32[2,4,48,128]{3,2,1,0:T(8,128)S(1)} %get-tuple-element.40), channel_id=1, source_target_pairs={{0,130},{1,131},{2,132},{3,133},{4,134},{5,135},{6,136},{7,137},{8... | collective-permute-start | bytes 589832 | tf_op jit(solution)/shard_map/ppermute | solution.py:352
  219.8 9.6 %collective-permute-start.13 = (f32[2,6,48,128]{3,2,1,0:T(8,128)S(1)}, f32[2,6,48,128]{3,2,1,0:T(8,128)S(1)}, u32[]{:S(2)}, u32[]{:S(2)}) collective-permute-start(f32[2,6,48,128]{3,2,1,0:T(8,128)S(1)} %fusion.53), channel_id=1, source_target_pairs={{0,128},{32,160},{64,192},{96,224},{1,129},{33,161},{65,193},{97,2... | collective-permute-start | bytes 884744 | tf_op jit(solution)/shard_map/ppermute | solution.py:345
  221.1 21.8 %collective-permute-start.4 = (f32[10,96,128]{2,1,0:T(8,128)S(1)}, f32[10,96,128]{2,1,0:T(8,128)S(1)}, u32[]{:S(2)}, u32[]{:S(2)}) collective-permute-start(f32[10,96,128]{2,1,0:T(8,128)S(1)} %get-tuple-element.20), channel_id=1, source_target_pairs={{0,32},{32,64},{64,96},{96,128},{128,160},{160,192},{192,224},{1,3... | collective-permute-start | bytes 1474568 | tf_op jit(solution)/shard_map/ppermute | solution.py:345
  223.3 8.5 %collective-permute-start.14 = (f32[2,4,48,128]{3,2,1,0:T(8,128)S(1)}, f32[2,4,48,128]{3,2,1,0:T(8,128)S(1)}, u32[]{:S(2)}, u32[]{:S(2)}) collective-permute-start(f32[2,4,48,128]{3,2,1,0:T(8,128)S(1)} %get-tuple-element.39), channel_id=1, source_target_pairs={{2,128},{3,129},{4,130},{5,131},{6,132},{7,133},{8,134},{9,135},{1... | collective-permute-start | bytes 589832 | tf_op jit(solution)/shard_map/ppermute | solution.py:352
  (10 other events, 8.2 us)

commit v3 on v2

--- a/solution.py
+++ b/solution.py
@@ -1,5 +1,3 @@
-import functools
-
 import jax
 import jax.numpy as jnp
 from jax import lax
@@ -19,6 +17,7 @@
 SMEM = pl.BlockSpec(memory_space=pltpu.SMEM)
 
 P_INIT, P_MOB, P_FREE, P_KAP, PARCEL = 12, 16, 20, 24, 27
+O_INIT, O_MOB, O_FREE, O_KAP, OWN = 16, 20, 24, 28, 32
 
 
 def shifted(values, by, axis):
@@ -26,7 +25,7 @@
     return pltpu.roll(values, by % size, axis)
 
 
-def parcel_kernel(who, rates, source, initial, mobility, labels, electrode, far, near, kappa, free):
+def parcel_kernel(who, rates, source, initial, mobility, labels, electrode, far, near, own):
     odd = who[0]
 
     @pl.loop(0, SLAB)
@@ -35,9 +34,13 @@
         value = jnp.zeros(kind.shape, jnp.float32)
         for n in range(rates.shape[0]):
             value = jnp.where(kind == n, rates[n], value)
-        kappa[p] = value
+        own[O_KAP + p] = value
         open_cell = 1.0 - electrode[p].astype(jnp.float32)
-        free[p] = open_cell
+        own[O_FREE + p] = open_cell
+        own[O_INIT + p] = initial[p]
+        own[O_MOB + p] = mobility[p]
+        for t in range(STEPS):
+            own[SLAB * t + p] = 0.5 * source[t, p]
         for out in (far, near):
             out[P_INIT + p] = initial[p]
             out[P_MOB + p] = mobility[p]
@@ -47,22 +50,22 @@
 
         @pl.loop(0, SLAB - 1)
         def _(j):
-            out[P_KAP + j] = kappa[begin + j]
+            out[P_KAP + j] = own[O_KAP + begin + j]
             for t in range(STEPS):
-                out[3 * t + j] = 0.5 * source[t, begin + j]
-
-
-def load_static(odd, source, initial, mobility, kappa, free, far, near, force, begin, mob, kap, open_cell):
-    rows = pl.ds(EDGE, mobility.shape[1])
+                out[3 * t + j] = own[SLAB * t + begin + j]
+
+
+def load_static(odd, fixed, far, near, force, begin, mob, kap, open_cell):
+    rows = pl.ds(EDGE, fixed.shape[1])
 
     @pl.loop(0, SLAB)
     def _(p):
-        begin[4 + p] = initial[p]
-        mob[4 + p, rows] = mobility[p]
-        open_cell[4 + p] = free[p]
-        kap[3 + p] = kappa[p]
+        begin[4 + p] = fixed[O_INIT + p]
+        mob[4 + p, rows] = fixed[O_MOB + p]
+        open_cell[4 + p] = fixed[O_FREE + p]
+        kap[3 + p] = fixed[O_KAP + p]
         for t in range(STEPS):
-            force[t, 3 + p] = 0.5 * source[t, p]
+            force[t, 3 + p] = fixed[SLAB * t + p]
         for block, wide in ((far, 8 * odd), (near, 8 - 8 * odd)):
             begin[wide + p] = block[P_INIT + p]
             mob[wide + p, rows] = block[P_MOB + p]
@@ -111,32 +114,29 @@
 
 def clear_edges(cells):
     zero = jnp.zeros((EDGE, cells.shape[-1]), jnp.float32)
-    for b in range(cells.shape[0]):
+
+    @pl.loop(0, cells.shape[1])
+    def _(p):
         for t in range(STEPS):
-
-            @pl.loop(0, cells.shape[2])
-            def _(p):
-                cells[b, t, p, pl.ds(0, EDGE)] = zero
-                cells[b, t, p, pl.ds(cells.shape[3] - EDGE, EDGE)] = zero
-
-
-def gathered(w, cells, b, t, p, r):
-    here = cells[b, t, p, pl.ds(EDGE + r, 8)]
-    total = w[0] * cells[b, t, p - 1, pl.ds(EDGE + r, 8)]
-    total += w[1] * cells[b, t, p + 1, pl.ds(EDGE + r, 8)]
-    total += w[2] * cells[b, t, p, pl.ds(EDGE + r - 1, 8)]
-    total += w[3] * cells[b, t, p, pl.ds(EDGE + r + 1, 8)]
+            cells[t, p, pl.ds(0, EDGE)] = zero
+            cells[t, p, pl.ds(cells.shape[2] - EDGE, EDGE)] = zero
+
+
+def gathered(w, cells, t, p, r):
+    here = cells[t, p, pl.ds(EDGE + r, 8)]
+    total = w[0] * cells[t, p - 1, pl.ds(EDGE + r, 8)]
+    total += w[1] * cells[t, p + 1, pl.ds(EDGE + r, 8)]
+    total += w[2] * cells[t, p, pl.ds(EDGE + r - 1, 8)]
+    total += w[3] * cells[t, p, pl.ds(EDGE + r + 1, 8)]
     total += w[4] * shifted(here, 1, 1)
     total += w[5] * shifted(here, -1, 1)
     return here, total
 
 
-def run_sweep(cells, weights, kap, open_cell, force, opening):
-    height = cells.shape[3] - 2 * EDGE
-
-    @pl.loop(0, PASSES)
-    def _(number):
-        b = number % 2
+def run_sweep(cells, other, weights, kap, open_cell, force, opening):
+    height = cells.shape[2] - 2 * EDGE
+    for number in range(PASSES):
+        source, target = (cells, other) if number % 2 == 0 else (other, cells)
 
         @pl.loop(number, 10 - number)
         def _(j):
@@ -147,10 +147,10 @@
                 gain = DAMPING * open_cell[j + 1, rows]
                 former = opening[j, rows]
                 for t in range(STEPS):
-                    here, total = gathered(w, cells, b, t, j + 1, r)
+                    here, total = gathered(w, source, t, j + 1, r)
                     pull = rate * jnp.abs(here)
                     residue = force[t, j, rows] + former + total - here * (w[6] + 0.5 * pull)
-                    cells[1 - b, t, j + 1, pl.ds(EDGE + r, 8)] = here + gain * residue / (w[6] + pull)
+                    target[t, j + 1, pl.ds(EDGE + r, 8)] = here + gain * residue / (w[6] + pull)
                     former = here
 
 
@@ -158,11 +158,11 @@
     return 0.25 * ((read(0, 0) + read(0, 1)) + (read(1, 0) + read(1, 1)))
 
 
-def first_kernel(who, source, initial, mobility, kappa, free, far, near, to_far, to_near, rough_out,
-                 force, begin, mob, kap, open_cell, weights, cells):
+def first_kernel(who, fixed, far, near, to_far, to_near, rough_out, closing,
+                 force, begin, mob, kap, open_cell, weights, cells, other):
     odd = who[0]
-    height = mobility.shape[1]
-    load_static(odd, source, initial, mobility, kappa, free, far, near, force, begin, mob, kap, open_cell)
+    height = fixed.shape[1]
+    load_static(odd, fixed, far, near, force, begin, mob, kap, open_cell)
     make_weights(mob, weights, 0, 10)
     clear_edges(cells)
 
@@ -170,26 +170,29 @@
     def _(p):
         value = begin[p]
         for t in range(STEPS):
-            cells[0, t, p, pl.ds(EDGE, height)] = value
-
-    run_sweep(cells, weights, kap, open_cell, force, begin.at[pl.ds(1, 10)])
+            cells[t, p, pl.ds(EDGE, height)] = value
+
+    clear_edges(other)
+    run_sweep(cells, other, weights, kap, open_cell, force, begin.at[pl.ds(1, 10)])
+    for p in range(SLAB):
+        closing[p] = cells[STEPS - 1, 4 + p, pl.ds(EDGE, height)]
     half = height // 2
     for a in range(6):
         rough_out[a] = halved(lambda x, y: mob[2 * a + x, pl.ds(EDGE + y, half, stride=2)])
     for out, base in ((to_far, 4 - 4 * odd), (to_near, 4 * odd)):
         for t in range(STEPS):
             for p in range(SLAB):
-                out[4 * t + p] = cells[0, t, 4 + p, pl.ds(EDGE, height)]
+                out[4 * t + p] = cells[t, 4 + p, pl.ds(EDGE, height)]
         out[16, pl.ds(0, half)] = rough_out[base]
         out[16, pl.ds(half, half)] = rough_out[base + 1]
 
 
-def residual_kernel(who, source, initial, mobility, kappa, free, far, near, own, low_far, low_near,
-                    both, closing, force, begin, mob, kap, open_cell, weights, cells, residues):
+def residual_kernel(who, fixed, far, near, own, low_far, low_near,
+                    both, force, begin, mob, kap, open_cell, weights, cells, residues):
     odd, leading, place, count = who[0], who[1], who[2], who[3]
-    height = mobility.shape[1]
+    height = fixed.shape[1]
     half = height // 2
-    load_static(odd, source, initial, mobility, kappa, free, far, near, force, begin, mob, kap, open_cell)
+    load_static(odd, fixed, far, near, force, begin, mob, kap, open_cell)
     make_weights(mob, weights, 1, 9)
     clear_edges(cells)
     rows = pl.ds(EDGE, height)
@@ -197,9 +200,9 @@
 
         @pl.loop(0, SLAB)
         def _(p):
-            cells[0, t, 4 + p, rows] = own[4 * t + p]
-            cells[0, t, 8 * odd + p, rows] = low_far[4 * t + p]
-            cells[0, t, 8 - 8 * odd + p, rows] = low_near[4 * t + p]
+            cells[t, 4 + p, rows] = own[4 * t + p]
+            cells[t, 8 * odd + p, rows] = low_far[4 * t + p]
+            cells[t, 8 - 8 * odd + p, rows] = low_near[4 * t + p]
 
     @pl.loop(1, 9)
     def _(j):
@@ -210,7 +213,7 @@
             former = jnp.where(leading == 1, begin[j + 1, rows], 0.0)
             acc = jnp.zeros_like(former)
             for t in range(STEPS):
-                here, total = gathered(w, cells, 0, t, j + 1, r)
+                here, total = gathered(w, cells, t, j + 1, r)
                 pull = rate * jnp.abs(here)
                 acc += force[t, j, rows] + former + total - here * (w[6] + 0.5 * pull)
                 former = here
@@ -221,19 +224,15 @@
         inside = jnp.logical_and(coarse >= 0, coarse < 2 * count)
         value = halved(lambda x, y: residues[2 * a + x, pl.ds(y, half, stride=2)])
         both[0, a] = jnp.where(inside, value, 0.0)
-        both[1, a] = halved(lambda x, y: cells[0, STEPS - 1, 2 + 2 * a + x, pl.ds(EDGE + y, half, stride=2)])
-
-    @pl.loop(0, 10)
-    def _(j):
-        closing[j] = cells[0, STEPS - 1, j + 1, pl.ds(EDGE, height)]
-
-
-def last_kernel(who, source, initial, mobility, kappa, free, far, near, own, low_far, low_near, arriving, correction,
-                out, force, begin, mob, kap, open_cell, weights, cells, opening):
+        both[1, a] = halved(lambda x, y: cells[STEPS - 1, 2 + 2 * a + x, pl.ds(EDGE + y, half, stride=2)])
+
+
+def last_kernel(who, fixed, far, near, own, low_far, low_near, arriving, side_far, side_near, correction,
+                out, force, begin, mob, kap, open_cell, weights, cells, other, opening):
     odd, leading = who[0], who[1]
-    height = mobility.shape[1]
+    height = fixed.shape[1]
     half = height // 2
-    load_static(odd, source, initial, mobility, kappa, free, far, near, force, begin, mob, kap, open_cell)
+    load_static(odd, fixed, far, near, force, begin, mob, kap, open_cell)
     make_weights(mob, weights, 0, 10)
     clear_edges(cells)
     for y in range(2):
@@ -246,17 +245,26 @@
                 plane = at + p
                 change = open_cell[plane, rows] * correction[0, plane // 2]
                 for t in range(STEPS):
-                    cells[0, t, plane, into] = block[4 * t + p, rows] + change
-
-        @pl.loop(0, 10)
-        def _(j):
-            base = jnp.where(leading == 1, begin[j + 1, rows], arriving[j, rows])
+                    cells[t, plane, into] = block[4 * t + p, rows] + change
+
+        def enter(j, value):
+            base = jnp.where(leading == 1, begin[j + 1, rows], value)
             opening[j, rows] = base + open_cell[j + 1, rows] * correction[1, (j + 1) // 2]
 
-    run_sweep(cells, weights, kap, open_cell, force, opening)
+        @pl.loop(0, SLAB)
+        def _(p):
+            enter(3 + p, arriving[p, rows])
+
+        @pl.loop(0, SLAB - 1)
+        def _(p):
+            enter(7 * odd + p, side_far[3 + p, rows])
+            enter(7 - 7 * odd + p, side_near[3 + p, rows])
+
+    clear_edges(other)
+    run_sweep(cells, other, weights, kap, open_cell, force, opening)
     for t in range(STEPS):
         for p in range(SLAB):
-            out[t, p] = cells[0, t, 4 + p, pl.ds(EDGE, height)]
+            out[t, p] = cells[t, 4 + p, pl.ds(EDGE, height)]
 
 
 def windows(height, depth):
@@ -273,7 +281,7 @@
     ]
 
 
-def call(kernel, name, inputs, outputs, scratch, scalars=1):
+def call(kernel, name, inputs, outputs, scratch, scalars=1, grant=28):
     return pl.pallas_call(
         kernel,
         out_shape=[jax.ShapeDtypeStruct(o, jnp.float32) for o in outputs],
@@ -281,7 +289,7 @@
         out_specs=[VMEM] * len(outputs),
         scratch_shapes=scratch,
         name=name,
-        compiler_params=pltpu.CompilerParams(vmem_limit_bytes=28 << 20),
+        compiler_params=pltpu.CompilerParams(vmem_limit_bytes=grant << 20),
     )(*inputs)
 
 
@@ -327,11 +335,22 @@
         return values
 
 
-def traded(far, near):
+def traded(far, near, steps=0):
+    times = lax.axis_size("tm")
     count = lax.axis_size("space")
-    far_pairs = [(i, i + 1 if i % 2 else i - 1) for i in range(1, count - 1)]
-    near_pairs = [(i, i ^ 1) for i in range(count)]
-    return lax.ppermute(far, "space", far_pairs), lax.ppermute(near, "space", near_pairs)
+    far_of = [i + 1 if i % 2 else i - 1 for i in range(count)]
+    near_of = [i ^ 1 for i in range(count)]
+
+    def send(value, to):
+        pairs = [
+            (k * count + i, (k + steps) * count + to[i])
+            for k in range(times - steps)
+            for i in range(count)
+            if 0 <= to[i] < count
+        ]
+        return lax.ppermute(value, ("tm", "space"), pairs)
+
+    return send(far, far_of), send(near, near_of)
 
 
 def by_side(odd, far, near):
@@ -364,36 +383,38 @@
         & (2 * place + jnp.arange(-reach, 2 + reach) < 2 * lax.axis_size("space"))
     ).astype(jnp.float32)
 
-    far, near, kappa, free = call(
+    far, near, fixed = call(
         parcel_kernel,
         "parcel",
         (who, rates, source, initial, mobility, labels, electrode),
-        [(PARCEL,) + plane] * 2 + [initial.shape] * 2,
+        [(PARCEL,) + plane] * 2 + [(OWN,) + plane],
         [],
         2,
+        60,
     )
     far, near = traded(far, near)
-    static = (who, source, initial, mobility, kappa, free, far, near)
+    static = (who, fixed, far, near)
     tall = (height + 2 * EDGE, depth)
 
     coarse = (height // 2, depth)
-    to_far, to_near, rough = call(
+    to_far, to_near, rough, closing = call(
         first_kernel,
         "first",
         static,
-        [(17,) + plane] * 2 + [(6,) + coarse],
-        windows(height, depth) + [pltpu.VMEM((2, STEPS, 12) + tall, jnp.float32)],
+        [(17,) + plane] * 2 + [(6,) + coarse, initial.shape],
+        windows(height, depth) + [pltpu.VMEM((STEPS, 12) + tall, jnp.float32)] * 2,
     )
     got_far, got_near = traded(to_far, to_near)
+    opening = arrived(closing, 1)
     states = (to_far, got_far, got_near)
 
-    both, closing = call(
+    (both,) = call(
         residual_kernel,
         "residual",
         static + states,
-        [(2, 4) + coarse, (10,) + plane],
+        [(2, 4) + coarse],
         windows(height, depth)
-        + [pltpu.VMEM((1, STEPS, 12) + tall, jnp.float32), pltpu.VMEM((8,) + plane, jnp.float32)],
+        + [pltpu.VMEM((STEPS, 12) + tall, jnp.float32), pltpu.VMEM((8,) + plane, jnp.float32)],
     )
     rough_of = lambda b: b[16].reshape((2,) + coarse)
     low, high = by_side(odd == 1, rough_of(got_far), rough_of(got_near))
@@ -408,14 +429,17 @@
     pair = jnp.stack([inner(rhs, 0, 1), inner(rhs1, 0, 1)])
     pair = pair + Coupling(inner(rough_w, 0, 3), inside(1)).step(jnp.stack([rhs1, rhs2]))
 
-    cargo = lambda c: jnp.concatenate([pair.reshape((4,) + coarse), c], axis=0)
-    to_low, to_high = cargo(rough_w[8:10]), cargo(rough_w[0:2])
-    low, high = by_side(odd == 1, *traded(*by_side(odd == 1, to_low, to_high)))
-    opening = arrived(closing, 1)
+    flat = lambda v: v.reshape((-1,) + plane)
+    unflat = lambda v: v.reshape((-1,) + coarse)
+    cargo = lambda c, o: jnp.concatenate([flat(pair), flat(c), o], axis=0)
+    to_low = cargo(rough_w[8:10], opening[: SLAB - 1])
+    to_high = cargo(rough_w[0:2], opening[1:])
+    side_far, side_near = traded(*by_side(odd == 1, to_low, to_high))
+    low, high = by_side(odd == 1, unflat(side_far[:3]), unflat(side_near[:3]))
     pair_of = lambda b: b[:4].reshape(pair.shape)
     rough_far = jnp.concatenate([low[4:], rough_w, high[4:]], axis=0)
     pair = jnp.concatenate([pair_of(low), pair, pair_of(high)], axis=1)
-    low, high = arrived(pair, 2, -1), arrived(pair, 2, 1)
+    low, high = by_side(odd == 1, *traded(pair, pair, 2))
     middle = jnp.where(place == 0, high[:, :2], low[:, 4:])
     older = jnp.concatenate([low[:, :4], middle, high[:, 2:]], axis=1)
     coupling = Coupling(rough_far, inside(6))
@@ -426,10 +450,11 @@
     (density,) = call(
         last_kernel,
         "last",
-        static + states + (opening, correction),
+        static + states + (opening, side_far, side_near, correction),
         [source.shape],
         windows(height, depth)
-        + [pltpu.VMEM((2, STEPS, 12) + tall, jnp.float32), pltpu.VMEM((10,) + plane, jnp.float32)],
+        + [pltpu.VMEM((STEPS, 12) + tall, jnp.float32)] * 2
+        + [pltpu.VMEM((10,) + plane, jnp.float32)],
     )
     return density
 

time: 352 us -> 146 us (0.41)
  Pallas kernels: 223 us -> 29.2 us
  local copies, waits for them, and re-layouts: 16.4 us -> 7.37 us
  waiting for transfers between devices: 60.8 us -> 54.9 us
    pallas_call x4, Pallas kernels: 223 us -> 29.2 us  [call(): pl.pallas_call(kernel, out_shape=[jax.ShapeDtypeStruct(o, jnp.float32) fo...]
    ppermute x4 -> x2, waiting for transfers between devices: 18.2 us -> 8.25 us  [arrived(): return lax.ppermute(value, ('tm', 'space'), pairs)]
    ppermute x4 -> x2, starting transfers between devices: 11.3 us -> 2.58 us  [arrived(): return lax.ppermute(value, ('tm', 'space'), pairs)]
    unnamed x44 -> x32, local copies, waits for them, and re-layouts: 15 us -> 6.71 us
    ppermute x6 -> x8, starting transfers between devices: 21.1 us -> 29 us  [send(): return lax.ppermute(value, ('tm', 'space'), pairs)]
    ppermute x6 -> x8, waiting for transfers between devices: 28.4 us -> 30 us  [send(): return lax.ppermute(value, ('tm', 'space'), pairs)]
  transfers between devices with their start and end apart: 15 -> 15, of which waited for: 10 -> 9; matrix products, arithmetic and copies ran while one was open for 2% -> 1% of each run, Pallas kernels for 0% -> 0%
where the time goes in v3:
time: 146 us; the launch traced here: 145 us
  waiting for transfers between devices  54.9 us (38%)
  starting transfers between devices  45.5 us (31%)
  Pallas kernels  29.2 us (20%)
  local copies, waits for them, and re-layouts  7.37 us (5%)
  other arithmetic  7.31 us (5%)
    ppermute x8, waiting for transfers between devices, send(): return lax.ppermute(value, ('tm', 'space'), pairs)  30 us
    pallas_call x4, Pallas kernels, call(): pl.pallas_call(kernel, out_shape=[jax.ShapeDtypeStruct(o, jnp.float32) fo...  29.2 us
    ppermute x8, starting transfers between devices, send(): return lax.ppermute(value, ('tm', 'space'), pairs)  29 us
    ppermute x5, waiting for transfers between devices, arrived(): lax.ppermute(value, 'tm', [(k, k + steps) for k in range(times - steps)])  16.6 us
    ppermute x5, starting transfers between devices, arrived(): lax.ppermute(value, 'tm', [(k, k + steps) for k in range(times - steps)])  13.9 us
    ppermute x2, waiting for transfers between devices, arrived(): return lax.ppermute(value, ('tm', 'space'), pairs)  8.25 us
    unnamed x32, local copies, waits for them, and re-layouts  6.71 us
  transfers between devices with their start and end apart: 15, of which 9 were waited for; matrix products, arithmetic and copies ran while one was open for 1% of the time, Pallas kernels for 0%

profile of v3, /device:TPU:6, one launch (start us, length us, event | category | flops | bytes accessed | tf_op | source)
XLA Modules:
  0.0 145.0 jit_solution(16669663424293901891)
XLA Ops:
  0.6 3.8 %parcel.1 = (f32[27,96,128]{2,1,0:T(8,128)}, f32[27,96,128]{2,1,0:T(8,128)}, f32[32,96,128]{2,1,0:T(8,128)}) custom-call(s32[4]{0:T(128)} %pad_add_fusion.who, f32[4]{0:T(128)} %rates.1, f32[4,4,96,128]{3,2,1,0:T(8,128)} %source.1, f32[4,96,128]{2,1,0:T(8,128)} %initial.1, f32[4,96,128]{2,1,0:T(8,128)} %mobility.1, s32[4,96,128]{2,1,0:T(8,128)} %labels.1, ...), custom_call_target="tpu_custom_call" | custom-call | tf_op jit(solution)/shard_map/parcel/pallas_call | solution.py:285
  4.3 8.0 %collective-permute-start = (f32[27,96,128]{2,1,0:T(8,128)}, f32[27,96,128]{2,1,0:T(8,128)S(1)}, u32[]{:S(2)}, u32[]{:S(2)}) collective-permute-start(f32[27,96,128]{2,1,0:T(8,128)} %get-tuple-element.13), channel_id=1, source_target_pairs={{1,2},{2,1},{3,4},{4,3},{5,6},{6,5},{7,8},{8,7},{9,10},{10,9},{11,... | collective-permute-start | bytes 3981320 | tf_op jit(solution)/shard_map/ppermute | solution.py:351
  12.5 15.5 %collective-permute-done.far = f32[27,96,128]{2,1,0:T(8,128)S(1)} collective-permute-done((f32[27,96,128]{2,1,0:T(8,128)}, f32[27,96,128]{2,1,0:T(8,128)S(1)}, u32[]{:S(2)}, u32[]{:S(2)}) %collective-permute-start) | collective-permute-done | bytes 1327136 | tf_op jit(solution)/shard_map/ppermute | solution.py:351
  29.1 1.4 copy-done
  30.5 1.3 copy-done.3
  31.8 9.8 %first.1 = (f32[17,96,128]{2,1,0:T(8,128)}, f32[17,96,128]{2,1,0:T(8,128)}, f32[6,48,128]{2,1,0:T(8,128)S(1)}, f32[4,96,128]{2,1,0:T(8,128)S(1)}) custom-call(s32[4]{0:T(128)S(1)} %copy-done.6, f32[32,96,128]{2,1,0:T(8,128)S(1)} %copy-done, f32[27,96,128]{2,1,0:T(8,128)S(1)} %collective-permute-done.far, f32[27,96,128]{2,1,0:T(8,128)S(1)} %copy-done.3), custom_call_target="tpu_custom_call" | custom-call | tf_op jit(solution)/shard_map/first/pallas_call | solution.py:285
  41.6 7.2 %collective-permute-start.2 = (f32[17,96,128]{2,1,0:T(8,128)}, f32[17,96,128]{2,1,0:T(8,128)}, u32[]{:S(2)}, u32[]{:S(2)}) collective-permute-start(f32[17,96,128]{2,1,0:T(8,128)} %get-tuple-element.15.own), channel_id=1, source_target_pairs={{1,2},{2,1},{3,4},{4,3},{5,6},{6,5},{7,8},{8,7},{9,10},{10,9},{11,... | collective-permute-start | bytes 2506760 | tf_op jit(solution)/shard_map/ppermute | solution.py:351
  49.1 3.5 %collective-permute-start.4 = (f32[4,96,128]{2,1,0:T(8,128)S(1)}, f32[4,96,128]{2,1,0:T(8,128)S(1)}, u32[]{:S(2)}, u32[]{:S(2)}) collective-permute-start(f32[4,96,128]{2,1,0:T(8,128)S(1)} %get-tuple-element.17), channel_id=1, source_target_pairs={{0,32},{32,64},{64,96},{96,128},{128,160},{160,192},{192,224},{1,3... | collective-permute-start | bytes 589832 | tf_op jit(solution)/shard_map/ppermute | solution.py:364
  52.7 7.7 %collective-permute-done.4.arriving = f32[4,96,128]{2,1,0:T(8,128)S(1)} collective-permute-done((f32[4,96,128]{2,1,0:T(8,128)S(1)}, f32[4,96,128]{2,1,0:T(8,128)S(1)}, u32[]{:S(2)}, u32[]{:S(2)}) %collective-permute-start.4) | collective-permute-done | bytes 196640 | tf_op jit(solution)/shard_map/ppermute | solution.py:364
  61.8 4.8 %residual.1 = f32[2,4,48,128]{3,2,1,0:T(8,128)S(1)} custom-call(s32[4]{0:T(128)S(1)} %copy-done.6, f32[32,96,128]{2,1,0:T(8,128)S(1)} %copy-done.1, f32[27,96,128]{2,1,0:T(8,128)S(1)} %collective-permute-done.far, f32[27,96,128]{2,1,0:T(8,128)S(1)} %copy-done.4, f32[17,96,128]{2,1,0:T(8,128)} %get-tuple-element.15.own, ...), custom_call_target="tpu_custom_call" | custom-call | tf_op jit(solution)/shard_map/residual/pallas_call | solution.py:285
  66.6 2.4 %collective-permute-start.5 = (f32[2,4,48,128]{3,2,1,0:T(8,128)S(1)}, f32[2,4,48,128]{3,2,1,0:T(8,128)S(1)}, u32[]{:S(2)}, u32[]{:S(2)}) collective-permute-start(f32[2,4,48,128]{3,2,1,0:T(8,128)S(1)} %residual.1), channel_id=1, source_target_pairs={{0,32},{32,64},{64,96},{96,128},{128,160},{160,192},{192,224},{1,3... | collective-permute-start | bytes 589832 | tf_op jit(solution)/shard_map/ppermute | solution.py:364
  68.9 4.8 %collective-permute-start.6 = (f32[2,4,48,128]{3,2,1,0:T(8,128)S(1)}, f32[2,4,48,128]{3,2,1,0:T(8,128)S(1)}, u32[]{:S(2)}, u32[]{:S(2)}) collective-permute-start(f32[2,4,48,128]{3,2,1,0:T(8,128)S(1)} %residual.1), channel_id=1, source_target_pairs={{0,64},{32,96},{64,128},{96,160},{128,192},{160,224},{1,65},{33,97... | collective-permute-start | bytes 589832 | tf_op jit(solution)/shard_map/ppermute | solution.py:364
  73.8 1.9 %collective-permute-start.7 = (f32[4,48,128]{2,1,0:T(8,128)S(1)}, f32[4,48,128]{2,1,0:T(8,128)S(1)}, u32[]{:S(2)}, u32[]{:S(2)}) collective-permute-start(f32[4,48,128]{2,1,0:T(8,128)S(1)} %get-tuple-element.46), channel_id=1, source_target_pairs={{0,96},{32,128},{64,160},{96,192},{128,224},{1,97},{33,129},{65,16... | collective-permute-start | bytes 294920 | tf_op jit(solution)/shard_map/ppermute | solution.py:364
  76.6 2.9 %collective-permute-done.5 = f32[2,4,48,128]{3,2,1,0:T(8,128)S(1)} collective-permute-done((f32[2,4,48,128]{3,2,1,0:T(8,128)S(1)}, f32[2,4,48,128]{3,2,1,0:T(8,128)S(1)}, u32[]{:S(2)}, u32[]{:S(2)}) %collective-permute-start.5) | collective-permute-done | bytes 196640 | tf_op jit(solution)/shard_map/ppermute | solution.py:364
  79.5 1.7 %collective-permute-done.6 = f32[2,4,48,128]{3,2,1,0:T(8,128)S(1)} collective-permute-done((f32[2,4,48,128]{3,2,1,0:T(8,128)S(1)}, f32[2,4,48,128]{3,2,1,0:T(8,128)S(1)}, u32[]{:S(2)}, u32[]{:S(2)}) %collective-permute-start.6) | collective-permute-done | bytes 196640 | tf_op jit(solution)/shard_map/ppermute | solution.py:364
  82.3 5.5 %collective-permute-start.8 = (f32[6,96,128]{2,1,0:T(8,128)}, f32[6,96,128]{2,1,0:T(8,128)S(1)}, u32[]{:S(2)}, u32[]{:S(2)}) collective-permute-start(f32[6,96,128]{2,1,0:T(8,128)} %get-tuple-element.40), channel_id=1, source_target_pairs={{1,2},{2,1},{3,4},{4,3},{5,6},{6,5},{7,8},{8,7},{9,10},{10,9},{11,... | collective-permute-start | bytes 884744 | tf_op jit(solution)/shard_map/ppermute | solution.py:351
  88.1 6.1 %collective-permute-done.8.side_far = f32[6,96,128]{2,1,0:T(8,128)S(1)} collective-permute-done((f32[6,96,128]{2,1,0:T(8,128)}, f32[6,96,128]{2,1,0:T(8,128)S(1)}, u32[]{:S(2)}, u32[]{:S(2)}) %collective-permute-start.8) | collective-permute-done | bytes 294944 | tf_op jit(solution)/shard_map/ppermute | solution.py:351
  96.1 1.9 %collective-permute-start.10 = (f32[2,6,48,128]{3,2,1,0:T(8,128)S(1)}, f32[2,6,48,128]{3,2,1,0:T(8,128)S(1)}, u32[]{:S(2)}, u32[]{:S(2)}) collective-permute-start(f32[2,6,48,128]{3,2,1,0:T(8,128)S(1)} %pad_maximum_fusion.3), channel_id=1, source_target_pairs={{0,65},{1,64},{2,67},{3,66},{4,69},{5,68},{6,71},{7,70},{8,73},{9,... | collective-permute-start | bytes 884744 | tf_op jit(solution)/shard_map/ppermute | solution.py:351
  98.1 6.1 %collective-permute-start.11 = (f32[2,6,48,128]{3,2,1,0:T(8,128)S(1)}, f32[2,6,48,128]{3,2,1,0:T(8,128)S(1)}, u32[]{:S(2)}, u32[]{:S(2)}) collective-permute-start(f32[2,6,48,128]{3,2,1,0:T(8,128)S(1)} %pad_maximum_fusion.3), channel_id=1, source_target_pairs={{1,66},{2,65},{3,68},{4,67},{5,70},{6,69},{7,72},{8,71},{9,74},{10... | collective-permute-start | bytes 884744 | tf_op jit(solution)/shard_map/ppermute | solution.py:351
  104.9 3.2 %collective-permute-done.10 = f32[2,6,48,128]{3,2,1,0:T(8,128)S(1)} collective-permute-done((f32[2,6,48,128]{3,2,1,0:T(8,128)S(1)}, f32[2,6,48,128]{3,2,1,0:T(8,128)S(1)}, u32[]{:S(2)}, u32[]{:S(2)}) %collective-permute-start.10) | collective-permute-done | bytes 294944 | tf_op jit(solution)/shard_map/ppermute | solution.py:351
  108.1 5.1 %collective-permute-done.11 = f32[2,6,48,128]{3,2,1,0:T(8,128)S(1)} collective-permute-done((f32[2,6,48,128]{3,2,1,0:T(8,128)S(1)}, f32[2,6,48,128]{3,2,1,0:T(8,128)S(1)}, u32[]{:S(2)}, u32[]{:S(2)}) %collective-permute-start.11) | collective-permute-done | bytes 294944 | tf_op jit(solution)/shard_map/ppermute | solution.py:351
  118.7 8.3 %collective-permute-done.12 = f32[2,4,48,128]{3,2,1,0:T(8,128)S(1)} collective-permute-done((f32[2,4,48,128]{3,2,1,0:T(8,128)S(1)}, f32[2,4,48,128]{3,2,1,0:T(8,128)S(1)}, u32[]{:S(2)}, u32[]{:S(2)}) %collective-permute-start.12) | collective-permute-done | bytes 196640 | tf_op jit(solution)/shard_map/ppermute | solution.py:371
  126.9 4.3 %collective-permute-done.13 = f32[2,6,48,128]{3,2,1,0:T(8,128)S(1)} collective-permute-done((f32[2,6,48,128]{3,2,1,0:T(8,128)S(1)}, f32[2,6,48,128]{3,2,1,0:T(8,128)S(1)}, u32[]{:S(2)}, u32[]{:S(2)}) %collective-permute-start.13) | collective-permute-done | bytes 294944 | tf_op jit(solution)/shard_map/ppermute | solution.py:364
  134.0 11.0 %last.1 = f32[4,4,96,128]{3,2,1,0:T(8,128)} custom-call(s32[4]{0:T(128)S(1)} %copy-done.6, f32[32,96,128]{2,1,0:T(8,128)S(1)} %copy-done.1, f32[27,96,128]{2,1,0:T(8,128)S(1)} %collective-permute-done.far, f32[27,96,128]{2,1,0:T(8,128)S(1)} %copy-done.5, f32[17,96,128]{2,1,0:T(8,128)} %get-tuple-element.15.own, ...), custom_call_target="tpu_custom_call" | custom-call | tf_op jit(solution)/shard_map/last/pallas_call | solution.py:285
  (110 shorter events, 16.1 us)
Async XLA Ops:
  0.6 28.5 %copy-start.6 = (s32[4]{0:T(128)S(1)}, s32[4]{0:T(128)}, u32[]{:S(2)}) copy-start(s32[4]{0:T(128)} %pad_add_fusion.who) | copy-start | bytes 52
  4.3 23.7 %collective-permute-start = (f32[27,96,128]{2,1,0:T(8,128)}, f32[27,96,128]{2,1,0:T(8,128)S(1)}, u32[]{:S(2)}, u32[]{:S(2)}) collective-permute-start(f32[27,96,128]{2,1,0:T(8,128)} %get-tuple-element.13), channel_id=1, source_target_pairs={{1,2},{2,1},{3,4},{4,3},{5,6},{6,5},{7,8},{8,7},{9,10},{10,9},{11,... | collective-permute-start | bytes 3981320 | tf_op jit(solution)/shard_map/ppermute | solution.py:351
  12.4 15.7 %collective-permute-start.1 = (f32[27,96,128]{2,1,0:T(8,128)}, f32[27,96,128]{2,1,0:T(8,128)S(1)}, u32[]{:S(2)}, u32[]{:S(2)}) collective-permute-start(f32[27,96,128]{2,1,0:T(8,128)} %get-tuple-element.14), channel_id=1, source_target_pairs={{0,1},{1,0},{2,3},{3,2},{4,5},{5,4},{6,7},{7,6},{8,9},{9,8},{10,11... | collective-permute-start | bytes 3981320 | tf_op jit(solution)/shard_map/ppermute | solution.py:351
  29.1 1.4 copy-start
  31.8 28.6 %copy-start.1 = (f32[32,96,128]{2,1,0:T(8,128)S(1)}, f32[32,96,128]{2,1,0:T(8,128)}, u32[]{:S(2)}) copy-start(f32[32,96,128]{2,1,0:T(8,128)} %get-tuple-element.12.fixed) | copy-start | bytes 4718596
  41.6 18.8 %collective-permute-start.2 = (f32[17,96,128]{2,1,0:T(8,128)}, f32[17,96,128]{2,1,0:T(8,128)}, u32[]{:S(2)}, u32[]{:S(2)}) collective-permute-start(f32[17,96,128]{2,1,0:T(8,128)} %get-tuple-element.15.own), channel_id=1, source_target_pairs={{1,2},{2,1},{3,4},{4,3},{5,6},{6,5},{7,8},{8,7},{9,10},{10,9},{11,... | collective-permute-start | bytes 2506760 | tf_op jit(solution)/shard_map/ppermute | solution.py:351
  48.9 11.6 %collective-permute-start.3 = (f32[17,96,128]{2,1,0:T(8,128)}, f32[17,96,128]{2,1,0:T(8,128)}, u32[]{:S(2)}, u32[]{:S(2)}) collective-permute-start(f32[17,96,128]{2,1,0:T(8,128)} %get-tuple-element.16), channel_id=1, source_target_pairs={{0,1},{1,0},{2,3},{3,2},{4,5},{5,4},{6,7},{7,6},{8,9},{9,8},{10,11... | collective-permute-start | bytes 2506760 | tf_op jit(solution)/shard_map/ppermute | solution.py:351
  49.1 11.3 %collective-permute-start.4 = (f32[4,96,128]{2,1,0:T(8,128)S(1)}, f32[4,96,128]{2,1,0:T(8,128)S(1)}, u32[]{:S(2)}, u32[]{:S(2)}) collective-permute-start(f32[4,96,128]{2,1,0:T(8,128)S(1)} %get-tuple-element.17), channel_id=1, source_target_pairs={{0,32},{32,64},{64,96},{96,128},{128,160},{160,192},{192,224},{1,3... | collective-permute-start | bytes 589832 | tf_op jit(solution)/shard_map/ppermute | solution.py:364
  60.5 1.3 copy-start.4
  66.6 12.9 %collective-permute-start.5 = (f32[2,4,48,128]{3,2,1,0:T(8,128)S(1)}, f32[2,4,48,128]{3,2,1,0:T(8,128)S(1)}, u32[]{:S(2)}, u32[]{:S(2)}) collective-permute-start(f32[2,4,48,128]{3,2,1,0:T(8,128)S(1)} %residual.1), channel_id=1, source_target_pairs={{0,32},{32,64},{64,96},{96,128},{128,160},{160,192},{192,224},{1,3... | collective-permute-start | bytes 589832 | tf_op jit(solution)/shard_map/ppermute | solution.py:364
  68.9 12.3 %collective-permute-start.6 = (f32[2,4,48,128]{3,2,1,0:T(8,128)S(1)}, f32[2,4,48,128]{3,2,1,0:T(8,128)S(1)}, u32[]{:S(2)}, u32[]{:S(2)}) collective-permute-start(f32[2,4,48,128]{3,2,1,0:T(8,128)S(1)} %residual.1), channel_id=1, source_target_pairs={{0,64},{32,96},{64,128},{96,160},{128,192},{160,224},{1,65},{33,97... | collective-permute-start | bytes 589832 | tf_op jit(solution)/shard_map/ppermute | solution.py:364
  73.8 7.5 %collective-permute-start.7 = (f32[4,48,128]{2,1,0:T(8,128)S(1)}, f32[4,48,128]{2,1,0:T(8,128)S(1)}, u32[]{:S(2)}, u32[]{:S(2)}) collective-permute-start(f32[4,48,128]{2,1,0:T(8,128)S(1)} %get-tuple-element.46), channel_id=1, source_target_pairs={{0,96},{32,128},{64,160},{96,192},{128,224},{1,97},{33,129},{65,16... | collective-permute-start | bytes 294920 | tf_op jit(solution)/shard_map/ppermute | solution.py:364
  76.6 5.8 %copy-start.9 = (f32[1,96,128]{2,1,0:T(8,128)}, f32[1,96,128]{2,1,0:T(8,128)S(1)}, u32[]{:S(2)}) copy-start(f32[1,96,128]{2,1,0:T(8,128)S(1)} %get-tuple-element.33) | copy-start | bytes 147460
  76.6 5.8 %copy-start.11 = (f32[1,96,128]{2,1,0:T(8,128)}, f32[1,96,128]{2,1,0:T(8,128)S(1)}, u32[]{:S(2)}) copy-start(f32[1,96,128]{2,1,0:T(8,128)S(1)} %get-tuple-element.34) | copy-start | bytes 147460
  82.3 11.9 %collective-permute-start.8 = (f32[6,96,128]{2,1,0:T(8,128)}, f32[6,96,128]{2,1,0:T(8,128)S(1)}, u32[]{:S(2)}, u32[]{:S(2)}) collective-permute-start(f32[6,96,128]{2,1,0:T(8,128)} %get-tuple-element.40), channel_id=1, source_target_pairs={{1,2},{2,1},{3,4},{4,3},{5,6},{6,5},{7,8},{8,7},{9,10},{10,9},{11,... | collective-permute-start | bytes 884744 | tf_op jit(solution)/shard_map/ppermute | solution.py:351
  87.8 6.4 %collective-permute-start.9 = (f32[6,96,128]{2,1,0:T(8,128)}, f32[6,96,128]{2,1,0:T(8,128)}, u32[]{:S(2)}, u32[]{:S(2)}) collective-permute-start(f32[6,96,128]{2,1,0:T(8,128)} %get-tuple-element.39), channel_id=1, source_target_pairs={{0,1},{1,0},{2,3},{3,2},{4,5},{5,4},{6,7},{7,6},{8,9},{9,8},{10,11... | collective-permute-start | bytes 884744 | tf_op jit(solution)/shard_map/ppermute | solution.py:351
  88.0 16.2 %copy-start.10 = (f32[1,96,128]{2,1,0:T(8,128)S(1)}, f32[1,96,128]{2,1,0:T(8,128)}, u32[]{:S(2)}) copy-start(f32[1,96,128]{2,1,0:T(8,128)} %copy-done.9) | copy-start | bytes 147460
  88.0 16.2 %copy-start.12 = (f32[1,96,128]{2,1,0:T(8,128)S(1)}, f32[1,96,128]{2,1,0:T(8,128)}, u32[]{:S(2)}) copy-start(f32[1,96,128]{2,1,0:T(8,128)} %copy-done.11) | copy-start | bytes 147460
  96.1 11.9 %collective-permute-start.10 = (f32[2,6,48,128]{3,2,1,0:T(8,128)S(1)}, f32[2,6,48,128]{3,2,1,0:T(8,128)S(1)}, u32[]{:S(2)}, u32[]{:S(2)}) collective-permute-start(f32[2,6,48,128]{3,2,1,0:T(8,128)S(1)} %pad_maximum_fusion.3), channel_id=1, source_target_pairs={{0,65},{1,64},{2,67},{3,66},{4,69},{5,68},{6,71},{7,70},{8,73},{9,... | collective-permute-start | bytes 884744 | tf_op jit(solution)/shard_map/ppermute | solution.py:351
  98.1 15.1 %collective-permute-start.11 = (f32[2,6,48,128]{3,2,1,0:T(8,128)S(1)}, f32[2,6,48,128]{3,2,1,0:T(8,128)S(1)}, u32[]{:S(2)}, u32[]{:S(2)}) collective-permute-start(f32[2,6,48,128]{3,2,1,0:T(8,128)S(1)} %pad_maximum_fusion.3), channel_id=1, source_target_pairs={{1,66},{2,65},{3,68},{4,67},{5,70},{6,69},{7,72},{8,71},{9,74},{10... | collective-permute-start | bytes 884744 | tf_op jit(solution)/shard_map/ppermute | solution.py:351
  114.6 12.3 %collective-permute-start.12 = (f32[2,4,48,128]{3,2,1,0:T(8,128)S(1)}, f32[2,4,48,128]{3,2,1,0:T(8,128)S(1)}, u32[]{:S(2)}, u32[]{:S(2)}) collective-permute-start(f32[2,4,48,128]{3,2,1,0:T(8,128)S(1)} %get-tuple-element.42), channel_id=1, source_target_pairs={{0,130},{1,131},{2,132},{3,133},{4,134},{5,135},{6,136},{7,137},{8... | collective-permute-start | bytes 589832 | tf_op jit(solution)/shard_map/ppermute | solution.py:371
  115.9 15.3 %collective-permute-start.13 = (f32[2,6,48,128]{3,2,1,0:T(8,128)S(1)}, f32[2,6,48,128]{3,2,1,0:T(8,128)S(1)}, u32[]{:S(2)}, u32[]{:S(2)}) collective-permute-start(f32[2,6,48,128]{3,2,1,0:T(8,128)S(1)} %fusion.55), channel_id=1, source_target_pairs={{0,128},{32,160},{64,192},{96,224},{1,129},{33,161},{65,193},{97,2... | collective-permute-start | bytes 884744 | tf_op jit(solution)/shard_map/ppermute | solution.py:364
  117.4 13.9 %collective-permute-start.14 = (f32[2,4,48,128]{3,2,1,0:T(8,128)S(1)}, f32[2,4,48,128]{3,2,1,0:T(8,128)S(1)}, u32[]{:S(2)}, u32[]{:S(2)}) collective-permute-start(f32[2,4,48,128]{3,2,1,0:T(8,128)S(1)} %get-tuple-element.41), channel_id=1, source_target_pairs={{2,128},{3,129},{4,130},{5,131},{6,132},{7,133},{8,134},{9,135},{1... | collective-permute-start | bytes 589832 | tf_op jit(solution)/shard_map/ppermute | solution.py:371
  132.7 1.3 copy-start.5
  (4 other events, 4.2 us)

commit v4 on v3

--- a/solution.py
+++ b/solution.py
@@ -25,8 +25,18 @@
     return pltpu.roll(values, by % size, axis)
 
 
-def parcel_kernel(who, rates, source, initial, mobility, labels, electrode, far, near, own):
-    odd = who[0]
+def parcel_kernel(rates, source_at, initial_at, mobility_at, labels_at, electrode_at, far, near, own,
+                  source, initial, mobility, labels, electrode, done):
+    odd = lax.rem(lax.axis_index("space"), 2)
+    places = (
+        (labels_at, labels), (electrode_at, electrode), (initial_at, initial),
+        (mobility_at, mobility), (source_at, source),
+    )
+    copies = [pltpu.make_async_copy(there, here, done.at[n]) for n, (there, here) in enumerate(places)]
+    for copy in copies:
+        copy.start()
+    for copy in copies:
+        copy.wait()
 
     @pl.loop(0, SLAB)
     def _(p):
@@ -158,8 +168,8 @@
     return 0.25 * ((read(0, 0) + read(0, 1)) + (read(1, 0) + read(1, 1)))
 
 
-def first_kernel(who, fixed, far, near, to_far, to_near, rough_out, closing,
-                 force, begin, mob, kap, open_cell, weights, cells, other):
+def first_kernel(who, fixed, far, near, to_far, to_near, closing,
+                 force, begin, mob, kap, open_cell, weights, cells, other, rough):
     odd = who[0]
     height = fixed.shape[1]
     load_static(odd, fixed, far, near, force, begin, mob, kap, open_cell)
@@ -178,17 +188,17 @@
         closing[p] = cells[STEPS - 1, 4 + p, pl.ds(EDGE, height)]
     half = height // 2
     for a in range(6):
-        rough_out[a] = halved(lambda x, y: mob[2 * a + x, pl.ds(EDGE + y, half, stride=2)])
+        rough[a] = halved(lambda x, y: mob[2 * a + x, pl.ds(EDGE + y, half, stride=2)])
     for out, base in ((to_far, 4 - 4 * odd), (to_near, 4 * odd)):
         for t in range(STEPS):
             for p in range(SLAB):
                 out[4 * t + p] = cells[t, 4 + p, pl.ds(EDGE, height)]
-        out[16, pl.ds(0, half)] = rough_out[base]
-        out[16, pl.ds(half, half)] = rough_out[base + 1]
-
-
-def residual_kernel(who, fixed, far, near, own, low_far, low_near,
-                    both, force, begin, mob, kap, open_cell, weights, cells, residues):
+        out[16, pl.ds(0, half)] = rough[base]
+        out[16, pl.ds(half, half)] = rough[base + 1]
+
+
+def residual_kernel(who, fixed, far, near, own, low_far, low_near, arriving,
+                    base, closing, both, rhs, rough, force, begin, mob, kap, open_cell, weights, cells, residues):
     odd, leading, place, count = who[0], who[1], who[2], who[3]
     height = fixed.shape[1]
     half = height // 2
@@ -223,8 +233,16 @@
         coarse = 2 * place - 1 + a
         inside = jnp.logical_and(coarse >= 0, coarse < 2 * count)
         value = halved(lambda x, y: residues[2 * a + x, pl.ds(y, half, stride=2)])
-        both[0, a] = jnp.where(inside, value, 0.0)
-        both[1, a] = halved(lambda x, y: cells[STEPS - 1, 2 + 2 * a + x, pl.ds(EDGE + y, half, stride=2)])
+        base[a] = jnp.where(inside, value, 0.0)
+        closing[a] = halved(lambda x, y: cells[STEPS - 1, 2 + 2 * a + x, pl.ds(EDGE + y, half, stride=2)])
+        both[0, a] = base[a]
+        both[1, a] = closing[a]
+    for a in range(2):
+        rhs[a] = base[1 + a] + halved(lambda x, y: arriving[2 * a + x, pl.ds(y, half, stride=2)])
+        for block, at in ((low_far, 8 * odd), (low_near, 8 - 8 * odd)):
+            rough[at + a] = block[16, pl.ds(half * a, half)]
+    for a in range(6):
+        rough[2 + a] = halved(lambda x, y: mob[2 * a + x, pl.ds(EDGE + y, half, stride=2)])
 
 
 def last_kernel(who, fixed, far, near, own, low_far, low_near, arriving, side_far, side_near, correction,
@@ -281,15 +299,15 @@
     ]
 
 
-def call(kernel, name, inputs, outputs, scratch, scalars=1, grant=28):
+def call(kernel, name, inputs, outputs, scratch):
     return pl.pallas_call(
         kernel,
         out_shape=[jax.ShapeDtypeStruct(o, jnp.float32) for o in outputs],
-        in_specs=[SMEM] * scalars + [VMEM] * (len(inputs) - scalars),
+        in_specs=[SMEM] + [VMEM] * (len(inputs) - 1),
         out_specs=[VMEM] * len(outputs),
         scratch_shapes=scratch,
         name=name,
-        compiler_params=pltpu.CompilerParams(vmem_limit_bytes=grant << 20),
+        compiler_params=pltpu.CompilerParams(vmem_limit_bytes=28 << 20),
     )(*inputs)
 
 
@@ -335,40 +353,31 @@
         return values
 
 
-def traded(far, near, steps=0):
+def sent(value, steps, to):
     times = lax.axis_size("tm")
     count = lax.axis_size("space")
+    pairs = [
+        (k * count + i, (k + steps) * count + to[i])
+        for k in range(times - steps)
+        for i in range(count)
+        if 0 <= to[i] < count
+    ]
+    return lax.ppermute(value, ("tm", "space"), pairs)
+
+
+def traded(far, near):
+    count = lax.axis_size("space")
     far_of = [i + 1 if i % 2 else i - 1 for i in range(count)]
-    near_of = [i ^ 1 for i in range(count)]
-
-    def send(value, to):
-        pairs = [
-            (k * count + i, (k + steps) * count + to[i])
-            for k in range(times - steps)
-            for i in range(count)
-            if 0 <= to[i] < count
-        ]
-        return lax.ppermute(value, ("tm", "space"), pairs)
-
-    return send(far, far_of), send(near, near_of)
+    return sent(far, 0, far_of), sent(near, 0, [i ^ 1 for i in range(count)])
 
 
 def by_side(odd, far, near):
     return jnp.where(odd, near, far), jnp.where(odd, far, near)
 
 
-def arrived(value, steps, shift=0):
+def arrived(value, steps):
     times = lax.axis_size("tm")
-    count = lax.axis_size("space")
-    if shift == 0:
-        return lax.ppermute(value, "tm", [(k, k + steps) for k in range(times - steps)])
-    pairs = [
-        (k * count + s + shift, (k + steps) * count + s)
-        for k in range(times - steps)
-        for s in range(count)
-        if 0 <= s + shift < count
-    ]
-    return lax.ppermute(value, ("tm", "space"), pairs)
+    return lax.ppermute(value, "tm", [(k, k + steps) for k in range(times - steps)])
 
 
 def on_device(source, initial, mobility, labels, electrode, rates):
@@ -383,50 +392,48 @@
         & (2 * place + jnp.arange(-reach, 2 + reach) < 2 * lax.axis_size("space"))
     ).astype(jnp.float32)
 
-    far, near, fixed = call(
+    there = pl.BlockSpec(memory_space=pltpu.HBM)
+    fields = (source, initial, mobility, labels, electrode)
+    far, near, fixed = pl.pallas_call(
         parcel_kernel,
-        "parcel",
-        (who, rates, source, initial, mobility, labels, electrode),
-        [(PARCEL,) + plane] * 2 + [(OWN,) + plane],
-        [],
-        2,
-        60,
-    )
+        out_shape=[jax.ShapeDtypeStruct((n,) + plane, jnp.float32) for n in (PARCEL, PARCEL, OWN)],
+        in_specs=[SMEM] + [there] * len(fields),
+        out_specs=[VMEM] * 3,
+        scratch_shapes=[pltpu.VMEM(v.shape, v.dtype) for v in fields] + [pltpu.SemaphoreType.DMA((len(fields),))],
+        name="parcel",
+        compiler_params=pltpu.CompilerParams(vmem_limit_bytes=60 << 20),
+    )(rates, *fields)
     far, near = traded(far, near)
     static = (who, fixed, far, near)
     tall = (height + 2 * EDGE, depth)
 
     coarse = (height // 2, depth)
-    to_far, to_near, rough, closing = call(
+    to_far, to_near, closing = call(
         first_kernel,
         "first",
         static,
-        [(17,) + plane] * 2 + [(6,) + coarse, initial.shape],
-        windows(height, depth) + [pltpu.VMEM((STEPS, 12) + tall, jnp.float32)] * 2,
+        [(17,) + plane] * 2 + [initial.shape],
+        windows(height, depth) + [pltpu.VMEM((STEPS, 12) + tall, jnp.float32)] * 2
+        + [pltpu.VMEM((6,) + coarse, jnp.float32)],
     )
     got_far, got_near = traded(to_far, to_near)
     opening = arrived(closing, 1)
     states = (to_far, got_far, got_near)
 
-    (both,) = call(
+    base, closing, both, rhs, rough_w = call(
         residual_kernel,
         "residual",
-        static + states,
-        [(2, 4) + coarse],
+        static + states + (opening,),
+        [(4,) + coarse] * 2 + [(2, 4) + coarse, (2,) + coarse, (10,) + coarse],
         windows(height, depth)
         + [pltpu.VMEM((STEPS, 12) + tall, jnp.float32), pltpu.VMEM((8,) + plane, jnp.float32)],
     )
-    rough_of = lambda b: b[16].reshape((2,) + coarse)
-    low, high = by_side(odd == 1, rough_of(got_far), rough_of(got_near))
-    rough_w = jnp.concatenate([low, rough, high], axis=0)
-
-    one = arrived(both, 1)
+    one = arrived(base, 1)
     two = arrived(both, 2)
-    three = arrived(both[1], 3)
-    rhs = both[0] + one[1]
-    rhs1 = one[0] + two[1]
+    three = arrived(closing, 3)
+    rhs1 = one + two[1]
     rhs2 = two[0] + three
-    pair = jnp.stack([inner(rhs, 0, 1), inner(rhs1, 0, 1)])
+    pair = jnp.stack([rhs, inner(rhs1, 0, 1)])
     pair = pair + Coupling(inner(rough_w, 0, 3), inside(1)).step(jnp.stack([rhs1, rhs2]))
 
     flat = lambda v: v.reshape((-1,) + plane)
@@ -439,12 +446,24 @@
     pair_of = lambda b: b[:4].reshape(pair.shape)
     rough_far = jnp.concatenate([low[4:], rough_w, high[4:]], axis=0)
     pair = jnp.concatenate([pair_of(low), pair, pair_of(high)], axis=1)
-    low, high = by_side(odd == 1, *traded(pair, pair, 2))
-    middle = jnp.where(place == 0, high[:, :2], low[:, 4:])
-    older = jnp.concatenate([low[:, :4], middle, high[:, 2:]], axis=1)
+    joined = lambda *parts: jnp.concatenate(parts, axis=1)
+    count = lax.axis_size("space")
+    gap = jnp.zeros_like(pair[:, :2])
+    got = sent(pair, 2, [i if i in (0, count - 1) else i + 1 if i % 2 else i - 1 for i in range(count)])
+    got = jnp.where(place == 0, joined(gap, got[:, :4]), got)
+    got = jnp.where(place == count - 1, joined(got[:, 2:], gap), got)
+    mate = sent(got, 0, [i ^ 1 for i in range(count)])
+    older = jnp.where(odd == 1, joined(mate[:, 2:], got), joined(got, mate[:, :4]))
     coupling = Coupling(rough_far, inside(6))
     pair = pair + coupling.steps(older, 2)
-    older = jnp.concatenate([arrived(pair[:, :4], 4, -2), arrived(pair, 4), arrived(pair[:, 2:], 4, 2)], axis=1)
+    got = joined(sent(pair, 4, [i - 2 if i % 2 else i + 2 for i in range(count)]), sent(pair[:, 2:4], 4, range(count)))
+    mate = sent(got, 0, [i ^ 1 for i in range(count)])
+    centre, beside = got[:, 6:], mate[:, 6:]
+    older = jnp.where(
+        odd == 1,
+        joined(mate[:, 2:6], beside, centre, got[:, :6]),
+        joined(got[:, :6], centre, beside, mate[:, :4]),
+    )
     correction = pair + coupling.steps(older, 4)
 
     (density,) = call(

time: 146 us -> 143 us (0.979)
  local copies, waits for them, and re-layouts: 7.37 us -> 12.6 us
  waiting for transfers between devices: 54.9 us -> 51.4 us
  starting transfers between devices: 45.5 us -> 43.2 us
  other arithmetic: 7.31 us -> 5.14 us
    pallas_call x4 -> x3, Pallas kernels: 29.2 us -> 24.4 us  [call(): pl.pallas_call(kernel, out_shape=[jax.ShapeDtypeStruct(o, jnp.float32) fo...]
    pallas_call x0 -> x1, Pallas kernels: none -> 4.52 us  [on_device(): pl.pallas_call(parcel_kernel, out_shape=[jax.ShapeDtypeStruct((n,) + plan...]
    ppermute x5 -> x4, waiting for transfers between devices: 16.6 us -> 13.1 us  [arrived(): lax.ppermute(value, 'tm', [(k, k + steps) for k in range(times - steps)])]
    unnamed x32 -> x28, local copies, waits for them, and re-layouts: 6.71 us -> 9.48 us
    select_n x4 -> x2, other arithmetic: 2.69 us -> 0.07 us  [by_side(): return (jnp.where(odd, near, far), jnp.where(odd, far, near))]
    ppermute x5 -> x4, starting transfers between devices: 13.9 us -> 12.1 us  [arrived(): lax.ppermute(value, 'tm', [(k, k + steps) for k in range(times - steps)])]
    slice x2, local copies, waits for them, and re-layouts: 0.01 us -> 1.6 us  [on_device(): rough_far = jnp.concatenate([low[4:], rough_w, high[4:]], axis=0)]
    ppermute x10 -> x11, starting transfers between devices: 31.6 us -> 31.1 us  [sent(): return lax.ppermute(value, ('tm', 'space'), pairs)]
  transfers between devices with their start and end apart: 15 -> 15, of which waited for: 9 -> 10; matrix products, arithmetic and copies ran while one was open for 1% -> 2% of each run, Pallas kernels for 0% -> 0%
where the time goes in v4:
time: 143 us; the launch traced here: 142 us
  waiting for transfers between devices  51.4 us (36%)
  starting transfers between devices  43.2 us (30%)
  Pallas kernels  28.9 us (20%)
  local copies, waits for them, and re-layouts  12.6 us (9%)
  other arithmetic  5.14 us (4%)
    ppermute x11, waiting for transfers between devices, sent(): return lax.ppermute(value, ('tm', 'space'), pairs)  38.3 us
    ppermute x11, starting transfers between devices, sent(): return lax.ppermute(value, ('tm', 'space'), pairs)  31.1 us
    pallas_call x3, Pallas kernels, call(): pl.pallas_call(kernel, out_shape=[jax.ShapeDtypeStruct(o, jnp.float32) fo...  24.4 us
    ppermute x4, waiting for transfers between devices, arrived(): lax.ppermute(value, 'tm', [(k, k + steps) for k in range(times - steps)])  13.1 us
    ppermute x4, starting transfers between devices, arrived(): lax.ppermute(value, 'tm', [(k, k + steps) for k in range(times - steps)])  12.1 us
    unnamed x28, local copies, waits for them, and re-layouts  9.48 us
    pallas_call x1, Pallas kernels, on_device(): pl.pallas_call(parcel_kernel, out_shape=[jax.ShapeDtypeStruct((n,) + plan...  4.52 us
  transfers between devices with their start and end apart: 15, of which 10 were waited for; matrix products, arithmetic and copies ran while one was open for 2% of the time, Pallas kernels for 0%

profile of v4, /device:TPU:6, one launch (start us, length us, event | category | flops | bytes accessed | tf_op | source)
XLA Modules:
  0.0 141.9 jit_solution(6905524759694160742)
XLA Ops:
  0.0 4.5 %parcel.1 = (f32[27,96,128]{2,1,0:T(8,128)}, f32[27,96,128]{2,1,0:T(8,128)}, f32[32,96,128]{2,1,0:T(8,128)}) custom-call(f32[4]{0:T(128)} %rates.1, f32[4,4,96,128]{3,2,1,0:T(8,128)} %source_at.1, f32[4,96,128]{2,1,0:T(8,128)} %initial_at.1, f32[4,96,128]{2,1,0:T(8,128)} %mobility_at.1, s32[4,96,128]{2,1,0:T(8,128)} %labels_at.1, s32[4,96,128]{2,1,0:T(8,128)} %electrode_at.1), custom_call_target="tpu_custom_call" | custom-call | tf_op jit(solution)/shard_map/parcel/pallas_call | solution.py:397
  4.5 8.0 %collective-permute-start = (f32[27,96,128]{2,1,0:T(8,128)}, f32[27,96,128]{2,1,0:T(8,128)S(1)}, u32[]{:S(2)}, u32[]{:S(2)}) collective-permute-start(f32[27,96,128]{2,1,0:T(8,128)} %get-tuple-element.17), channel_id=1, source_target_pairs={{1,2},{2,1},{3,4},{4,3},{5,6},{6,5},{7,8},{8,7},{9,10},{10,9},{11,... | collective-permute-start | bytes 3981320 | tf_op jit(solution)/shard_map/ppermute | solution.py:365
  12.8 15.5 %collective-permute-done.far = f32[27,96,128]{2,1,0:T(8,128)S(1)} collective-permute-done((f32[27,96,128]{2,1,0:T(8,128)}, f32[27,96,128]{2,1,0:T(8,128)S(1)}, u32[]{:S(2)}, u32[]{:S(2)}) %collective-permute-start) | collective-permute-done | bytes 1327136 | tf_op jit(solution)/shard_map/ppermute | solution.py:365
  29.3 1.4 copy-done
  30.7 1.3 copy-done.3
  32.1 9.3 %first.1 = (f32[17,96,128]{2,1,0:T(8,128)}, f32[17,96,128]{2,1,0:T(8,128)}, f32[4,96,128]{2,1,0:T(8,128)S(1)}) custom-call(s32[4]{0:T(128)S(1)} %pad_add_fusion.who, f32[32,96,128]{2,1,0:T(8,128)S(1)} %copy-done, f32[27,96,128]{2,1,0:T(8,128)S(1)} %collective-permute-done.far, f32[27,96,128]{2,1,0:T(8,128)S(1)} %copy-done.3), custom_call_target="tpu_custom_call" | custom-call | tf_op jit(solution)/shard_map/first/pallas_call | solution.py:303
  41.3 7.2 %collective-permute-start.2 = (f32[17,96,128]{2,1,0:T(8,128)}, f32[17,96,128]{2,1,0:T(8,128)}, u32[]{:S(2)}, u32[]{:S(2)}) collective-permute-start(f32[17,96,128]{2,1,0:T(8,128)} %get-tuple-element.19.own), channel_id=1, source_target_pairs={{1,2},{2,1},{3,4},{4,3},{5,6},{6,5},{7,8},{8,7},{9,10},{10,9},{11,... | collective-permute-start | bytes 2506760 | tf_op jit(solution)/shard_map/ppermute | solution.py:365
  48.8 3.5 %collective-permute-start.4 = (f32[4,96,128]{2,1,0:T(8,128)S(1)}, f32[4,96,128]{2,1,0:T(8,128)S(1)}, u32[]{:S(2)}, u32[]{:S(2)}) collective-permute-start(f32[4,96,128]{2,1,0:T(8,128)S(1)} %get-tuple-element.21), channel_id=1, source_target_pairs={{0,32},{32,64},{64,96},{96,128},{128,160},{160,192},{192,224},{1,3... | collective-permute-start | bytes 589832 | tf_op jit(solution)/shard_map/ppermute | solution.py:380
  52.3 7.7 %collective-permute-done.4.arriving = f32[4,96,128]{2,1,0:T(8,128)S(1)} collective-permute-done((f32[4,96,128]{2,1,0:T(8,128)S(1)}, f32[4,96,128]{2,1,0:T(8,128)S(1)}, u32[]{:S(2)}, u32[]{:S(2)}) %collective-permute-start.4) | collective-permute-done | bytes 196640 | tf_op jit(solution)/shard_map/ppermute | solution.py:380
  60.1 1.3 copy-done.4
  61.5 4.7 %residual.1 = (f32[4,48,128]{2,1,0:T(8,128)S(1)}, f32[4,48,128]{2,1,0:T(8,128)S(1)}, f32[2,4,48,128]{3,2,1,0:T(8,128)S(1)}, f32[2,48,128]{2,1,0:T(8,128)S(1)}, f32[10,48,128]{2,1,0:T(8,128)S(1)}) custom-call(s32[4]{0:T(128)S(1)} %pad_add_fusion.who, f32[32,96,128]{2,1,0:T(8,128)S(1)} %copy-done.1, f32[27,96,128]{2,1,0:T(8,128)S(1)} %collective-permute-done.far, ...), custom_call_target="tpu_custom_call" | custom-call | tf_op jit(solution)/shard_map/residual/pallas_call | solution.py:303
  66.2 4.1 %collective-permute-start.6 = (f32[2,4,48,128]{3,2,1,0:T(8,128)S(1)}, f32[2,4,48,128]{3,2,1,0:T(8,128)S(1)}, u32[]{:S(2)}, u32[]{:S(2)}) collective-permute-start(f32[2,4,48,128]{3,2,1,0:T(8,128)S(1)} %get-tuple-element.24), channel_id=1, source_target_pairs={{0,64},{32,96},{64,128},{96,160},{128,192},{160,224},{1,65},{33,97... | collective-permute-start | bytes 589832 | tf_op jit(solution)/shard_map/ppermute | solution.py:380
  70.3 2.6 %collective-permute-start.5 = (f32[4,48,128]{2,1,0:T(8,128)S(1)}, f32[4,48,128]{2,1,0:T(8,128)S(1)}, u32[]{:S(2)}, u32[]{:S(2)}) collective-permute-start(f32[4,48,128]{2,1,0:T(8,128)S(1)} %get-tuple-element.23), channel_id=1, source_target_pairs={{0,32},{32,64},{64,96},{96,128},{128,160},{160,192},{192,224},{1,3... | collective-permute-start | bytes 294920 | tf_op jit(solution)/shard_map/ppermute | solution.py:380
  72.9 1.9 %collective-permute-start.7 = (f32[4,48,128]{2,1,0:T(8,128)S(1)}, f32[4,48,128]{2,1,0:T(8,128)S(1)}, u32[]{:S(2)}, u32[]{:S(2)}) collective-permute-start(f32[4,48,128]{2,1,0:T(8,128)S(1)} %get-tuple-element.26), channel_id=1, source_target_pairs={{0,96},{32,128},{64,160},{96,192},{128,224},{1,97},{33,129},{65,16... | collective-permute-start | bytes 294920 | tf_op jit(solution)/shard_map/ppermute | solution.py:380
  74.9 4.4 %collective-permute-done.5 = f32[4,48,128]{2,1,0:T(8,128)S(1)} collective-permute-done((f32[4,48,128]{2,1,0:T(8,128)S(1)}, f32[4,48,128]{2,1,0:T(8,128)S(1)}, u32[]{:S(2)}, u32[]{:S(2)}) %collective-permute-start.5) | collective-permute-done | bytes 98336 | tf_op jit(solution)/shard_map/ppermute | solution.py:380
  80.5 5.5 %collective-permute-start.8 = (f32[6,96,128]{2,1,0:T(8,128)S(1)}, f32[6,96,128]{2,1,0:T(8,128)S(1)}, u32[]{:S(2)}, u32[]{:S(2)}) collective-permute-start(f32[6,96,128]{2,1,0:T(8,128)S(1)} %get-tuple-element.44), channel_id=1, source_target_pairs={{1,2},{2,1},{3,4},{4,3},{5,6},{6,5},{7,8},{8,7},{9,10},{10,9},{11,... | collective-permute-start | bytes 884744 | tf_op jit(solution)/shard_map/ppermute | solution.py:365
  86.2 6.0 %collective-permute-done.8.side_far = f32[6,96,128]{2,1,0:T(8,128)S(1)} collective-permute-done((f32[6,96,128]{2,1,0:T(8,128)S(1)}, f32[6,96,128]{2,1,0:T(8,128)S(1)}, u32[]{:S(2)}, u32[]{:S(2)}) %collective-permute-start.8) | collective-permute-done | bytes 294944 | tf_op jit(solution)/shard_map/ppermute | solution.py:365
  95.7 7.3 %collective-permute-start.10 = (f32[2,6,48,128]{3,2,1,0:T(8,128)}, f32[2,6,48,128]{3,2,1,0:T(8,128)}, u32[]{:S(2)}, u32[]{:S(2)}) collective-permute-start(f32[2,6,48,128]{3,2,1,0:T(8,128)} %pad_maximum_fusion.7), channel_id=1, source_target_pairs={{0,64},{1,66},{2,65},{3,68},{4,67},{5,70},{6,69},{7,72},{8,71},{9,... | collective-permute-start | bytes 884744 | tf_op jit(solution)/shard_map/ppermute | solution.py:365
  104.7 5.0 %collective-permute-done.10 = f32[2,6,48,128]{3,2,1,0:T(8,128)} collective-permute-done((f32[2,6,48,128]{3,2,1,0:T(8,128)}, f32[2,6,48,128]{3,2,1,0:T(8,128)}, u32[]{:S(2)}, u32[]{:S(2)}) %collective-permute-start.10) | collective-permute-done | bytes 294944 | tf_op jit(solution)/shard_map/ppermute | solution.py:365
  114.7 1.3 collective-permute-start.12
  116.1 1.3 collective-permute-start.13
  117.4 8.2 %collective-permute-done.13 = f32[2,2,48,128]{3,2,1,0:T(8,128)S(1)} collective-permute-done((f32[2,2,48,128]{3,2,1,0:T(8,128)S(1)}, f32[2,2,48,128]{3,2,1,0:T(8,128)S(1)}, u32[]{:S(2)}, u32[]{:S(2)}) %collective-permute-start.13) | collective-permute-done | bytes 98336 | tf_op jit(solution)/shard_map/ppermute | solution.py:365
  127.0 1.5 %collective-permute-done.14 = f32[2,8,48,128]{3,2,1,0:T(8,128)S(1)} collective-permute-done((f32[2,8,48,128]{3,2,1,0:T(8,128)S(1)}, f32[2,8,48,128]{3,2,1,0:T(8,128)S(1)}, u32[]{:S(2)}, u32[]{:S(2)}) %collective-permute-start.14) | collective-permute-done | bytes 393248 | tf_op jit(solution)/shard_map/ppermute | solution.py:365
  131.5 10.4 %last.1 = f32[4,4,96,128]{3,2,1,0:T(8,128)} custom-call(s32[4]{0:T(128)S(1)} %pad_add_fusion.who, f32[32,96,128]{2,1,0:T(8,128)S(1)} %copy-done.1, f32[27,96,128]{2,1,0:T(8,128)S(1)} %collective-permute-done.far, f32[27,96,128]{2,1,0:T(8,128)S(1)} %copy-done.5, f32[17,96,128]{2,1,0:T(8,128)} %get-tuple-element.19.own, ...), custom_call_target="tpu_custom_call" | custom-call | tf_op jit(solution)/shard_map/last/pallas_call | solution.py:303
  (106 shorter events, 17.3 us)
Async XLA Ops:
  4.5 23.7 %collective-permute-start = (f32[27,96,128]{2,1,0:T(8,128)}, f32[27,96,128]{2,1,0:T(8,128)S(1)}, u32[]{:S(2)}, u32[]{:S(2)}) collective-permute-start(f32[27,96,128]{2,1,0:T(8,128)} %get-tuple-element.17), channel_id=1, source_target_pairs={{1,2},{2,1},{3,4},{4,3},{5,6},{6,5},{7,8},{8,7},{9,10},{10,9},{11,... | collective-permute-start | bytes 3981320 | tf_op jit(solution)/shard_map/ppermute | solution.py:365
  12.6 15.7 %collective-permute-start.1 = (f32[27,96,128]{2,1,0:T(8,128)}, f32[27,96,128]{2,1,0:T(8,128)S(1)}, u32[]{:S(2)}, u32[]{:S(2)}) collective-permute-start(f32[27,96,128]{2,1,0:T(8,128)} %get-tuple-element.18), channel_id=1, source_target_pairs={{0,1},{1,0},{2,3},{3,2},{4,5},{5,4},{6,7},{7,6},{8,9},{9,8},{10,11... | collective-permute-start | bytes 3981320 | tf_op jit(solution)/shard_map/ppermute | solution.py:365
  28.2 1.1 copy-start.2
  29.3 1.4 copy-start
  30.7 1.3 copy-start.3
  32.1 28.1 %copy-start.1 = (f32[32,96,128]{2,1,0:T(8,128)S(1)}, f32[32,96,128]{2,1,0:T(8,128)}, u32[]{:S(2)}) copy-start(f32[32,96,128]{2,1,0:T(8,128)} %get-tuple-element.16.fixed) | copy-start | bytes 4718596
  41.3 18.8 %collective-permute-start.2 = (f32[17,96,128]{2,1,0:T(8,128)}, f32[17,96,128]{2,1,0:T(8,128)}, u32[]{:S(2)}, u32[]{:S(2)}) collective-permute-start(f32[17,96,128]{2,1,0:T(8,128)} %get-tuple-element.19.own), channel_id=1, source_target_pairs={{1,2},{2,1},{3,4},{4,3},{5,6},{6,5},{7,8},{8,7},{9,10},{10,9},{11,... | collective-permute-start | bytes 2506760 | tf_op jit(solution)/shard_map/ppermute | solution.py:365
  48.6 11.5 %collective-permute-start.3 = (f32[17,96,128]{2,1,0:T(8,128)}, f32[17,96,128]{2,1,0:T(8,128)}, u32[]{:S(2)}, u32[]{:S(2)}) collective-permute-start(f32[17,96,128]{2,1,0:T(8,128)} %get-tuple-element.20), channel_id=1, source_target_pairs={{0,1},{1,0},{2,3},{3,2},{4,5},{5,4},{6,7},{7,6},{8,9},{9,8},{10,11... | collective-permute-start | bytes 2506760 | tf_op jit(solution)/shard_map/ppermute | solution.py:365
  48.8 11.3 %collective-permute-start.4 = (f32[4,96,128]{2,1,0:T(8,128)S(1)}, f32[4,96,128]{2,1,0:T(8,128)S(1)}, u32[]{:S(2)}, u32[]{:S(2)}) collective-permute-start(f32[4,96,128]{2,1,0:T(8,128)S(1)} %get-tuple-element.21), channel_id=1, source_target_pairs={{0,32},{32,64},{64,96},{96,128},{128,160},{160,192},{192,224},{1,3... | collective-permute-start | bytes 589832 | tf_op jit(solution)/shard_map/ppermute | solution.py:380
  60.1 1.3 copy-start.4
  66.2 14.1 %collective-permute-start.6 = (f32[2,4,48,128]{3,2,1,0:T(8,128)S(1)}, f32[2,4,48,128]{3,2,1,0:T(8,128)S(1)}, u32[]{:S(2)}, u32[]{:S(2)}) collective-permute-start(f32[2,4,48,128]{3,2,1,0:T(8,128)S(1)} %get-tuple-element.24), channel_id=1, source_target_pairs={{0,64},{32,96},{64,128},{96,160},{128,192},{160,224},{1,65},{33,97... | collective-permute-start | bytes 589832 | tf_op jit(solution)/shard_map/ppermute | solution.py:380
  70.3 9.0 %collective-permute-start.5 = (f32[4,48,128]{2,1,0:T(8,128)S(1)}, f32[4,48,128]{2,1,0:T(8,128)S(1)}, u32[]{:S(2)}, u32[]{:S(2)}) collective-permute-start(f32[4,48,128]{2,1,0:T(8,128)S(1)} %get-tuple-element.23), channel_id=1, source_target_pairs={{0,32},{32,64},{64,96},{96,128},{128,160},{160,192},{192,224},{1,3... | collective-permute-start | bytes 294920 | tf_op jit(solution)/shard_map/ppermute | solution.py:380
  72.9 7.4 %collective-permute-start.7 = (f32[4,48,128]{2,1,0:T(8,128)S(1)}, f32[4,48,128]{2,1,0:T(8,128)S(1)}, u32[]{:S(2)}, u32[]{:S(2)}) collective-permute-start(f32[4,48,128]{2,1,0:T(8,128)S(1)} %get-tuple-element.26), channel_id=1, source_target_pairs={{0,96},{32,128},{64,160},{96,192},{128,224},{1,97},{33,129},{65,16... | collective-permute-start | bytes 294920 | tf_op jit(solution)/shard_map/ppermute | solution.py:380
  80.5 11.7 %collective-permute-start.8 = (f32[6,96,128]{2,1,0:T(8,128)S(1)}, f32[6,96,128]{2,1,0:T(8,128)S(1)}, u32[]{:S(2)}, u32[]{:S(2)}) collective-permute-start(f32[6,96,128]{2,1,0:T(8,128)S(1)} %get-tuple-element.44), channel_id=1, source_target_pairs={{1,2},{2,1},{3,4},{4,3},{5,6},{6,5},{7,8},{8,7},{9,10},{10,9},{11,... | collective-permute-start | bytes 884744 | tf_op jit(solution)/shard_map/ppermute | solution.py:365
  86.1 6.1 %collective-permute-start.9 = (f32[6,96,128]{2,1,0:T(8,128)S(1)}, f32[6,96,128]{2,1,0:T(8,128)S(1)}, u32[]{:S(2)}, u32[]{:S(2)}) collective-permute-start(f32[6,96,128]{2,1,0:T(8,128)S(1)} %get-tuple-element.43), channel_id=1, source_target_pairs={{0,1},{1,0},{2,3},{3,2},{4,5},{5,4},{6,7},{7,6},{8,9},{9,8},{10,11... | collective-permute-start | bytes 884744 | tf_op jit(solution)/shard_map/ppermute | solution.py:365
  95.7 14.1 %collective-permute-start.10 = (f32[2,6,48,128]{3,2,1,0:T(8,128)}, f32[2,6,48,128]{3,2,1,0:T(8,128)}, u32[]{:S(2)}, u32[]{:S(2)}) collective-permute-start(f32[2,6,48,128]{3,2,1,0:T(8,128)} %pad_maximum_fusion.7), channel_id=1, source_target_pairs={{0,64},{1,66},{2,65},{3,68},{4,67},{5,70},{6,69},{7,72},{8,71},{9,... | collective-permute-start | bytes 884744 | tf_op jit(solution)/shard_map/ppermute | solution.py:365
  111.8 1.7 %collective-permute-start.11 = (f32[2,6,48,128]{3,2,1,0:T(8,128)S(1)}, f32[2,6,48,128]{3,2,1,0:T(8,128)S(1)}, u32[]{:S(2)}, u32[]{:S(2)}) collective-permute-start(f32[2,6,48,128]{3,2,1,0:T(8,128)S(1)} %pad_select_fusion), channel_id=1, source_target_pairs={{0,1},{1,0},{2,3},{3,2},{4,5},{5,4},{6,7},{7,6},{8,9},{9,8},{10,11... | collective-permute-start | bytes 884744 | tf_op jit(solution)/shard_map/ppermute | solution.py:365
  113.6 0.9 copy-start.11
  114.7 11.9 %collective-permute-start.12 = (f32[2,6,48,128]{3,2,1,0:T(8,128)S(1)}, f32[2,6,48,128]{3,2,1,0:T(8,128)S(1)}, u32[]{:S(2)}, u32[]{:S(2)}) collective-permute-start(f32[2,6,48,128]{3,2,1,0:T(8,128)S(1)} %fusion.59), channel_id=1, source_target_pairs={{0,130},{2,132},{3,129},{4,134},{5,131},{6,136},{7,133},{8,138},{9... | collective-permute-start | bytes 884744 | tf_op jit(solution)/shard_map/ppermute | solution.py:365
  116.1 9.5 %collective-permute-start.13 = (f32[2,2,48,128]{3,2,1,0:T(8,128)S(1)}, f32[2,2,48,128]{3,2,1,0:T(8,128)S(1)}, u32[]{:S(2)}, u32[]{:S(2)}) collective-permute-start(f32[2,2,48,128]{3,2,1,0:T(8,128)S(1)} %slice.501), channel_id=1, source_target_pairs={{0,128},{1,129},{2,130},{3,131},{4,132},{5,133},{6,134},{7,135},{8... | collective-permute-start | bytes 294920 | tf_op jit(solution)/shard_map/ppermute | solution.py:365
  126.7 1.8 %collective-permute-start.14 = (f32[2,8,48,128]{3,2,1,0:T(8,128)S(1)}, f32[2,8,48,128]{3,2,1,0:T(8,128)S(1)}, u32[]{:S(2)}, u32[]{:S(2)}) collective-permute-start(f32[2,8,48,128]{3,2,1,0:T(8,128)S(1)} %pad_maximum_fusion.2), channel_id=1, source_target_pairs={{0,1},{1,0},{2,3},{3,2},{4,5},{5,4},{6,7},{7,6},{8,9},{9,8},{10,11... | collective-permute-start | bytes 1179656 | tf_op jit(solution)/shard_map/ppermute | solution.py:365
  130.1 1.3 copy-start.5
  130.1 1.4 copy-start.7
  130.1 1.4 %copy-start.9 = (f32[6,96,128]{2,1,0:T(8,128)S(1)}, f32[6,96,128]{2,1,0:T(8,128)}, u32[]{:S(2)}) copy-start(f32[6,96,128]{2,1,0:T(8,128)} %copy-done.8) | copy-start | bytes 884740
  (5 other events, 3.4 us)

commit v5 on v4

--- a/solution.py
+++ b/solution.py
@@ -25,18 +25,8 @@
     return pltpu.roll(values, by % size, axis)
 
 
-def parcel_kernel(rates, source_at, initial_at, mobility_at, labels_at, electrode_at, far, near, own,
-                  source, initial, mobility, labels, electrode, done):
+def parcel_kernel(rates, source, initial, mobility, labels, electrode, far, near, own):
     odd = lax.rem(lax.axis_index("space"), 2)
-    places = (
-        (labels_at, labels), (electrode_at, electrode), (initial_at, initial),
-        (mobility_at, mobility), (source_at, source),
-    )
-    copies = [pltpu.make_async_copy(there, here, done.at[n]) for n, (there, here) in enumerate(places)]
-    for copy in copies:
-        copy.start()
-    for copy in copies:
-        copy.wait()
 
     @pl.loop(0, SLAB)
     def _(p):
@@ -143,9 +133,9 @@
     return here, total
 
 
-def run_sweep(cells, other, weights, kap, open_cell, force, opening):
+def run_sweep(cells, other, weights, kap, open_cell, force, opening, done=0):
     height = cells.shape[2] - 2 * EDGE
-    for number in range(PASSES):
+    for number in range(done, PASSES):
         source, target = (cells, other) if number % 2 == 0 else (other, cells)
 
         @pl.loop(number, 10 - number)
@@ -164,6 +154,22 @@
                     former = here
 
 
+def first_pass(cells, other, weights, kap, open_cell, force):
+    height = cells.shape[2] - 2 * EDGE
+
+    @pl.loop(0, 10)
+    def _(j):
+        for r in range(0, height, 8):
+            rows = pl.ds(r, 8)
+            w = [weights[j, n, rows] for n in range(7)]
+            here, total = gathered(w, cells, 0, j + 1, r)
+            pull = kap[j, rows] * jnp.abs(here)
+            shared = here + total - here * (w[6] + 0.5 * pull)
+            gain = DAMPING * open_cell[j + 1, rows] / (w[6] + pull)
+            for t in range(STEPS):
+                other[t, j + 1, pl.ds(EDGE + r, 8)] = here + gain * (force[t, j, rows] + shared)
+
+
 def halved(read):
     return 0.25 * ((read(0, 0) + read(0, 1)) + (read(1, 0) + read(1, 1)))
 
@@ -178,12 +184,11 @@
 
     @pl.loop(0, 12)
     def _(p):
-        value = begin[p]
-        for t in range(STEPS):
-            cells[t, p, pl.ds(EDGE, height)] = value
+        cells[0, p, pl.ds(EDGE, height)] = begin[p]
 
     clear_edges(other)
-    run_sweep(cells, other, weights, kap, open_cell, force, begin.at[pl.ds(1, 10)])
+    first_pass(cells, other, weights, kap, open_cell, force)
+    run_sweep(cells, other, weights, kap, open_cell, force, begin.at[pl.ds(1, 10)], 1)
     for p in range(SLAB):
         closing[p] = cells[STEPS - 1, 4 + p, pl.ds(EDGE, height)]
     half = height // 2
@@ -245,7 +250,27 @@
         rough[2 + a] = halved(lambda x, y: mob[2 * a + x, pl.ds(EDGE + y, half, stride=2)])
 
 
-def last_kernel(who, fixed, far, near, own, low_far, low_near, arriving, side_far, side_near, correction,
+def join_kernel(who, side_far, side_near, pair, rough, arriving, pairs, roughs, opening):
+    odd = who[0]
+    half = pair.shape[2]
+    for a in range(2):
+        for q in range(2):
+            pairs[q, 2 + a] = pair[q, a]
+    for a in range(10):
+        roughs[2 + a] = rough[a]
+    for p in range(SLAB):
+        opening[3 + p] = arriving[p]
+    for block, up in ((side_far, odd), (side_near, 1 - odd)):
+        for a in range(2):
+            rows = pl.ds(half * a, half)
+            for q in range(2):
+                pairs[q, 4 * up + a] = block[q, rows]
+            roughs[12 * up + a] = block[2, rows]
+        for j in range(SLAB - 1):
+            opening[7 * up + j] = block[3 + j]
+
+
+def last_kernel(who, fixed, far, near, own, low_far, low_near, arriving, correction,
                 out, force, begin, mob, kap, open_cell, weights, cells, other, opening):
     odd, leading = who[0], who[1]
     height = fixed.shape[1]
@@ -265,18 +290,10 @@
                 for t in range(STEPS):
                     cells[t, plane, into] = block[4 * t + p, rows] + change
 
-        def enter(j, value):
-            base = jnp.where(leading == 1, begin[j + 1, rows], value)
+        @pl.loop(0, 10)
+        def _(j):
+            base = jnp.where(leading == 1, begin[j + 1, rows], arriving[j, rows])
             opening[j, rows] = base + open_cell[j + 1, rows] * correction[1, (j + 1) // 2]
-
-        @pl.loop(0, SLAB)
-        def _(p):
-            enter(3 + p, arriving[p, rows])
-
-        @pl.loop(0, SLAB - 1)
-        def _(p):
-            enter(7 * odd + p, side_far[3 + p, rows])
-            enter(7 - 7 * odd + p, side_near[3 + p, rows])
 
     clear_edges(other)
     run_sweep(cells, other, weights, kap, open_cell, force, opening)
@@ -299,7 +316,7 @@
     ]
 
 
-def call(kernel, name, inputs, outputs, scratch):
+def call(kernel, name, inputs, outputs, scratch, grant=28):
     return pl.pallas_call(
         kernel,
         out_shape=[jax.ShapeDtypeStruct(o, jnp.float32) for o in outputs],
@@ -307,7 +324,7 @@
         out_specs=[VMEM] * len(outputs),
         scratch_shapes=scratch,
         name=name,
-        compiler_params=pltpu.CompilerParams(vmem_limit_bytes=28 << 20),
+        compiler_params=pltpu.CompilerParams(vmem_limit_bytes=grant << 20),
     )(*inputs)
 
 
@@ -392,14 +409,12 @@
         & (2 * place + jnp.arange(-reach, 2 + reach) < 2 * lax.axis_size("space"))
     ).astype(jnp.float32)
 
-    there = pl.BlockSpec(memory_space=pltpu.HBM)
     fields = (source, initial, mobility, labels, electrode)
     far, near, fixed = pl.pallas_call(
         parcel_kernel,
         out_shape=[jax.ShapeDtypeStruct((n,) + plane, jnp.float32) for n in (PARCEL, PARCEL, OWN)],
-        in_specs=[SMEM] + [there] * len(fields),
+        in_specs=[SMEM] + [VMEM] * len(fields),
         out_specs=[VMEM] * 3,
-        scratch_shapes=[pltpu.VMEM(v.shape, v.dtype) for v in fields] + [pltpu.SemaphoreType.DMA((len(fields),))],
         name="parcel",
         compiler_params=pltpu.CompilerParams(vmem_limit_bytes=60 << 20),
     )(rates, *fields)
@@ -437,15 +452,18 @@
     pair = pair + Coupling(inner(rough_w, 0, 3), inside(1)).step(jnp.stack([rhs1, rhs2]))
 
     flat = lambda v: v.reshape((-1,) + plane)
-    unflat = lambda v: v.reshape((-1,) + coarse)
     cargo = lambda c, o: jnp.concatenate([flat(pair), flat(c), o], axis=0)
     to_low = cargo(rough_w[8:10], opening[: SLAB - 1])
     to_high = cargo(rough_w[0:2], opening[1:])
     side_far, side_near = traded(*by_side(odd == 1, to_low, to_high))
-    low, high = by_side(odd == 1, unflat(side_far[:3]), unflat(side_near[:3]))
-    pair_of = lambda b: b[:4].reshape(pair.shape)
-    rough_far = jnp.concatenate([low[4:], rough_w, high[4:]], axis=0)
-    pair = jnp.concatenate([pair_of(low), pair, pair_of(high)], axis=1)
+    pair, rough_far, opening = call(
+        join_kernel,
+        "join",
+        (who, side_far, side_near, pair, rough_w, opening),
+        [(2, 6) + coarse, (14,) + coarse, (10,) + plane],
+        [],
+        12,
+    )
     joined = lambda *parts: jnp.concatenate(parts, axis=1)
     count = lax.axis_size("space")
     gap = jnp.zeros_like(pair[:, :2])
@@ -469,7 +487,7 @@
     (density,) = call(
         last_kernel,
         "last",
-        static + states + (opening, side_far, side_near, correction),
+        static + states + (opening, correction),
         [source.shape],
         windows(height, depth)
         + [pltpu.VMEM((STEPS, 12) + tall, jnp.float32)] * 2

time: 143 us -> 138 us (0.965)
  waiting for transfers between devices: 51.4 us -> 58.8 us
  local copies, waits for them, and re-layouts: 12.6 us -> 6.78 us
  starting transfers between devices: 43.2 us -> 38.9 us
    ppermute x11, waiting for transfers between devices: 38.3 us -> 43.5 us  [sent(): return lax.ppermute(value, ('tm', 'space'), pairs)]
    ppermute x11, starting transfers between devices: 31.1 us -> 27.5 us  [sent(): return lax.ppermute(value, ('tm', 'space'), pairs)]
    unnamed x28 -> x12, local copies, waits for them, and re-layouts: 9.48 us -> 6.14 us
    ppermute x4, waiting for transfers between devices: 13.1 us -> 15.2 us  [arrived(): lax.ppermute(value, 'tm', [(k, k + steps) for k in range(times - steps)])]
    slice x4 -> x0, local copies, waits for them, and re-layouts: 1.62 us -> none  [the longest x2 1.6 us: on_device(): rough_far = jnp.concatenate([low[4:], rough_w, high[4:]], axis=0)]
    pallas_call x3 -> x4, Pallas kernels: 24.4 us -> 24.6 us  [call(): pl.pallas_call(kernel, out_shape=[jax.ShapeDtypeStruct(o, jnp.float32) fo...]
  transfers between devices with their start and end apart: 15 -> 15, of which waited for: 10 -> 9; matrix products, arithmetic and copies ran while one was open for 2% -> 1% of each run, Pallas kernels for 0% -> 0%
where the time goes in v5:
time: 138 us
  waiting for transfers between devices  58.8 us (43%)
  starting transfers between devices  38.9 us (28%)
  Pallas kernels  28.4 us (21%)
  local copies, waits for them, and re-layouts  6.78 us (5%)
  other arithmetic  4.2 us (3%)
    ppermute x11, waiting for transfers between devices, sent(): return lax.ppermute(value, ('tm', 'space'), pairs)  43.5 us
    ppermute x11, starting transfers between devices, sent(): return lax.ppermute(value, ('tm', 'space'), pairs)  27.5 us
    pallas_call x4, Pallas kernels, call(): pl.pallas_call(kernel, out_shape=[jax.ShapeDtypeStruct(o, jnp.float32) fo...  24.6 us
    ppermute x4, waiting for transfers between devices, arrived(): lax.ppermute(value, 'tm', [(k, k + steps) for k in range(times - steps)])  15.2 us
    ppermute x4, starting transfers between devices, arrived(): lax.ppermute(value, 'tm', [(k, k + steps) for k in range(times - steps)])  11.4 us
    unnamed x12, local copies, waits for them, and re-layouts  6.14 us
    pallas_call x1, Pallas kernels, on_device(): pl.pallas_call(parcel_kernel, out_shape=[jax.ShapeDtypeStruct((n,) + plan...  3.73 us
  transfers between devices with their start and end apart: 15, of which 9 were waited for; matrix products, arithmetic and copies ran while one was open for 1% of the time, Pallas kernels for 0%

profile of v5, /device:TPU:6, one launch (start us, length us, event | category | flops | bytes accessed | tf_op | source)
XLA Modules:
  0.0 137.6 jit_solution(15555694422872718769)
XLA Ops:
  0.0 3.7 %parcel.1 = (f32[27,96,128]{2,1,0:T(8,128)}, f32[27,96,128]{2,1,0:T(8,128)}, f32[32,96,128]{2,1,0:T(8,128)}) custom-call(f32[4]{0:T(128)} %rates.1, f32[4,4,96,128]{3,2,1,0:T(8,128)} %source.1, f32[4,96,128]{2,1,0:T(8,128)} %initial.1, f32[4,96,128]{2,1,0:T(8,128)} %mobility.1, s32[4,96,128]{2,1,0:T(8,128)} %labels.1, s32[4,96,128]{2,1,0:T(8,128)} %electrode.1), custom_call_target="tpu_custom_call" | custom-call | tf_op jit(solution)/shard_map/parcel/pallas_call | solution.py:413
  3.7 8.0 %collective-permute-start = (f32[27,96,128]{2,1,0:T(8,128)}, f32[27,96,128]{2,1,0:T(8,128)S(1)}, u32[]{:S(2)}, u32[]{:S(2)}) collective-permute-start(f32[27,96,128]{2,1,0:T(8,128)} %get-tuple-element.20), channel_id=1, source_target_pairs={{1,2},{2,1},{3,4},{4,3},{5,6},{6,5},{7,8},{8,7},{9,10},{10,9},{11,... | collective-permute-start | bytes 3981320 | tf_op jit(solution)/shard_map/ppermute | solution.py:382
  12.0 15.5 %collective-permute-done.far = f32[27,96,128]{2,1,0:T(8,128)S(1)} collective-permute-done((f32[27,96,128]{2,1,0:T(8,128)}, f32[27,96,128]{2,1,0:T(8,128)S(1)}, u32[]{:S(2)}, u32[]{:S(2)}) %collective-permute-start) | collective-permute-done | bytes 1327136 | tf_op jit(solution)/shard_map/ppermute | solution.py:382
  28.5 1.4 %copy-done = f32[32,96,128]{2,1,0:T(8,128)S(1)} copy-done((f32[32,96,128]{2,1,0:T(8,128)S(1)}, f32[32,96,128]{2,1,0:T(8,128)}, u32[]{:S(2)}) %copy-start) | copy-done | bytes 1572888
  29.9 1.3 copy-done.3
  31.2 8.3 %first.1 = (f32[17,96,128]{2,1,0:T(8,128)}, f32[17,96,128]{2,1,0:T(8,128)}, f32[4,96,128]{2,1,0:T(8,128)S(1)}) custom-call(s32[4]{0:T(128)S(1)} %pad_add_fusion.who, f32[32,96,128]{2,1,0:T(8,128)S(1)} %copy-done, f32[27,96,128]{2,1,0:T(8,128)S(1)} %collective-permute-done.far, f32[27,96,128]{2,1,0:T(8,128)S(1)} %copy-done.3), custom_call_target="tpu_custom_call" | custom-call | tf_op jit(solution)/shard_map/first/pallas_call | solution.py:320
  39.6 7.2 %collective-permute-start.2 = (f32[17,96,128]{2,1,0:T(8,128)}, f32[17,96,128]{2,1,0:T(8,128)}, u32[]{:S(2)}, u32[]{:S(2)}) collective-permute-start(f32[17,96,128]{2,1,0:T(8,128)} %get-tuple-element.22.own), channel_id=1, source_target_pairs={{1,2},{2,1},{3,4},{4,3},{5,6},{6,5},{7,8},{8,7},{9,10},{10,9},{11,... | collective-permute-start | bytes 2506760 | tf_op jit(solution)/shard_map/ppermute | solution.py:382
  47.0 3.5 %collective-permute-start.4 = (f32[4,96,128]{2,1,0:T(8,128)S(1)}, f32[4,96,128]{2,1,0:T(8,128)S(1)}, u32[]{:S(2)}, u32[]{:S(2)}) collective-permute-start(f32[4,96,128]{2,1,0:T(8,128)S(1)} %get-tuple-element.24), channel_id=1, source_target_pairs={{0,32},{32,64},{64,96},{96,128},{128,160},{160,192},{192,224},{1,3... | collective-permute-start | bytes 589832 | tf_op jit(solution)/shard_map/ppermute | solution.py:397
  50.6 7.7 %collective-permute-done.4.arriving = f32[4,96,128]{2,1,0:T(8,128)S(1)} collective-permute-done((f32[4,96,128]{2,1,0:T(8,128)S(1)}, f32[4,96,128]{2,1,0:T(8,128)S(1)}, u32[]{:S(2)}, u32[]{:S(2)}) %collective-permute-start.4) | collective-permute-done | bytes 196640 | tf_op jit(solution)/shard_map/ppermute | solution.py:397
  58.4 1.3 copy-done.4
  59.7 4.7 %residual.1 = (f32[4,48,128]{2,1,0:T(8,128)S(1)}, f32[4,48,128]{2,1,0:T(8,128)S(1)}, f32[2,4,48,128]{3,2,1,0:T(8,128)S(1)}, f32[2,48,128]{2,1,0:T(8,128)S(1)}, f32[10,48,128]{2,1,0:T(8,128)S(1)}) custom-call(s32[4]{0:T(128)S(1)} %pad_add_fusion.who, f32[32,96,128]{2,1,0:T(8,128)S(1)} %copy-done.1, f32[27,96,128]{2,1,0:T(8,128)S(1)} %collective-permute-done.far, ...), custom_call_target="tpu_custom_call" | custom-call | tf_op jit(solution)/shard_map/residual/pallas_call | solution.py:320
  64.4 3.9 %collective-permute-start.7 = (f32[4,48,128]{2,1,0:T(8,128)S(1)}, f32[4,48,128]{2,1,0:T(8,128)S(1)}, u32[]{:S(2)}, u32[]{:S(2)}) collective-permute-start(f32[4,48,128]{2,1,0:T(8,128)S(1)} %get-tuple-element.29), channel_id=1, source_target_pairs={{0,96},{32,128},{64,160},{96,192},{128,224},{1,97},{33,129},{65,16... | collective-permute-start | bytes 294920 | tf_op jit(solution)/shard_map/ppermute | solution.py:397
  68.3 1.9 %collective-permute-start.6 = (f32[2,4,48,128]{3,2,1,0:T(8,128)S(1)}, f32[2,4,48,128]{3,2,1,0:T(8,128)S(1)}, u32[]{:S(2)}, u32[]{:S(2)}) collective-permute-start(f32[2,4,48,128]{3,2,1,0:T(8,128)S(1)} %get-tuple-element.27), channel_id=1, source_target_pairs={{0,64},{32,96},{64,128},{96,160},{128,192},{160,224},{1,65},{33,97... | collective-permute-start | bytes 589832 | tf_op jit(solution)/shard_map/ppermute | solution.py:397
  70.3 2.1 %collective-permute-start.5 = (f32[4,48,128]{2,1,0:T(8,128)S(1)}, f32[4,48,128]{2,1,0:T(8,128)S(1)}, u32[]{:S(2)}, u32[]{:S(2)}) collective-permute-start(f32[4,48,128]{2,1,0:T(8,128)S(1)} %get-tuple-element.26), channel_id=1, source_target_pairs={{0,32},{32,64},{64,96},{96,128},{128,160},{160,192},{192,224},{1,3... | collective-permute-start | bytes 294920 | tf_op jit(solution)/shard_map/ppermute | solution.py:397
  72.5 7.5 %collective-permute-done.5 = f32[4,48,128]{2,1,0:T(8,128)S(1)} collective-permute-done((f32[4,48,128]{2,1,0:T(8,128)S(1)}, f32[4,48,128]{2,1,0:T(8,128)S(1)}, u32[]{:S(2)}, u32[]{:S(2)}) %collective-permute-start.5) | collective-permute-done | bytes 98336 | tf_op jit(solution)/shard_map/ppermute | solution.py:397
  81.1 5.2 %collective-permute-start.8 = (f32[6,96,128]{2,1,0:T(8,128)}, f32[6,96,128]{2,1,0:T(8,128)}, u32[]{:S(2)}, u32[]{:S(2)}) collective-permute-start(f32[6,96,128]{2,1,0:T(8,128)} %get-tuple-element.48), channel_id=1, source_target_pairs={{1,2},{2,1},{3,4},{4,3},{5,6},{6,5},{7,8},{8,7},{9,10},{10,9},{11,... | collective-permute-start | bytes 884744 | tf_op jit(solution)/shard_map/ppermute | solution.py:382
  86.3 6.7 %collective-permute-done.8.side_far = f32[6,96,128]{2,1,0:T(8,128)} collective-permute-done((f32[6,96,128]{2,1,0:T(8,128)}, f32[6,96,128]{2,1,0:T(8,128)}, u32[]{:S(2)}, u32[]{:S(2)}) %collective-permute-start.8) | collective-permute-done | bytes 294944 | tf_op jit(solution)/shard_map/ppermute | solution.py:382
  94.2 4.0 %collective-permute-start.10 = (f32[2,6,48,128]{3,2,1,0:T(8,128)S(1)}, f32[2,6,48,128]{3,2,1,0:T(8,128)S(1)}, u32[]{:S(2)}, u32[]{:S(2)}) collective-permute-start(f32[2,6,48,128]{3,2,1,0:T(8,128)S(1)} %get-tuple-element.31), channel_id=1, source_target_pairs={{0,64},{1,66},{2,65},{3,68},{4,67},{5,70},{6,69},{7,72},{8,71},{9,... | collective-permute-start | bytes 884744 | tf_op jit(solution)/shard_map/ppermute | solution.py:382
  98.3 9.7 %collective-permute-done.10 = f32[2,6,48,128]{3,2,1,0:T(8,128)S(1)} collective-permute-done((f32[2,6,48,128]{3,2,1,0:T(8,128)S(1)}, f32[2,6,48,128]{3,2,1,0:T(8,128)S(1)}, u32[]{:S(2)}, u32[]{:S(2)}) %collective-permute-start.10) | collective-permute-done | bytes 294944 | tf_op jit(solution)/shard_map/ppermute | solution.py:382
  110.5 1.3 collective-permute-start.12
  111.8 1.3 collective-permute-start.13
  113.1 8.2 %collective-permute-done.13 = f32[2,2,48,128]{3,2,1,0:T(8,128)S(1)} collective-permute-done((f32[2,2,48,128]{3,2,1,0:T(8,128)S(1)}, f32[2,2,48,128]{3,2,1,0:T(8,128)S(1)}, u32[]{:S(2)}, u32[]{:S(2)}) %collective-permute-start.13) | collective-permute-done | bytes 98336 | tf_op jit(solution)/shard_map/ppermute | solution.py:382
  122.8 1.5 %collective-permute-done.14 = f32[2,8,48,128]{3,2,1,0:T(8,128)S(1)} collective-permute-done((f32[2,8,48,128]{3,2,1,0:T(8,128)S(1)}, f32[2,8,48,128]{3,2,1,0:T(8,128)S(1)}, u32[]{:S(2)}, u32[]{:S(2)}) %collective-permute-start.14) | collective-permute-done | bytes 393248 | tf_op jit(solution)/shard_map/ppermute | solution.py:382
  127.2 10.4 %last.1 = f32[4,4,96,128]{3,2,1,0:T(8,128)} custom-call(s32[4]{0:T(128)S(1)} %pad_add_fusion.who, f32[32,96,128]{2,1,0:T(8,128)S(1)} %copy-done.1, f32[27,96,128]{2,1,0:T(8,128)S(1)} %collective-permute-done.far, f32[27,96,128]{2,1,0:T(8,128)S(1)} %copy-done.5, f32[17,96,128]{2,1,0:T(8,128)} %get-tuple-element.22.own, ...), custom_call_target="tpu_custom_call" | custom-call | tf_op jit(solution)/shard_map/last/pallas_call | solution.py:320
  (85 shorter events, 10.6 us)
Async XLA Ops:
  3.7 23.7 %collective-permute-start = (f32[27,96,128]{2,1,0:T(8,128)}, f32[27,96,128]{2,1,0:T(8,128)S(1)}, u32[]{:S(2)}, u32[]{:S(2)}) collective-permute-start(f32[27,96,128]{2,1,0:T(8,128)} %get-tuple-element.20), channel_id=1, source_target_pairs={{1,2},{2,1},{3,4},{4,3},{5,6},{6,5},{7,8},{8,7},{9,10},{10,9},{11,... | collective-permute-start | bytes 3981320 | tf_op jit(solution)/shard_map/ppermute | solution.py:382
  11.8 15.7 %collective-permute-start.1 = (f32[27,96,128]{2,1,0:T(8,128)}, f32[27,96,128]{2,1,0:T(8,128)S(1)}, u32[]{:S(2)}, u32[]{:S(2)}) collective-permute-start(f32[27,96,128]{2,1,0:T(8,128)} %get-tuple-element.21), channel_id=1, source_target_pairs={{0,1},{1,0},{2,3},{3,2},{4,5},{5,4},{6,7},{7,6},{8,9},{9,8},{10,11... | collective-permute-start | bytes 3981320 | tf_op jit(solution)/shard_map/ppermute | solution.py:382
  27.4 1.1 copy-start.2
  28.5 1.4 %copy-start = (f32[32,96,128]{2,1,0:T(8,128)S(1)}, f32[32,96,128]{2,1,0:T(8,128)}, u32[]{:S(2)}) copy-start(f32[32,96,128]{2,1,0:T(8,128)} %get-tuple-element.19.fixed) | copy-start | bytes 4718596
  29.9 1.3 copy-start.3
  31.2 27.1 %copy-start.1 = (f32[32,96,128]{2,1,0:T(8,128)S(1)}, f32[32,96,128]{2,1,0:T(8,128)}, u32[]{:S(2)}) copy-start(f32[32,96,128]{2,1,0:T(8,128)} %get-tuple-element.19.fixed) | copy-start | bytes 4718596
  39.6 18.8 %collective-permute-start.2 = (f32[17,96,128]{2,1,0:T(8,128)}, f32[17,96,128]{2,1,0:T(8,128)}, u32[]{:S(2)}, u32[]{:S(2)}) collective-permute-start(f32[17,96,128]{2,1,0:T(8,128)} %get-tuple-element.22.own), channel_id=1, source_target_pairs={{1,2},{2,1},{3,4},{4,3},{5,6},{6,5},{7,8},{8,7},{9,10},{10,9},{11,... | collective-permute-start | bytes 2506760 | tf_op jit(solution)/shard_map/ppermute | solution.py:382
  46.8 11.5 %collective-permute-start.3 = (f32[17,96,128]{2,1,0:T(8,128)}, f32[17,96,128]{2,1,0:T(8,128)}, u32[]{:S(2)}, u32[]{:S(2)}) collective-permute-start(f32[17,96,128]{2,1,0:T(8,128)} %get-tuple-element.23), channel_id=1, source_target_pairs={{0,1},{1,0},{2,3},{3,2},{4,5},{5,4},{6,7},{7,6},{8,9},{9,8},{10,11... | collective-permute-start | bytes 2506760 | tf_op jit(solution)/shard_map/ppermute | solution.py:382
  47.0 11.3 %collective-permute-start.4 = (f32[4,96,128]{2,1,0:T(8,128)S(1)}, f32[4,96,128]{2,1,0:T(8,128)S(1)}, u32[]{:S(2)}, u32[]{:S(2)}) collective-permute-start(f32[4,96,128]{2,1,0:T(8,128)S(1)} %get-tuple-element.24), channel_id=1, source_target_pairs={{0,32},{32,64},{64,96},{96,128},{128,160},{160,192},{192,224},{1,3... | collective-permute-start | bytes 589832 | tf_op jit(solution)/shard_map/ppermute | solution.py:397
  58.4 1.3 copy-start.4
  64.4 8.1 %collective-permute-start.7 = (f32[4,48,128]{2,1,0:T(8,128)S(1)}, f32[4,48,128]{2,1,0:T(8,128)S(1)}, u32[]{:S(2)}, u32[]{:S(2)}) collective-permute-start(f32[4,48,128]{2,1,0:T(8,128)S(1)} %get-tuple-element.29), channel_id=1, source_target_pairs={{0,96},{32,128},{64,160},{96,192},{128,224},{1,97},{33,129},{65,16... | collective-permute-start | bytes 294920 | tf_op jit(solution)/shard_map/ppermute | solution.py:397
  68.3 11.7 %collective-permute-start.6 = (f32[2,4,48,128]{3,2,1,0:T(8,128)S(1)}, f32[2,4,48,128]{3,2,1,0:T(8,128)S(1)}, u32[]{:S(2)}, u32[]{:S(2)}) collective-permute-start(f32[2,4,48,128]{3,2,1,0:T(8,128)S(1)} %get-tuple-element.27), channel_id=1, source_target_pairs={{0,64},{32,96},{64,128},{96,160},{128,192},{160,224},{1,65},{33,97... | collective-permute-start | bytes 589832 | tf_op jit(solution)/shard_map/ppermute | solution.py:397
  70.3 9.8 %collective-permute-start.5 = (f32[4,48,128]{2,1,0:T(8,128)S(1)}, f32[4,48,128]{2,1,0:T(8,128)S(1)}, u32[]{:S(2)}, u32[]{:S(2)}) collective-permute-start(f32[4,48,128]{2,1,0:T(8,128)S(1)} %get-tuple-element.26), channel_id=1, source_target_pairs={{0,32},{32,64},{64,96},{96,128},{128,160},{160,192},{192,224},{1,3... | collective-permute-start | bytes 294920 | tf_op jit(solution)/shard_map/ppermute | solution.py:397
  81.1 12.0 %collective-permute-start.8 = (f32[6,96,128]{2,1,0:T(8,128)}, f32[6,96,128]{2,1,0:T(8,128)}, u32[]{:S(2)}, u32[]{:S(2)}) collective-permute-start(f32[6,96,128]{2,1,0:T(8,128)} %get-tuple-element.48), channel_id=1, source_target_pairs={{1,2},{2,1},{3,4},{4,3},{5,6},{6,5},{7,8},{8,7},{9,10},{10,9},{11,... | collective-permute-start | bytes 884744 | tf_op jit(solution)/shard_map/ppermute | solution.py:382
  86.2 6.8 %collective-permute-start.9 = (f32[6,96,128]{2,1,0:T(8,128)}, f32[6,96,128]{2,1,0:T(8,128)}, u32[]{:S(2)}, u32[]{:S(2)}) collective-permute-start(f32[6,96,128]{2,1,0:T(8,128)} %get-tuple-element.47), channel_id=1, source_target_pairs={{0,1},{1,0},{2,3},{3,2},{4,5},{5,4},{6,7},{7,6},{8,9},{9,8},{10,11... | collective-permute-start | bytes 884744 | tf_op jit(solution)/shard_map/ppermute | solution.py:382
  94.2 13.8 %collective-permute-start.10 = (f32[2,6,48,128]{3,2,1,0:T(8,128)S(1)}, f32[2,6,48,128]{3,2,1,0:T(8,128)S(1)}, u32[]{:S(2)}, u32[]{:S(2)}) collective-permute-start(f32[2,6,48,128]{3,2,1,0:T(8,128)S(1)} %get-tuple-element.31), channel_id=1, source_target_pairs={{0,64},{1,66},{2,65},{3,68},{4,67},{5,70},{6,69},{7,72},{8,71},{9,... | collective-permute-start | bytes 884744 | tf_op jit(solution)/shard_map/ppermute | solution.py:382
  108.1 1.7 %collective-permute-start.11 = (f32[2,6,48,128]{3,2,1,0:T(8,128)S(1)}, f32[2,6,48,128]{3,2,1,0:T(8,128)S(1)}, u32[]{:S(2)}, u32[]{:S(2)}) collective-permute-start(f32[2,6,48,128]{3,2,1,0:T(8,128)S(1)} %pad_select_fusion), channel_id=1, source_target_pairs={{0,1},{1,0},{2,3},{3,2},{4,5},{5,4},{6,7},{7,6},{8,9},{9,8},{10,11... | collective-permute-start | bytes 884744 | tf_op jit(solution)/shard_map/ppermute | solution.py:382
  110.5 11.9 %collective-permute-start.12 = (f32[2,6,48,128]{3,2,1,0:T(8,128)S(1)}, f32[2,6,48,128]{3,2,1,0:T(8,128)S(1)}, u32[]{:S(2)}, u32[]{:S(2)}) collective-permute-start(f32[2,6,48,128]{3,2,1,0:T(8,128)S(1)} %fusion.59), channel_id=1, source_target_pairs={{0,130},{2,132},{3,129},{4,134},{5,131},{6,136},{7,133},{8,138},{9... | collective-permute-start | bytes 884744 | tf_op jit(solution)/shard_map/ppermute | solution.py:382
  111.8 9.5 %collective-permute-start.13 = (f32[2,2,48,128]{3,2,1,0:T(8,128)S(1)}, f32[2,2,48,128]{3,2,1,0:T(8,128)S(1)}, u32[]{:S(2)}, u32[]{:S(2)}) collective-permute-start(f32[2,2,48,128]{3,2,1,0:T(8,128)S(1)} %slice.465), channel_id=1, source_target_pairs={{0,128},{1,129},{2,130},{3,131},{4,132},{5,133},{6,134},{7,135},{8... | collective-permute-start | bytes 294920 | tf_op jit(solution)/shard_map/ppermute | solution.py:382
  122.5 1.8 %collective-permute-start.14 = (f32[2,8,48,128]{3,2,1,0:T(8,128)S(1)}, f32[2,8,48,128]{3,2,1,0:T(8,128)S(1)}, u32[]{:S(2)}, u32[]{:S(2)}) collective-permute-start(f32[2,8,48,128]{3,2,1,0:T(8,128)S(1)} %pad_maximum_fusion.2), channel_id=1, source_target_pairs={{0,1},{1,0},{2,3},{3,2},{4,5},{5,4},{6,7},{7,6},{8,9},{9,8},{10,11... | collective-permute-start | bytes 1179656 | tf_op jit(solution)/shard_map/ppermute | solution.py:382
  125.8 1.3 copy-start.5

commit v6 on v5

--- a/solution.py
+++ b/solution.py
@@ -15,6 +15,7 @@
 
 VMEM = pl.BlockSpec(memory_space=pltpu.VMEM)
 SMEM = pl.BlockSpec(memory_space=pltpu.SMEM)
+HBM = pl.BlockSpec(memory_space=pltpu.HBM)
 
 P_INIT, P_MOB, P_FREE, P_KAP, PARCEL = 12, 16, 20, 24, 27
 O_INIT, O_MOB, O_FREE, O_KAP, OWN = 16, 20, 24, 28, 32
@@ -55,35 +56,39 @@
                 out[3 * t + j] = own[SLAB * t + begin + j]
 
 
-def load_static(odd, fixed, far, near, force, begin, mob, kap, open_cell):
-    rows = pl.ds(EDGE, fixed.shape[1])
-
-    @pl.loop(0, SLAB)
-    def _(p):
-        begin[4 + p] = fixed[O_INIT + p]
-        mob[4 + p, rows] = fixed[O_MOB + p]
-        open_cell[4 + p] = fixed[O_FREE + p]
-        kap[3 + p] = fixed[O_KAP + p]
-        for t in range(STEPS):
-            force[t, 3 + p] = fixed[SLAB * t + p]
-        for block, wide in ((far, 8 * odd), (near, 8 - 8 * odd)):
-            begin[wide + p] = block[P_INIT + p]
-            mob[wide + p, rows] = block[P_MOB + p]
-            open_cell[wide + p] = block[P_FREE + p]
-
-    @pl.loop(0, SLAB - 1)
-    def _(p):
-        for block, wide in ((far, 7 * odd), (near, 7 - 7 * odd)):
-            kap[wide + p] = block[P_KAP + p]
-            for t in range(STEPS):
-                force[t, wide + p] = block[3 * t + p]
-
+def start_static(odd, fixed, far, near, force, begin, mob, kap, open_cell, done):
+    height = fixed.shape[1]
     zero = jnp.zeros((EDGE, mob.shape[2]), jnp.float32)
 
     @pl.loop(0, mob.shape[0])
     def _(p):
         mob[p, pl.ds(0, EDGE)] = zero
-        mob[p, pl.ds(mob.shape[1] - EDGE, EDGE)] = zero
+        mob[p, pl.ds(EDGE + height, EDGE)] = zero
+
+    moves = []
+    own_at = (O_INIT, O_MOB, O_FREE, O_KAP)
+    side_at = (P_INIT, P_MOB, P_FREE, P_KAP)
+    for block, count, (i, m, o, k), deep, shallow in (
+        (fixed, SLAB, own_at, 4, 3),
+        (far, SLAB - 1, side_at, 8 * odd, 7 * odd),
+        (near, SLAB - 1, side_at, 8 - 8 * odd, 7 - 7 * odd),
+    ):
+        window = pl.ds(deep, SLAB)
+        moves.append((block.at[pl.ds(m, SLAB)], mob.at[window, pl.ds(EDGE, height)]))
+        moves.append((block.at[pl.ds(i, SLAB)], begin.at[window]))
+        moves.append((block.at[pl.ds(o, SLAB)], open_cell.at[window]))
+        moves.append((block.at[pl.ds(k, count)], kap.at[pl.ds(shallow, count)]))
+        for t in range(STEPS):
+            moves.append((block.at[pl.ds(count * t, count)], force.at[t, pl.ds(shallow, count)]))
+    copies = [pltpu.make_async_copy(here, there, done.at[n]) for n, (here, there) in enumerate(moves)]
+    for copy in copies:
+        copy.start()
+    return copies
+
+
+def finish(copies):
+    for copy in copies:
+        copy.wait()
 
 
 def make_weights(mob, weights, first, last):
@@ -175,18 +180,19 @@
 
 
 def first_kernel(who, fixed, far, near, to_far, to_near, closing,
-                 force, begin, mob, kap, open_cell, weights, cells, other, rough):
+                 force, begin, mob, kap, open_cell, weights, cells, other, rough, done):
     odd = who[0]
     height = fixed.shape[1]
-    load_static(odd, fixed, far, near, force, begin, mob, kap, open_cell)
+    copies = start_static(odd, fixed, far, near, force, begin, mob, kap, open_cell, done)
+    clear_edges(cells)
+    clear_edges(other)
+    finish(copies)
     make_weights(mob, weights, 0, 10)
-    clear_edges(cells)
 
     @pl.loop(0, 12)
     def _(p):
         cells[0, p, pl.ds(EDGE, height)] = begin[p]
 
-    clear_edges(other)
     first_pass(cells, other, weights, kap, open_cell, force)
     run_sweep(cells, other, weights, kap, open_cell, force, begin.at[pl.ds(1, 10)], 1)
     for p in range(SLAB):
@@ -203,12 +209,11 @@
 
 
 def residual_kernel(who, fixed, far, near, own, low_far, low_near, arriving,
-                    base, closing, both, rhs, rough, force, begin, mob, kap, open_cell, weights, cells, residues):
+                    base, closing, both, rhs, rough, force, begin, mob, kap, open_cell, weights, cells, residues, done):
     odd, leading, place, count = who[0], who[1], who[2], who[3]
     height = fixed.shape[1]
     half = height // 2
-    load_static(odd, fixed, far, near, force, begin, mob, kap, open_cell)
-    make_weights(mob, weights, 1, 9)
+    copies = start_static(odd, fixed, far, near, force, begin, mob, kap, open_cell, done)
     clear_edges(cells)
     rows = pl.ds(EDGE, height)
     for t in range(STEPS):
@@ -218,6 +223,9 @@
             cells[t, 4 + p, rows] = own[4 * t + p]
             cells[t, 8 * odd + p, rows] = low_far[4 * t + p]
             cells[t, 8 - 8 * odd + p, rows] = low_near[4 * t + p]
+
+    finish(copies)
+    make_weights(mob, weights, 1, 9)
 
     @pl.loop(1, 9)
     def _(j):
@@ -271,13 +279,15 @@
 
 
 def last_kernel(who, fixed, far, near, own, low_far, low_near, arriving, correction,
-                out, force, begin, mob, kap, open_cell, weights, cells, other, opening):
+                out, force, begin, mob, kap, open_cell, weights, cells, other, opening, done):
     odd, leading = who[0], who[1]
     height = fixed.shape[1]
     half = height // 2
-    load_static(odd, fixed, far, near, force, begin, mob, kap, open_cell)
+    copies = start_static(odd, fixed, far, near, force, begin, mob, kap, open_cell, done)
+    clear_edges(cells)
+    clear_edges(other)
+    finish(copies)
     make_weights(mob, weights, 0, 10)
-    clear_edges(cells)
     for y in range(2):
         rows = pl.ds(y, half, stride=2)
         into = pl.ds(EDGE + y, half, stride=2)
@@ -295,7 +305,6 @@
             base = jnp.where(leading == 1, begin[j + 1, rows], arriving[j, rows])
             opening[j, rows] = base + open_cell[j + 1, rows] * correction[1, (j + 1) // 2]
 
-    clear_edges(other)
     run_sweep(cells, other, weights, kap, open_cell, force, opening)
     for t in range(STEPS):
         for p in range(SLAB):
@@ -316,13 +325,13 @@
     ]
 
 
-def call(kernel, name, inputs, outputs, scratch, grant=28):
+def call(kernel, name, inputs, outputs, scratch, grant=24, held=3):
     return pl.pallas_call(
         kernel,
         out_shape=[jax.ShapeDtypeStruct(o, jnp.float32) for o in outputs],
-        in_specs=[SMEM] + [VMEM] * (len(inputs) - 1),
+        in_specs=[SMEM] + [HBM] * held + [VMEM] * (len(inputs) - 1 - held),
         out_specs=[VMEM] * len(outputs),
-        scratch_shapes=scratch,
+        scratch_shapes=scratch + [pltpu.SemaphoreType.DMA((24,))] * (held > 0),
         name=name,
         compiler_params=pltpu.CompilerParams(vmem_limit_bytes=grant << 20),
     )(*inputs)
@@ -419,6 +428,7 @@
         compiler_params=pltpu.CompilerParams(vmem_limit_bytes=60 << 20),
     )(rates, *fields)
     far, near = traded(far, near)
+    fixed, far, near = (pltpu.with_memory_space_constraint(v, pltpu.HBM) for v in (fixed, far, near))
     static = (who, fixed, far, near)
     tall = (height + 2 * EDGE, depth)
 
@@ -463,6 +473,7 @@
         [(2, 6) + coarse, (14,) + coarse, (10,) + plane],
         [],
         12,
+        0,
     )
     joined = lambda *parts: jnp.concatenate(parts, axis=1)
     count = lax.axis_size("space")

time: 138 us -> 136 us (0.986)
  local copies, waits for them, and re-layouts: 6.78 us -> 1.7 us
  Pallas kernels: 28.4 us -> 31.9 us
    unnamed x12 -> x2, local copies, waits for them, and re-layouts: 6.14 us -> 1.07 us
    pallas_call x4, Pallas kernels: 24.6 us -> 28.1 us  [call(): pl.pallas_call(kernel, out_shape=[jax.ShapeDtypeStruct(o, jnp.float32) fo...]
where the time goes in v6:
time: 136 us
  waiting for transfers between devices  59.3 us (44%)
  starting transfers between devices  38.2 us (28%)
  Pallas kernels  31.9 us (23%)
  other arithmetic  4.1 us (3%)
  local copies, waits for them, and re-layouts  1.7 us (1%)
    ppermute x11, waiting for transfers between devices, sent(): return lax.ppermute(value, ('tm', 'space'), pairs)  43.9 us
    pallas_call x4, Pallas kernels, call(): pl.pallas_call(kernel, out_shape=[jax.ShapeDtypeStruct(o, jnp.float32) fo...  28.1 us
    ppermute x11, starting transfers between devices, sent(): return lax.ppermute(value, ('tm', 'space'), pairs)  27.1 us
    ppermute x4, waiting for transfers between devices, arrived(): lax.ppermute(value, 'tm', [(k, k + steps) for k in range(times - steps)])  15.4 us
    ppermute x4, starting transfers between devices, arrived(): lax.ppermute(value, 'tm', [(k, k + steps) for k in range(times - steps)])  11.1 us
    pallas_call x1, Pallas kernels, on_device(): pl.pallas_call(parcel_kernel, out_shape=[jax.ShapeDtypeStruct((n,) + plan...  3.76 us
  transfers between devices with their start and end apart: 15, of which 9 were waited for; matrix products, arithmetic and copies ran while one was open for 1% of the time, Pallas kernels for 0%

profile of v6, /device:TPU:6, one launch (start us, length us, event | category | flops | bytes accessed | tf_op | source)
XLA Modules:
  0.0 135.7 jit_solution(16052579606765051708)
XLA Ops:
  0.0 3.8 %parcel.1 = (f32[27,96,128]{2,1,0:T(8,128)}, f32[27,96,128]{2,1,0:T(8,128)}, f32[32,96,128]{2,1,0:T(8,128)}) custom-call(f32[4]{0:T(128)} %rates.1, f32[4,4,96,128]{3,2,1,0:T(8,128)} %source.1, f32[4,96,128]{2,1,0:T(8,128)} %initial.1, f32[4,96,128]{2,1,0:T(8,128)} %mobility.1, s32[4,96,128]{2,1,0:T(8,128)} %labels.1, s32[4,96,128]{2,1,0:T(8,128)} %electrode.1), custom_call_target="tpu_custom_call" | custom-call | tf_op jit(solution)/shard_map/parcel/pallas_call | solution.py:422
  3.8 8.0 %collective-permute-start = (f32[27,96,128]{2,1,0:T(8,128)}, f32[27,96,128]{2,1,0:T(8,128)S(1)}, u32[]{:S(2)}, u32[]{:S(2)}) collective-permute-start(f32[27,96,128]{2,1,0:T(8,128)} %get-tuple-element.20), channel_id=1, source_target_pairs={{1,2},{2,1},{3,4},{4,3},{5,6},{6,5},{7,8},{8,7},{9,10},{10,9},{11,... | collective-permute-start | bytes 3981320 | tf_op jit(solution)/shard_map/ppermute | solution.py:391
  12.0 15.5 %collective-permute-done.far = f32[27,96,128]{2,1,0:T(8,128)S(1)} collective-permute-done((f32[27,96,128]{2,1,0:T(8,128)}, f32[27,96,128]{2,1,0:T(8,128)S(1)}, u32[]{:S(2)}, u32[]{:S(2)}) %collective-permute-start) | collective-permute-done | bytes 1327136 | tf_op jit(solution)/shard_map/ppermute | solution.py:391
  27.5 1.1 copy-done
  28.5 10.1 %first.1 = (f32[17,96,128]{2,1,0:T(8,128)S(1)}, f32[17,96,128]{2,1,0:T(8,128)}, f32[4,96,128]{2,1,0:T(8,128)S(1)}) custom-call(s32[4]{0:T(128)S(1)} %pad_add_fusion.who, f32[32,96,128]{2,1,0:T(8,128)} %get-tuple-element.19.fixed, f32[27,96,128]{2,1,0:T(8,128)} %copy-done, f32[27,96,128]{2,1,0:T(8,128)} %collective-permute-done.1.near), custom_call_target="tpu_custom_call" | custom-call | tf_op jit(solution)/shard_map/first/pallas_call | solution.py:329
  38.7 7.3 %collective-permute-start.2 = (f32[17,96,128]{2,1,0:T(8,128)S(1)}, f32[17,96,128]{2,1,0:T(8,128)S(1)}, u32[]{:S(2)}, u32[]{:S(2)}) collective-permute-start(f32[17,96,128]{2,1,0:T(8,128)S(1)} %get-tuple-element.22.own), channel_id=1, source_target_pairs={{1,2},{2,1},{3,4},{4,3},{5,6},{6,5},{7,8},{8,7},{9,10},{10,9},{11,... | collective-permute-start | bytes 2506760 | tf_op jit(solution)/shard_map/ppermute | solution.py:391
  46.1 3.5 %collective-permute-start.4 = (f32[4,96,128]{2,1,0:T(8,128)S(1)}, f32[4,96,128]{2,1,0:T(8,128)S(1)}, u32[]{:S(2)}, u32[]{:S(2)}) collective-permute-start(f32[4,96,128]{2,1,0:T(8,128)S(1)} %get-tuple-element.24), channel_id=1, source_target_pairs={{0,32},{32,64},{64,96},{96,128},{128,160},{160,192},{192,224},{1,3... | collective-permute-start | bytes 589832 | tf_op jit(solution)/shard_map/ppermute | solution.py:406
  49.7 7.7 %collective-permute-done.4.arriving = f32[4,96,128]{2,1,0:T(8,128)S(1)} collective-permute-done((f32[4,96,128]{2,1,0:T(8,128)S(1)}, f32[4,96,128]{2,1,0:T(8,128)S(1)}, u32[]{:S(2)}, u32[]{:S(2)}) %collective-permute-start.4) | collective-permute-done | bytes 196640 | tf_op jit(solution)/shard_map/ppermute | solution.py:406
  57.4 5.5 %residual.1 = (f32[4,48,128]{2,1,0:T(8,128)S(1)}, f32[4,48,128]{2,1,0:T(8,128)S(1)}, f32[2,4,48,128]{3,2,1,0:T(8,128)S(1)}, f32[2,48,128]{2,1,0:T(8,128)S(1)}, f32[10,48,128]{2,1,0:T(8,128)S(1)}) custom-call(s32[4]{0:T(128)S(1)} %pad_add_fusion.who, f32[32,96,128]{2,1,0:T(8,128)} %get-tuple-element.19.fixed, f32[27,96,128]{2,1,0:T(8,128)} %copy-done, ...), custom_call_target="tpu_custom_call" | custom-call | tf_op jit(solution)/shard_map/residual/pallas_call | solution.py:329
  63.0 3.6 %collective-permute-start.7 = (f32[4,48,128]{2,1,0:T(8,128)S(1)}, f32[4,48,128]{2,1,0:T(8,128)S(1)}, u32[]{:S(2)}, u32[]{:S(2)}) collective-permute-start(f32[4,48,128]{2,1,0:T(8,128)S(1)} %get-tuple-element.29), channel_id=1, source_target_pairs={{0,96},{32,128},{64,160},{96,192},{128,224},{1,97},{33,129},{65,16... | collective-permute-start | bytes 294920 | tf_op jit(solution)/shard_map/ppermute | solution.py:406
  66.6 1.9 %collective-permute-start.6 = (f32[2,4,48,128]{3,2,1,0:T(8,128)S(1)}, f32[2,4,48,128]{3,2,1,0:T(8,128)S(1)}, u32[]{:S(2)}, u32[]{:S(2)}) collective-permute-start(f32[2,4,48,128]{3,2,1,0:T(8,128)S(1)} %get-tuple-element.27), channel_id=1, source_target_pairs={{0,64},{32,96},{64,128},{96,160},{128,192},{160,224},{1,65},{33,97... | collective-permute-start | bytes 589832 | tf_op jit(solution)/shard_map/ppermute | solution.py:406
  68.5 2.1 %collective-permute-start.5 = (f32[4,48,128]{2,1,0:T(8,128)S(1)}, f32[4,48,128]{2,1,0:T(8,128)S(1)}, u32[]{:S(2)}, u32[]{:S(2)}) collective-permute-start(f32[4,48,128]{2,1,0:T(8,128)S(1)} %get-tuple-element.26), channel_id=1, source_target_pairs={{0,32},{32,64},{64,96},{96,128},{128,160},{160,192},{192,224},{1,3... | collective-permute-start | bytes 294920 | tf_op jit(solution)/shard_map/ppermute | solution.py:406
  70.8 7.7 %collective-permute-done.5 = f32[4,48,128]{2,1,0:T(8,128)S(1)} collective-permute-done((f32[4,48,128]{2,1,0:T(8,128)S(1)}, f32[4,48,128]{2,1,0:T(8,128)S(1)}, u32[]{:S(2)}, u32[]{:S(2)}) %collective-permute-start.5) | collective-permute-done | bytes 98336 | tf_op jit(solution)/shard_map/ppermute | solution.py:406
  79.6 4.9 %collective-permute-start.8 = (f32[6,96,128]{2,1,0:T(8,128)}, f32[6,96,128]{2,1,0:T(8,128)S(1)}, u32[]{:S(2)}, u32[]{:S(2)}) collective-permute-start(f32[6,96,128]{2,1,0:T(8,128)} %get-tuple-element.48), channel_id=1, source_target_pairs={{1,2},{2,1},{3,4},{4,3},{5,6},{6,5},{7,8},{8,7},{9,10},{10,9},{11,... | collective-permute-start | bytes 884744 | tf_op jit(solution)/shard_map/ppermute | solution.py:391
  84.6 6.8 %collective-permute-done.8.side_far = f32[6,96,128]{2,1,0:T(8,128)S(1)} collective-permute-done((f32[6,96,128]{2,1,0:T(8,128)}, f32[6,96,128]{2,1,0:T(8,128)S(1)}, u32[]{:S(2)}, u32[]{:S(2)}) %collective-permute-start.8) | collective-permute-done | bytes 294944 | tf_op jit(solution)/shard_map/ppermute | solution.py:391
  91.4 1.0 join.1
  92.5 3.8 %collective-permute-start.10 = (f32[2,6,48,128]{3,2,1,0:T(8,128)S(1)}, f32[2,6,48,128]{3,2,1,0:T(8,128)S(1)}, u32[]{:S(2)}, u32[]{:S(2)}) collective-permute-start(f32[2,6,48,128]{3,2,1,0:T(8,128)S(1)} %get-tuple-element.31), channel_id=1, source_target_pairs={{0,64},{1,66},{2,65},{3,68},{4,67},{5,70},{6,69},{7,72},{8,71},{9,... | collective-permute-start | bytes 884744 | tf_op jit(solution)/shard_map/ppermute | solution.py:391
  96.4 9.9 %collective-permute-done.10 = f32[2,6,48,128]{3,2,1,0:T(8,128)S(1)} collective-permute-done((f32[2,6,48,128]{3,2,1,0:T(8,128)S(1)}, f32[2,6,48,128]{3,2,1,0:T(8,128)S(1)}, u32[]{:S(2)}, u32[]{:S(2)}) %collective-permute-start.10) | collective-permute-done | bytes 294944 | tf_op jit(solution)/shard_map/ppermute | solution.py:391
  108.8 1.3 collective-permute-start.12
  110.1 1.3 collective-permute-start.13
  111.4 8.2 %collective-permute-done.13 = f32[2,2,48,128]{3,2,1,0:T(8,128)S(1)} collective-permute-done((f32[2,2,48,128]{3,2,1,0:T(8,128)S(1)}, f32[2,2,48,128]{3,2,1,0:T(8,128)S(1)}, u32[]{:S(2)}, u32[]{:S(2)}) %collective-permute-start.13) | collective-permute-done | bytes 98336 | tf_op jit(solution)/shard_map/ppermute | solution.py:391
  119.5 1.1 collective-permute-done.12
  121.0 1.5 %collective-permute-done.14 = f32[2,8,48,128]{3,2,1,0:T(8,128)S(1)} collective-permute-done((f32[2,8,48,128]{3,2,1,0:T(8,128)S(1)}, f32[2,8,48,128]{3,2,1,0:T(8,128)S(1)}, u32[]{:S(2)}, u32[]{:S(2)}) %collective-permute-start.14) | collective-permute-done | bytes 393248 | tf_op jit(solution)/shard_map/ppermute | solution.py:391
  124.3 11.4 %last.1 = f32[4,4,96,128]{3,2,1,0:T(8,128)} custom-call(s32[4]{0:T(128)S(1)} %pad_add_fusion.who, f32[32,96,128]{2,1,0:T(8,128)} %get-tuple-element.19.fixed, f32[27,96,128]{2,1,0:T(8,128)} %copy-done, f32[27,96,128]{2,1,0:T(8,128)} %collective-permute-done.1.near, f32[17,96,128]{2,1,0:T(8,128)S(1)} %get-tuple-element.22.own, ...), custom_call_target="tpu_custom_call" | custom-call | tf_op jit(solution)/shard_map/last/pallas_call | solution.py:329
  (75 shorter events, 6.1 us)
Async XLA Ops:
  3.8 23.7 %collective-permute-start = (f32[27,96,128]{2,1,0:T(8,128)}, f32[27,96,128]{2,1,0:T(8,128)S(1)}, u32[]{:S(2)}, u32[]{:S(2)}) collective-permute-start(f32[27,96,128]{2,1,0:T(8,128)} %get-tuple-element.20), channel_id=1, source_target_pairs={{1,2},{2,1},{3,4},{4,3},{5,6},{6,5},{7,8},{8,7},{9,10},{10,9},{11,... | collective-permute-start | bytes 3981320 | tf_op jit(solution)/shard_map/ppermute | solution.py:391
  11.8 15.7 %collective-permute-start.1 = (f32[27,96,128]{2,1,0:T(8,128)}, f32[27,96,128]{2,1,0:T(8,128)}, u32[]{:S(2)}, u32[]{:S(2)}) collective-permute-start(f32[27,96,128]{2,1,0:T(8,128)} %get-tuple-element.21), channel_id=1, source_target_pairs={{0,1},{1,0},{2,3},{3,2},{4,5},{5,4},{6,7},{7,6},{8,9},{9,8},{10,11... | collective-permute-start | bytes 3981320 | tf_op jit(solution)/shard_map/ppermute | solution.py:391
  27.5 1.1 copy-start
  38.7 18.8 %collective-permute-start.2 = (f32[17,96,128]{2,1,0:T(8,128)S(1)}, f32[17,96,128]{2,1,0:T(8,128)S(1)}, u32[]{:S(2)}, u32[]{:S(2)}) collective-permute-start(f32[17,96,128]{2,1,0:T(8,128)S(1)} %get-tuple-element.22.own), channel_id=1, source_target_pairs={{1,2},{2,1},{3,4},{4,3},{5,6},{6,5},{7,8},{8,7},{9,10},{10,9},{11,... | collective-permute-start | bytes 2506760 | tf_op jit(solution)/shard_map/ppermute | solution.py:391
  45.9 11.5 %collective-permute-start.3 = (f32[17,96,128]{2,1,0:T(8,128)}, f32[17,96,128]{2,1,0:T(8,128)S(1)}, u32[]{:S(2)}, u32[]{:S(2)}) collective-permute-start(f32[17,96,128]{2,1,0:T(8,128)} %get-tuple-element.23), channel_id=1, source_target_pairs={{0,1},{1,0},{2,3},{3,2},{4,5},{5,4},{6,7},{7,6},{8,9},{9,8},{10,11... | collective-permute-start | bytes 2506760 | tf_op jit(solution)/shard_map/ppermute | solution.py:391
  46.1 11.3 %collective-permute-start.4 = (f32[4,96,128]{2,1,0:T(8,128)S(1)}, f32[4,96,128]{2,1,0:T(8,128)S(1)}, u32[]{:S(2)}, u32[]{:S(2)}) collective-permute-start(f32[4,96,128]{2,1,0:T(8,128)S(1)} %get-tuple-element.24), channel_id=1, source_target_pairs={{0,32},{32,64},{64,96},{96,128},{128,160},{160,192},{192,224},{1,3... | collective-permute-start | bytes 589832 | tf_op jit(solution)/shard_map/ppermute | solution.py:406
  63.0 7.8 %collective-permute-start.7 = (f32[4,48,128]{2,1,0:T(8,128)S(1)}, f32[4,48,128]{2,1,0:T(8,128)S(1)}, u32[]{:S(2)}, u32[]{:S(2)}) collective-permute-start(f32[4,48,128]{2,1,0:T(8,128)S(1)} %get-tuple-element.29), channel_id=1, source_target_pairs={{0,96},{32,128},{64,160},{96,192},{128,224},{1,97},{33,129},{65,16... | collective-permute-start | bytes 294920 | tf_op jit(solution)/shard_map/ppermute | solution.py:406
  66.6 11.9 %collective-permute-start.6 = (f32[2,4,48,128]{3,2,1,0:T(8,128)S(1)}, f32[2,4,48,128]{3,2,1,0:T(8,128)S(1)}, u32[]{:S(2)}, u32[]{:S(2)}) collective-permute-start(f32[2,4,48,128]{3,2,1,0:T(8,128)S(1)} %get-tuple-element.27), channel_id=1, source_target_pairs={{0,64},{32,96},{64,128},{96,160},{128,192},{160,224},{1,65},{33,97... | collective-permute-start | bytes 589832 | tf_op jit(solution)/shard_map/ppermute | solution.py:406
  68.5 10.0 %collective-permute-start.5 = (f32[4,48,128]{2,1,0:T(8,128)S(1)}, f32[4,48,128]{2,1,0:T(8,128)S(1)}, u32[]{:S(2)}, u32[]{:S(2)}) collective-permute-start(f32[4,48,128]{2,1,0:T(8,128)S(1)} %get-tuple-element.26), channel_id=1, source_target_pairs={{0,32},{32,64},{64,96},{96,128},{128,160},{160,192},{192,224},{1,3... | collective-permute-start | bytes 294920 | tf_op jit(solution)/shard_map/ppermute | solution.py:406
  79.6 11.9 %collective-permute-start.8 = (f32[6,96,128]{2,1,0:T(8,128)}, f32[6,96,128]{2,1,0:T(8,128)S(1)}, u32[]{:S(2)}, u32[]{:S(2)}) collective-permute-start(f32[6,96,128]{2,1,0:T(8,128)} %get-tuple-element.48), channel_id=1, source_target_pairs={{1,2},{2,1},{3,4},{4,3},{5,6},{6,5},{7,8},{8,7},{9,10},{10,9},{11,... | collective-permute-start | bytes 884744 | tf_op jit(solution)/shard_map/ppermute | solution.py:391
  84.5 6.9 %collective-permute-start.9 = (f32[6,96,128]{2,1,0:T(8,128)}, f32[6,96,128]{2,1,0:T(8,128)}, u32[]{:S(2)}, u32[]{:S(2)}) collective-permute-start(f32[6,96,128]{2,1,0:T(8,128)} %get-tuple-element.47), channel_id=1, source_target_pairs={{0,1},{1,0},{2,3},{3,2},{4,5},{5,4},{6,7},{7,6},{8,9},{9,8},{10,11... | collective-permute-start | bytes 884744 | tf_op jit(solution)/shard_map/ppermute | solution.py:391
  92.5 13.8 %collective-permute-start.10 = (f32[2,6,48,128]{3,2,1,0:T(8,128)S(1)}, f32[2,6,48,128]{3,2,1,0:T(8,128)S(1)}, u32[]{:S(2)}, u32[]{:S(2)}) collective-permute-start(f32[2,6,48,128]{3,2,1,0:T(8,128)S(1)} %get-tuple-element.31), channel_id=1, source_target_pairs={{0,64},{1,66},{2,65},{3,68},{4,67},{5,70},{6,69},{7,72},{8,71},{9,... | collective-permute-start | bytes 884744 | tf_op jit(solution)/shard_map/ppermute | solution.py:391
  106.4 1.7 %collective-permute-start.11 = (f32[2,6,48,128]{3,2,1,0:T(8,128)S(1)}, f32[2,6,48,128]{3,2,1,0:T(8,128)S(1)}, u32[]{:S(2)}, u32[]{:S(2)}) collective-permute-start(f32[2,6,48,128]{3,2,1,0:T(8,128)S(1)} %pad_select_fusion), channel_id=1, source_target_pairs={{0,1},{1,0},{2,3},{3,2},{4,5},{5,4},{6,7},{7,6},{8,9},{9,8},{10,11... | collective-permute-start | bytes 884744 | tf_op jit(solution)/shard_map/ppermute | solution.py:391
  108.8 11.9 %collective-permute-start.12 = (f32[2,6,48,128]{3,2,1,0:T(8,128)S(1)}, f32[2,6,48,128]{3,2,1,0:T(8,128)S(1)}, u32[]{:S(2)}, u32[]{:S(2)}) collective-permute-start(f32[2,6,48,128]{3,2,1,0:T(8,128)S(1)} %fusion.59), channel_id=1, source_target_pairs={{0,130},{2,132},{3,129},{4,134},{5,131},{6,136},{7,133},{8,138},{9... | collective-permute-start | bytes 884744 | tf_op jit(solution)/shard_map/ppermute | solution.py:391
  110.1 9.5 %collective-permute-start.13 = (f32[2,2,48,128]{3,2,1,0:T(8,128)S(1)}, f32[2,2,48,128]{3,2,1,0:T(8,128)S(1)}, u32[]{:S(2)}, u32[]{:S(2)}) collective-permute-start(f32[2,2,48,128]{3,2,1,0:T(8,128)S(1)} %slice.465), channel_id=1, source_target_pairs={{0,128},{1,129},{2,130},{3,131},{4,132},{5,133},{6,134},{7,135},{8... | collective-permute-start | bytes 294920 | tf_op jit(solution)/shard_map/ppermute | solution.py:391
  120.7 1.8 %collective-permute-start.14 = (f32[2,8,48,128]{3,2,1,0:T(8,128)S(1)}, f32[2,8,48,128]{3,2,1,0:T(8,128)S(1)}, u32[]{:S(2)}, u32[]{:S(2)}) collective-permute-start(f32[2,8,48,128]{3,2,1,0:T(8,128)S(1)} %pad_maximum_fusion.2), channel_id=1, source_target_pairs={{0,1},{1,0},{2,3},{3,2},{4,5},{5,4},{6,7},{7,6},{8,9},{9,8},{10,11... | collective-permute-start | bytes 1179656 | tf_op jit(solution)/shard_map/ppermute | solution.py:391

commit v7 on v6

--- a/solution.py
+++ b/solution.py
@@ -16,6 +16,7 @@
 VMEM = pl.BlockSpec(memory_space=pltpu.VMEM)
 SMEM = pl.BlockSpec(memory_space=pltpu.SMEM)
 HBM = pl.BlockSpec(memory_space=pltpu.HBM)
+ANY = pl.BlockSpec(memory_space=pl.ANY)
 
 P_INIT, P_MOB, P_FREE, P_KAP, PARCEL = 12, 16, 20, 24, 27
 O_INIT, O_MOB, O_FREE, O_KAP, OWN = 16, 20, 24, 28, 32
@@ -329,7 +330,7 @@
     return pl.pallas_call(
         kernel,
         out_shape=[jax.ShapeDtypeStruct(o, jnp.float32) for o in outputs],
-        in_specs=[SMEM] + [HBM] * held + [VMEM] * (len(inputs) - 1 - held),
+        in_specs=[SMEM] + [HBM, ANY, ANY][:held] + [VMEM] * (len(inputs) - 1 - held),
         out_specs=[VMEM] * len(outputs),
         scratch_shapes=scratch + [pltpu.SemaphoreType.DMA((24,))] * (held > 0),
         name=name,
@@ -428,7 +429,7 @@
         compiler_params=pltpu.CompilerParams(vmem_limit_bytes=60 << 20),
     )(rates, *fields)
     far, near = traded(far, near)
-    fixed, far, near = (pltpu.with_memory_space_constraint(v, pltpu.HBM) for v in (fixed, far, near))
+    fixed = pltpu.with_memory_space_constraint(fixed, pltpu.HBM)
     static = (who, fixed, far, near)
     tall = (height + 2 * EDGE, depth)
 

time: 136 us -> 145 us (1.066)
  Pallas kernels: 31.9 us -> 36.7 us
  local copies, waits for them, and re-layouts: 1.7 us -> 4.72 us
    pallas_call x4, Pallas kernels: 28.1 us -> 32.9 us  [call(): pl.pallas_call(kernel, out_shape=[jax.ShapeDtypeStruct(o, jnp.float32) fo...]
    unnamed x2 -> x14, local copies, waits for them, and re-layouts: 1.07 us -> 4.08 us
where the time goes in v7:
time: 145 us; the launch traced here: 144 us
  waiting for transfers between devices  60.3 us (42%)
  starting transfers between devices  37.5 us (26%)
  Pallas kernels  36.7 us (25%)
  local copies, waits for them, and re-layouts  4.72 us (3%)
  other arithmetic  4.13 us (3%)
    ppermute x11, waiting for transfers between devices, sent(): return lax.ppermute(value, ('tm', 'space'), pairs)  44.5 us
    pallas_call x4, Pallas kernels, call(): pl.pallas_call(kernel, out_shape=[jax.ShapeDtypeStruct(o, jnp.float32) fo...  32.9 us
    ppermute x11, starting transfers between devices, sent(): return lax.ppermute(value, ('tm', 'space'), pairs)  26.6 us
    ppermute x4, waiting for transfers between devices, arrived(): lax.ppermute(value, 'tm', [(k, k + steps) for k in range(times - steps)])  15.9 us
    ppermute x4, starting transfers between devices, arrived(): lax.ppermute(value, 'tm', [(k, k + steps) for k in range(times - steps)])  11 us
    unnamed x14, local copies, waits for them, and re-layouts  4.08 us
    pallas_call x1, Pallas kernels, on_device(): pl.pallas_call(parcel_kernel, out_shape=[jax.ShapeDtypeStruct((n,) + plan...  3.73 us
  transfers between devices with their start and end apart: 15, of which 9 were waited for; matrix products, arithmetic and copies ran while one was open for 1% of the time, Pallas kernels for 0%

profile of v7, /device:TPU:6, one launch (start us, length us, event | category | flops | bytes accessed | tf_op | source)
XLA Modules:
  0.0 144.0 jit_solution(5918186871363209715)
XLA Ops:
  0.0 3.7 %parcel.1 = (f32[27,96,128]{2,1,0:T(8,128)}, f32[27,96,128]{2,1,0:T(8,128)}, f32[32,96,128]{2,1,0:T(8,128)}) custom-call(f32[4]{0:T(128)} %rates.1, f32[4,4,96,128]{3,2,1,0:T(8,128)} %source.1, f32[4,96,128]{2,1,0:T(8,128)} %initial.1, f32[4,96,128]{2,1,0:T(8,128)} %mobility.1, s32[4,96,128]{2,1,0:T(8,128)} %labels.1, s32[4,96,128]{2,1,0:T(8,128)} %electrode.1), custom_call_target="tpu_custom_call" | custom-call | tf_op jit(solution)/shard_map/parcel/pallas_call | solution.py:423
  3.7 8.0 %collective-permute-start = (f32[27,96,128]{2,1,0:T(8,128)}, f32[27,96,128]{2,1,0:T(8,128)S(1)}, u32[]{:S(2)}, u32[]{:S(2)}) collective-permute-start(f32[27,96,128]{2,1,0:T(8,128)} %get-tuple-element.20), channel_id=1, source_target_pairs={{1,2},{2,1},{3,4},{4,3},{5,6},{6,5},{7,8},{8,7},{9,10},{10,9},{11,... | collective-permute-start | bytes 3981320 | tf_op jit(solution)/shard_map/ppermute | solution.py:392
  12.0 15.5 %collective-permute-done.far = f32[27,96,128]{2,1,0:T(8,128)S(1)} collective-permute-done((f32[27,96,128]{2,1,0:T(8,128)}, f32[27,96,128]{2,1,0:T(8,128)S(1)}, u32[]{:S(2)}, u32[]{:S(2)}) %collective-permute-start) | collective-permute-done | bytes 1327136 | tf_op jit(solution)/shard_map/ppermute | solution.py:392
  27.4 11.0 %first.1 = (f32[17,96,128]{2,1,0:T(8,128)S(1)}, f32[17,96,128]{2,1,0:T(8,128)}, f32[4,96,128]{2,1,0:T(8,128)S(1)}) custom-call(s32[4]{0:T(128)S(1)} %pad_add_fusion.who, f32[32,96,128]{2,1,0:T(8,128)} %get-tuple-element.19.fixed, f32[27,96,128]{2,1,0:T(8,128)S(1)} %collective-permute-done.far, f32[27,96,128]{2,1,0:T(8,128)S(1)} %collective-permute-done.1.near), custom_call_target="tpu_custom_call" | custom-call | tf_op jit(solution)/shard_map/first/pallas_call | solution.py:330
  39.2 7.2 %collective-permute-start.2 = (f32[17,96,128]{2,1,0:T(8,128)S(1)}, f32[17,96,128]{2,1,0:T(8,128)}, u32[]{:S(2)}, u32[]{:S(2)}) collective-permute-start(f32[17,96,128]{2,1,0:T(8,128)S(1)} %get-tuple-element.22.own), channel_id=1, source_target_pairs={{1,2},{2,1},{3,4},{4,3},{5,6},{6,5},{7,8},{8,7},{9,10},{10,9},{11,... | collective-permute-start | bytes 2506760 | tf_op jit(solution)/shard_map/ppermute | solution.py:392
  46.6 3.5 %collective-permute-start.4 = (f32[4,96,128]{2,1,0:T(8,128)}, f32[4,96,128]{2,1,0:T(8,128)S(1)}, u32[]{:S(2)}, u32[]{:S(2)}) collective-permute-start(f32[4,96,128]{2,1,0:T(8,128)} %copy-done.6), channel_id=1, source_target_pairs={{0,32},{32,64},{64,96},{96,128},{128,160},{160,192},{192,224},{1,3... | collective-permute-start | bytes 589832 | tf_op jit(solution)/shard_map/ppermute | solution.py:407
  50.2 7.9 %collective-permute-done.4.arriving = f32[4,96,128]{2,1,0:T(8,128)S(1)} collective-permute-done((f32[4,96,128]{2,1,0:T(8,128)}, f32[4,96,128]{2,1,0:T(8,128)S(1)}, u32[]{:S(2)}, u32[]{:S(2)}) %collective-permute-start.4) | collective-permute-done | bytes 196640 | tf_op jit(solution)/shard_map/ppermute | solution.py:407
  58.2 7.6 %residual.1 = (f32[4,48,128]{2,1,0:T(8,128)S(1)}, f32[4,48,128]{2,1,0:T(8,128)S(1)}, f32[2,4,48,128]{3,2,1,0:T(8,128)S(1)}, f32[2,48,128]{2,1,0:T(8,128)S(1)}, f32[10,48,128]{2,1,0:T(8,128)S(1)}) custom-call(s32[4]{0:T(128)S(1)} %pad_add_fusion.who, f32[32,96,128]{2,1,0:T(8,128)} %get-tuple-element.19.fixed, f32[27,96,128]{2,1,0:T(8,128)S(1)} %collective-permute-done.far, ...), custom_call_target="tpu_custom_call" | custom-call | tf_op jit(solution)/shard_map/residual/pallas_call | solution.py:330
  65.8 3.4 %collective-permute-start.7 = (f32[4,48,128]{2,1,0:T(8,128)S(1)}, f32[4,48,128]{2,1,0:T(8,128)S(1)}, u32[]{:S(2)}, u32[]{:S(2)}) collective-permute-start(f32[4,48,128]{2,1,0:T(8,128)S(1)} %get-tuple-element.29), channel_id=1, source_target_pairs={{0,96},{32,128},{64,160},{96,192},{128,224},{1,97},{33,129},{65,16... | collective-permute-start | bytes 294920 | tf_op jit(solution)/shard_map/ppermute | solution.py:407
  69.2 1.9 %collective-permute-start.6 = (f32[2,4,48,128]{3,2,1,0:T(8,128)S(1)}, f32[2,4,48,128]{3,2,1,0:T(8,128)S(1)}, u32[]{:S(2)}, u32[]{:S(2)}) collective-permute-start(f32[2,4,48,128]{3,2,1,0:T(8,128)S(1)} %get-tuple-element.27), channel_id=1, source_target_pairs={{0,64},{32,96},{64,128},{96,160},{128,192},{160,224},{1,65},{33,97... | collective-permute-start | bytes 589832 | tf_op jit(solution)/shard_map/ppermute | solution.py:407
  71.1 2.1 %collective-permute-start.5 = (f32[4,48,128]{2,1,0:T(8,128)S(1)}, f32[4,48,128]{2,1,0:T(8,128)S(1)}, u32[]{:S(2)}, u32[]{:S(2)}) collective-permute-start(f32[4,48,128]{2,1,0:T(8,128)S(1)} %get-tuple-element.26), channel_id=1, source_target_pairs={{0,32},{32,64},{64,96},{96,128},{128,160},{160,192},{192,224},{1,3... | collective-permute-start | bytes 294920 | tf_op jit(solution)/shard_map/ppermute | solution.py:407
  73.4 7.9 %collective-permute-done.5 = f32[4,48,128]{2,1,0:T(8,128)S(1)} collective-permute-done((f32[4,48,128]{2,1,0:T(8,128)S(1)}, f32[4,48,128]{2,1,0:T(8,128)S(1)}, u32[]{:S(2)}, u32[]{:S(2)}) %collective-permute-start.5) | collective-permute-done | bytes 98336 | tf_op jit(solution)/shard_map/ppermute | solution.py:407
  83.1 4.7 %collective-permute-start.8 = (f32[6,96,128]{2,1,0:T(8,128)}, f32[6,96,128]{2,1,0:T(8,128)}, u32[]{:S(2)}, u32[]{:S(2)}) collective-permute-start(f32[6,96,128]{2,1,0:T(8,128)} %get-tuple-element.48), channel_id=1, source_target_pairs={{1,2},{2,1},{3,4},{4,3},{5,6},{6,5},{7,8},{8,7},{9,10},{10,9},{11,... | collective-permute-start | bytes 884744 | tf_op jit(solution)/shard_map/ppermute | solution.py:392
  87.9 7.1 %collective-permute-done.8.side_far = f32[6,96,128]{2,1,0:T(8,128)} collective-permute-done((f32[6,96,128]{2,1,0:T(8,128)}, f32[6,96,128]{2,1,0:T(8,128)}, u32[]{:S(2)}, u32[]{:S(2)}) %collective-permute-start.8) | collective-permute-done | bytes 294944 | tf_op jit(solution)/shard_map/ppermute | solution.py:392
  95.9 0.9 copy-done.3
  97.8 1.1 join.1
  98.9 3.5 %collective-permute-start.10 = (f32[2,6,48,128]{3,2,1,0:T(8,128)S(1)}, f32[2,6,48,128]{3,2,1,0:T(8,128)S(1)}, u32[]{:S(2)}, u32[]{:S(2)}) collective-permute-start(f32[2,6,48,128]{3,2,1,0:T(8,128)S(1)} %get-tuple-element.31), channel_id=1, source_target_pairs={{0,64},{1,66},{2,65},{3,68},{4,67},{5,70},{6,69},{7,72},{8,71},{9,... | collective-permute-start | bytes 884744 | tf_op jit(solution)/shard_map/ppermute | solution.py:392
  102.6 10.1 %collective-permute-done.10 = f32[2,6,48,128]{3,2,1,0:T(8,128)S(1)} collective-permute-done((f32[2,6,48,128]{3,2,1,0:T(8,128)S(1)}, f32[2,6,48,128]{3,2,1,0:T(8,128)S(1)}, u32[]{:S(2)}, u32[]{:S(2)}) %collective-permute-start.10) | collective-permute-done | bytes 294944 | tf_op jit(solution)/shard_map/ppermute | solution.py:392
  115.2 1.3 collective-permute-start.12
  116.5 1.3 collective-permute-start.13
  117.8 8.2 %collective-permute-done.13 = f32[2,2,48,128]{3,2,1,0:T(8,128)S(1)} collective-permute-done((f32[2,2,48,128]{3,2,1,0:T(8,128)S(1)}, f32[2,2,48,128]{3,2,1,0:T(8,128)S(1)}, u32[]{:S(2)}, u32[]{:S(2)}) %collective-permute-start.13) | collective-permute-done | bytes 98336 | tf_op jit(solution)/shard_map/ppermute | solution.py:392
  126.0 1.1 collective-permute-done.12
  127.5 1.5 %collective-permute-done.14 = f32[2,8,48,128]{3,2,1,0:T(8,128)S(1)} collective-permute-done((f32[2,8,48,128]{3,2,1,0:T(8,128)S(1)}, f32[2,8,48,128]{3,2,1,0:T(8,128)S(1)}, u32[]{:S(2)}, u32[]{:S(2)}) %collective-permute-start.14) | collective-permute-done | bytes 393248 | tf_op jit(solution)/shard_map/ppermute | solution.py:392
  130.8 13.2 %last.1 = f32[4,4,96,128]{3,2,1,0:T(8,128)} custom-call(s32[4]{0:T(128)S(1)} %pad_add_fusion.who, f32[32,96,128]{2,1,0:T(8,128)} %get-tuple-element.19.fixed, f32[27,96,128]{2,1,0:T(8,128)S(1)} %collective-permute-done.far, f32[27,96,128]{2,1,0:T(8,128)S(1)} %collective-permute-done.1.near, f32[17,96,128]{2,1,0:T(8,128)S(1)} %get-tuple-element.22.own, ...), custom_call_target="tpu_custom_call" | custom-call | tf_op jit(solution)/shard_map/last/pallas_call | solution.py:330
  (87 shorter events, 9.2 us)
Async XLA Ops:
  3.7 23.7 %collective-permute-start = (f32[27,96,128]{2,1,0:T(8,128)}, f32[27,96,128]{2,1,0:T(8,128)S(1)}, u32[]{:S(2)}, u32[]{:S(2)}) collective-permute-start(f32[27,96,128]{2,1,0:T(8,128)} %get-tuple-element.20), channel_id=1, source_target_pairs={{1,2},{2,1},{3,4},{4,3},{5,6},{6,5},{7,8},{8,7},{9,10},{10,9},{11,... | collective-permute-start | bytes 3981320 | tf_op jit(solution)/shard_map/ppermute | solution.py:392
  11.8 15.7 %collective-permute-start.1 = (f32[27,96,128]{2,1,0:T(8,128)}, f32[27,96,128]{2,1,0:T(8,128)S(1)}, u32[]{:S(2)}, u32[]{:S(2)}) collective-permute-start(f32[27,96,128]{2,1,0:T(8,128)} %get-tuple-element.21), channel_id=1, source_target_pairs={{0,1},{1,0},{2,3},{3,2},{4,5},{5,4},{6,7},{7,6},{8,9},{9,8},{10,11... | collective-permute-start | bytes 3981320 | tf_op jit(solution)/shard_map/ppermute | solution.py:392
  38.5 0.7 copy-start.6
  39.2 19.0 %collective-permute-start.2 = (f32[17,96,128]{2,1,0:T(8,128)S(1)}, f32[17,96,128]{2,1,0:T(8,128)}, u32[]{:S(2)}, u32[]{:S(2)}) collective-permute-start(f32[17,96,128]{2,1,0:T(8,128)S(1)} %get-tuple-element.22.own), channel_id=1, source_target_pairs={{1,2},{2,1},{3,4},{4,3},{5,6},{6,5},{7,8},{8,7},{9,10},{10,9},{11,... | collective-permute-start | bytes 2506760 | tf_op jit(solution)/shard_map/ppermute | solution.py:392
  46.4 11.7 %collective-permute-start.3 = (f32[17,96,128]{2,1,0:T(8,128)}, f32[17,96,128]{2,1,0:T(8,128)}, u32[]{:S(2)}, u32[]{:S(2)}) collective-permute-start(f32[17,96,128]{2,1,0:T(8,128)} %get-tuple-element.23), channel_id=1, source_target_pairs={{0,1},{1,0},{2,3},{3,2},{4,5},{5,4},{6,7},{7,6},{8,9},{9,8},{10,11... | collective-permute-start | bytes 2506760 | tf_op jit(solution)/shard_map/ppermute | solution.py:392
  46.6 11.5 %collective-permute-start.4 = (f32[4,96,128]{2,1,0:T(8,128)}, f32[4,96,128]{2,1,0:T(8,128)S(1)}, u32[]{:S(2)}, u32[]{:S(2)}) collective-permute-start(f32[4,96,128]{2,1,0:T(8,128)} %copy-done.6), channel_id=1, source_target_pairs={{0,32},{32,64},{64,96},{96,128},{128,160},{160,192},{192,224},{1,3... | collective-permute-start | bytes 589832 | tf_op jit(solution)/shard_map/ppermute | solution.py:407
  58.1 7.6 %copy-start = (f32[4,96,128]{2,1,0:T(8,128)}, f32[4,96,128]{2,1,0:T(8,128)S(1)}, u32[]{:S(2)}) copy-start(f32[4,96,128]{2,1,0:T(8,128)S(1)} %collective-permute-done.4.arriving) | copy-start | bytes 589828
  65.7 15.8 %copy-start.2 = (f32[10,48,128]{2,1,0:T(8,128)}, f32[10,48,128]{2,1,0:T(8,128)S(1)}, u32[]{:S(2)}) copy-start(f32[10,48,128]{2,1,0:T(8,128)S(1)} %get-tuple-element.28.rough) | copy-start | bytes 737284
  65.8 7.6 %collective-permute-start.7 = (f32[4,48,128]{2,1,0:T(8,128)S(1)}, f32[4,48,128]{2,1,0:T(8,128)S(1)}, u32[]{:S(2)}, u32[]{:S(2)}) collective-permute-start(f32[4,48,128]{2,1,0:T(8,128)S(1)} %get-tuple-element.29), channel_id=1, source_target_pairs={{0,96},{32,128},{64,160},{96,192},{128,224},{1,97},{33,129},{65,16... | collective-permute-start | bytes 294920 | tf_op jit(solution)/shard_map/ppermute | solution.py:407
  69.2 12.1 %collective-permute-start.6 = (f32[2,4,48,128]{3,2,1,0:T(8,128)S(1)}, f32[2,4,48,128]{3,2,1,0:T(8,128)S(1)}, u32[]{:S(2)}, u32[]{:S(2)}) collective-permute-start(f32[2,4,48,128]{3,2,1,0:T(8,128)S(1)} %get-tuple-element.27), channel_id=1, source_target_pairs={{0,64},{32,96},{64,128},{96,160},{128,192},{160,224},{1,65},{33,97... | collective-permute-start | bytes 589832 | tf_op jit(solution)/shard_map/ppermute | solution.py:407
  71.1 10.2 %collective-permute-start.5 = (f32[4,48,128]{2,1,0:T(8,128)S(1)}, f32[4,48,128]{2,1,0:T(8,128)S(1)}, u32[]{:S(2)}, u32[]{:S(2)}) collective-permute-start(f32[4,48,128]{2,1,0:T(8,128)S(1)} %get-tuple-element.26), channel_id=1, source_target_pairs={{0,32},{32,64},{64,96},{96,128},{128,160},{160,192},{192,224},{1,3... | collective-permute-start | bytes 294920 | tf_op jit(solution)/shard_map/ppermute | solution.py:407
  82.4 0.6 copy-start.4
  83.1 12.0 %collective-permute-start.8 = (f32[6,96,128]{2,1,0:T(8,128)}, f32[6,96,128]{2,1,0:T(8,128)}, u32[]{:S(2)}, u32[]{:S(2)}) collective-permute-start(f32[6,96,128]{2,1,0:T(8,128)} %get-tuple-element.48), channel_id=1, source_target_pairs={{1,2},{2,1},{3,4},{4,3},{5,6},{6,5},{7,8},{8,7},{9,10},{10,9},{11,... | collective-permute-start | bytes 884744 | tf_op jit(solution)/shard_map/ppermute | solution.py:392
  87.8 7.3 %collective-permute-start.9 = (f32[6,96,128]{2,1,0:T(8,128)}, f32[6,96,128]{2,1,0:T(8,128)}, u32[]{:S(2)}, u32[]{:S(2)}) collective-permute-start(f32[6,96,128]{2,1,0:T(8,128)} %get-tuple-element.47), channel_id=1, source_target_pairs={{0,1},{1,0},{2,3},{3,2},{4,5},{5,4},{6,7},{7,6},{8,9},{9,8},{10,11... | collective-permute-start | bytes 884744 | tf_op jit(solution)/shard_map/ppermute | solution.py:392
  95.0 0.9 copy-start.1
  95.9 0.9 copy-start.3
  96.9 0.9 copy-start.5
  98.9 13.8 %collective-permute-start.10 = (f32[2,6,48,128]{3,2,1,0:T(8,128)S(1)}, f32[2,6,48,128]{3,2,1,0:T(8,128)S(1)}, u32[]{:S(2)}, u32[]{:S(2)}) collective-permute-start(f32[2,6,48,128]{3,2,1,0:T(8,128)S(1)} %get-tuple-element.31), channel_id=1, source_target_pairs={{0,64},{1,66},{2,65},{3,68},{4,67},{5,70},{6,69},{7,72},{8,71},{9,... | collective-permute-start | bytes 884744 | tf_op jit(solution)/shard_map/ppermute | solution.py:392
  112.8 1.7 %collective-permute-start.11 = (f32[2,6,48,128]{3,2,1,0:T(8,128)S(1)}, f32[2,6,48,128]{3,2,1,0:T(8,128)S(1)}, u32[]{:S(2)}, u32[]{:S(2)}) collective-permute-start(f32[2,6,48,128]{3,2,1,0:T(8,128)S(1)} %pad_select_fusion), channel_id=1, source_target_pairs={{0,1},{1,0},{2,3},{3,2},{4,5},{5,4},{6,7},{7,6},{8,9},{9,8},{10,11... | collective-permute-start | bytes 884744 | tf_op jit(solution)/shard_map/ppermute | solution.py:392
  115.2 11.9 %collective-permute-start.12 = (f32[2,6,48,128]{3,2,1,0:T(8,128)S(1)}, f32[2,6,48,128]{3,2,1,0:T(8,128)S(1)}, u32[]{:S(2)}, u32[]{:S(2)}) collective-permute-start(f32[2,6,48,128]{3,2,1,0:T(8,128)S(1)} %fusion.59), channel_id=1, source_target_pairs={{0,130},{2,132},{3,129},{4,134},{5,131},{6,136},{7,133},{8,138},{9... | collective-permute-start | bytes 884744 | tf_op jit(solution)/shard_map/ppermute | solution.py:392
  116.5 9.5 %collective-permute-start.13 = (f32[2,2,48,128]{3,2,1,0:T(8,128)S(1)}, f32[2,2,48,128]{3,2,1,0:T(8,128)S(1)}, u32[]{:S(2)}, u32[]{:S(2)}) collective-permute-start(f32[2,2,48,128]{3,2,1,0:T(8,128)S(1)} %slice.465), channel_id=1, source_target_pairs={{0,128},{1,129},{2,130},{3,131},{4,132},{5,133},{6,134},{7,135},{8... | collective-permute-start | bytes 294920 | tf_op jit(solution)/shard_map/ppermute | solution.py:392
  127.2 1.8 %collective-permute-start.14 = (f32[2,8,48,128]{3,2,1,0:T(8,128)S(1)}, f32[2,8,48,128]{3,2,1,0:T(8,128)S(1)}, u32[]{:S(2)}, u32[]{:S(2)}) collective-permute-start(f32[2,8,48,128]{3,2,1,0:T(8,128)S(1)} %pad_maximum_fusion.2), channel_id=1, source_target_pairs={{0,1},{1,0},{2,3},{3,2},{4,5},{5,4},{6,7},{7,6},{8,9},{9,8},{10,11... | collective-permute-start | bytes 1179656 | tf_op jit(solution)/shard_map/ppermute | solution.py:392
